TPU v7x, 256 devices: a whole 4x4x8 slice. The times are simulated.
256 devices in a mesh: nodes: 64 (over y, z, core), rep: 4 (over x).
Axes of the slice: x: 4, y: 4, z: 8, core: 2. Of those that a mesh axis runs over, the one named last changes fastest.
Arguments:
- queries: bfloat16 [4, 32768, 1024], P('rep', 'nodes'), may hold values from -9 to 9
- keys: bfloat16 [4, 32768, 1024], P('rep', 'nodes'), may hold values from -9 to 9
- values: bfloat16 [4, 32768, 1024], P('rep', 'nodes'), may hold values from -6 to 6
- grad_out: bfloat16 [4, 32768, 1024], P('rep', 'nodes'), may hold values from -16 to 16
- w_out: bfloat16 [1024, 1024], replicated, may hold values from -0.1875 to 0.1875
- cluster_id: int32 [4, 32768], P('rep', 'nodes'), may hold values from 0 to 255, as said below
Outputs:
- grad_queries: bfloat16 [4, 32768, 1024], P('rep', 'nodes')
- grad_keys: bfloat16 [4, 32768, 1024], P('rep', 'nodes')
- grad_values: bfloat16 [4, 32768, 1024], P('rep', 'nodes')
- grad_w_out: float32 [1024, 1024], P('nodes')
Inputs may be any that keep to these rules, and one draw needn't show every extreme that they name: `cluster_id`: cluster c of a window is owned by index c // 4 of the nodes axis. The 512 nodes of one device name clusters of every owner, exactly 8 nodes for each owner. Clusters differ in size and may be empty.
All inputs are finite; a program needn't handle non-finite values.
Results may differ from a plain program's by a relative error of at most 0.013.
The roundings to bfloat16 on the way count: a program that leaves them out, or rounds other values in their place, can miss the bound.
Values may be sent and summed in bfloat16 or wider, within the bound.
No kernel may reach another device: no remote copies, remote signals or barrier semaphores. Data moves between devices by JAX's collectives and lax.ppermute only.
A program may use at most 128 MiB of HBM per device.

v0:
```python
import math

import jax
import jax.numpy as jnp
from jax import lax
from jax.experimental import pallas as pl
from jax.experimental.pallas import tpu as pltpu
from jax.sharding import PartitionSpec as P

HEAD_DIM = 128
CL_DEV = 4
UNIT = 256
UNITS_A = 2
LANES = 128
big_negative = -1e30
BF = jnp.bfloat16
F32 = jnp.float32


def mm(a, b, dims):
    return lax.dot_general(a, b, (dims, ((), ())), preferred_element_type=F32)


def nn(a, b):
    return mm(a, b, ((1,), (0,)))


def nt(a, b):
    return mm(a, b, ((1,), (1,)))


def tn(a, b):
    return mm(a, b, ((0,), (0,)))


def column_of(row, rows):
    return jnp.transpose(jnp.broadcast_to(row, (LANES, rows)))[:, :1]


def pack_first(rows, bucket, ids_ref, g_ref, q_ref, k_ref, v_ref, out_ref, pick_ref):
    ids_row = ids_ref[...].astype(F32)
    owner_row = jnp.floor(ids_row * (1.0 / CL_DEV))
    ids_col = column_of(ids_row, rows)
    owner_col = jnp.floor(ids_col * (1.0 / CL_DEV))
    tag_col = ids_col - owner_col * CL_DEV + 1.0
    down = lax.broadcasted_iota(jnp.int32, (rows, rows), 0)
    across = lax.broadcasted_iota(jnp.int32, (rows, rows), 1)
    same = (owner_col == owner_row) & (down < across)
    rank = jnp.sum(jnp.where(same, 1.0, 0.0), axis=0, keepdims=True)
    slot = (owner_row * bucket + rank).astype(jnp.int32)
    pick = jnp.where(down == slot, 1.0, 0.0).astype(BF)
    pick_ref[...] = pick
    width = g_ref.shape[1]
    out_ref[:, :width] = nn(pick, g_ref[...]).astype(BF)
    for u in range(q_ref.shape[1] // UNIT):
        for m, ref in enumerate((q_ref, k_ref, v_ref)):
            base = width + (3 * u + m) * UNIT
            out_ref[:, base : base + UNIT] = nn(pick, ref[:, u * UNIT : (u + 1) * UNIT]).astype(BF)
    base = out_ref.shape[1] - LANES
    tags = jnp.broadcast_to(tag_col, (rows, LANES)).astype(BF)
    out_ref[:, base:] = nn(pick, tags).astype(BF)


def pack_rest(pick_ref, q_ref, k_ref, v_ref, out_ref):
    pick = pick_ref[...]
    for m, ref in enumerate((q_ref, k_ref, v_ref)):
        out_ref[:, m * UNIT : (m + 1) * UNIT] = nn(pick, ref[...]).astype(BF)


def attend(scale, g_ref, tag_ref, w_ref, q_ref, k_ref, v_ref, ret_ref, att_ref, bias_ref):
    rows = g_ref.shape[0]

    @pl.when(pl.program_id(0) == 0)
    def _():
        tags = tag_ref[...].astype(F32)
        same = tags[:, :1] == jnp.transpose(tags)[:1, :]
        bias_ref[...] = jnp.where(same, 0.0, big_negative)

    grad_all = nn(g_ref[...], w_ref[...]).astype(BF)
    for h in range(UNIT // HEAD_DIM):
        cols = slice(h * HEAD_DIM, (h + 1) * HEAD_DIM)
        q, k, v, grad = q_ref[:, cols], k_ref[:, cols], v_ref[:, cols], grad_all[:, cols]
        scores = nt(q, k) * scale + bias_ref[...]
        weights = jnp.exp(scores - jnp.max(scores, axis=1, keepdims=True))
        probs = weights * (1.0 / jnp.sum(weights, axis=1, keepdims=True))
        low = probs.astype(BF)
        attended = nn(low, v).astype(BF)
        delta = jnp.sum(grad.astype(F32) * attended.astype(F32), axis=1, keepdims=True)
        grad_scores = (probs * (nt(grad, v) - delta) * scale).astype(BF)
        att_ref[:, cols] = attended
        for m, part in enumerate((nn(grad_scores, k), tn(grad_scores, q), tn(low, grad))):
            base = m * UNIT + h * HEAD_DIM
            ret_ref[:, base : base + HEAD_DIM] = part.astype(BF)


def unpack(held, back_ref, ret_ref, *refs):
    outs = refs[held:]
    for m, ref in enumerate(outs):
        ref[...] = nn(back_ref[...], ret_ref[:, m * UNIT : (m + 1) * UNIT]).astype(BF)


def cost(flops, nbytes, exps=0):
    return pl.CostEstimate(flops=flops, bytes_accessed=nbytes, transcendentals=exps)


def params():
    return pltpu.CompilerParams(vmem_limit_bytes=48 * 1024 * 1024)


def ring(size, shift):
    return [(i, (i + shift) % size) for i in range(size)]


def local(sizes, queries, keys, values, grad_out, w_out, cluster_id):
    ny, nz, nc, nx = sizes
    node_count = ny * nz * nc
    rows = queries.shape[1]
    width = queries.shape[2]
    bucket = rows // node_count
    units = width // UNIT
    ua, ub = UNITS_A, units - UNITS_A
    scale = 1.0 / math.sqrt(HEAD_DIM)
    norm_factor = 1.0 / math.sqrt(nx * node_count * rows)
    q, k, v, g = queries[0], keys[0], values[0], grad_out[0]

    def sds(shape, dtype=BF):
        return jax.ShapeDtypeStruct(shape, dtype)

    def full(shape):
        return pl.BlockSpec(shape, lambda *_: (0,) * len(shape))

    def exchange(rows_in):
        c = rows_in.shape[1]
        out = lax.all_to_all(
            rows_in.reshape(node_count, bucket, c), "nodes", split_axis=0, concat_axis=0, tiled=True
        )
        return out.reshape(rows, c)

    wide_a = width + 3 * UNIT * ua + LANES
    part_a = pl.BlockSpec((rows, UNIT * ua), lambda i: (0, 0))
    send_a, pick = pl.pallas_call(
        lambda *refs: pack_first(rows, bucket, *refs),
        out_shape=(sds((rows, wide_a)), sds((rows, rows))),
        grid=(1,),
        in_specs=[full((1, rows)), full((rows, width)), part_a, part_a, part_a],
        out_specs=(full((rows, wide_a)), full((rows, rows))),
        compiler_params=params(),
        cost_estimate=cost(2 * rows * rows * wide_a, 4 * rows * wide_a),
        name="pack_first",
    )(cluster_id, g, q, k, v)
    recv_a = exchange(send_a)

    part_b = pl.BlockSpec((rows, UNIT), lambda i: (0, i + ua))
    send_b = pl.pallas_call(
        pack_rest,
        out_shape=sds((rows, 3 * UNIT * ub)),
        grid=(ub,),
        in_specs=[full((rows, rows)), part_b, part_b, part_b],
        out_specs=pl.BlockSpec((rows, 3 * UNIT), lambda i: (0, i)),
        compiler_params=params(),
        cost_estimate=cost(2 * rows * rows * 3 * UNIT * ub, 4 * rows * 3 * UNIT * ub),
        name="pack_rest",
    )(pick, q, k, v)
    recv_b = exchange(send_b)
    back = jnp.transpose(pick)

    def attention(recv, first, unit0, n_units):
        def col(m):
            return pl.BlockSpec((rows, UNIT), lambda i: (0, first + 3 * i + m))

        return pl.pallas_call(
            lambda *refs: attend(scale, *refs),
            out_shape=(sds((rows, 3 * UNIT * n_units)), sds((rows, UNIT * n_units))),
            grid=(n_units,),
            in_specs=[
                full((rows, width)),
                pl.BlockSpec((rows, LANES), lambda i: (0, wide_a // LANES - 1)),
                pl.BlockSpec((width, UNIT), lambda i: (0, i + unit0)),
                col(0),
                col(1),
                col(2),
            ],
            out_specs=(
                pl.BlockSpec((rows, 3 * UNIT), lambda i: (0, i)),
                pl.BlockSpec((rows, UNIT), lambda i: (0, i)),
            ),
            scratch_shapes=[pltpu.VMEM((rows, rows), F32)],
            compiler_params=params(),
            cost_estimate=cost(
                2 * rows * UNIT * n_units * (6 * rows + width),
                2 * rows * UNIT * n_units * 7 + 4 * rows * width,
                rows * rows * n_units * UNIT // HEAD_DIM,
            ),
            name="attend",
        )(recv_a, recv_a, w_out, recv, recv, recv)

    ret_a, att_a = attention(recv_a, width // UNIT, 0, ua)
    home_a = exchange(ret_a)
    ret_b, att_b = attention(recv_b, 0, ua, ub)
    home_b = exchange(ret_b)

    out_sds = (sds((rows, width)),) * 3
    outs = pl.pallas_call(
        lambda *refs: unpack(0, *refs),
        out_shape=out_sds,
        grid=(ua,),
        in_specs=[full((rows, rows)), pl.BlockSpec((rows, 3 * UNIT), lambda i: (0, i))],
        out_specs=(pl.BlockSpec((rows, UNIT), lambda i: (0, i)),) * 3,
        compiler_params=params(),
        cost_estimate=cost(2 * rows * rows * 3 * UNIT * ua, 4 * rows * 3 * UNIT * ua),
        name="unpack_a",
    )(back, home_a)
    outs = pl.pallas_call(
        lambda *refs: unpack(3, *refs),
        out_shape=out_sds,
        grid=(ub,),
        in_specs=[full((rows, rows)), pl.BlockSpec((rows, 3 * UNIT), lambda i: (0, i))]
        + [pl.BlockSpec(memory_space=pl.ANY)] * 3,
        out_specs=(pl.BlockSpec((rows, UNIT), lambda i: (0, i + ua)),) * 3,
        input_output_aliases={2: 0, 3: 1, 4: 2},
        compiler_params=params(),
        cost_estimate=cost(2 * rows * rows * 3 * UNIT * ub, 4 * rows * 3 * UNIT * ub),
        name="unpack_b",
    )(back, home_b, *outs)

    node = lax.axis_index("nodes")
    ix = lax.axis_index("rep")
    iy, iz, ic = node // (nz * nc), (node // nc) % nz, node % nc

    def nid(y, z, c):
        return ((y % ny) * nz + z % nz) * nc + c % nc

    everyone = [(y, z, c) for y in range(ny) for z in range(nz) for c in range(nc)]

    def hop(dy, dz, dc):
        return [(nid(y, z, c), nid(y + dy, z + dz, c + dc)) for y, z, c in everyone]

    def pick_of(array, index, axis):
        return lax.dynamic_index_in_dim(array, index, axis, keepdims=False)

    att = jnp.concatenate([att_a, att_b], axis=1)
    weight = tn(recv_a[:, :width], att)
    weight = weight.reshape(ny * nz, nc, width // node_count, width)
    total = pick_of(weight, ic, 1)
    for s in range(1, nc):
        sent = pick_of(weight, (ic + s) % nc, 1).astype(BF)
        total = total + lax.ppermute(sent, "nodes", hop(0, 0, s))
    share = width // nx
    weight = total.reshape(width // nc, width)
    total = lax.dynamic_slice_in_dim(weight, ix * share, share, 1)
    for s in range(1, nx):
        sent = lax.dynamic_slice_in_dim(weight, ((ix + s) % nx) * share, share, 1).astype(BF)
        total = total + lax.ppermute(sent, "rep", ring(nx, s))
    weight = total.reshape(ny, width // nc // ny, share)
    total = pick_of(weight, iy, 0)
    for s in range(1, ny):
        sent = pick_of(weight, (iy + s) % ny, 0).astype(BF)
        total = total + lax.ppermute(sent, "nodes", hop(s, 0, 0))
    weight = total.reshape(nz, width // node_count, share)
    total = pick_of(weight, iz, 0)
    for s in range(1, nz):
        sent = pick_of(weight, (iz + s) % nz, 0).astype(BF)
        total = total + lax.ppermute(sent, "nodes", hop(0, s, 0))
    total = total * norm_factor
    grad_weight = jnp.zeros((width // node_count, width), F32)
    grad_weight = lax.dynamic_update_slice_in_dim(grad_weight, total, ix * share, 1)
    low = total.astype(BF)
    for s in range(1, nx):
        came = lax.ppermute(low, "rep", ring(nx, s)).astype(F32)
        at = ((ix + nx - s) % nx) * share
        grad_weight = lax.dynamic_update_slice_in_dim(grad_weight, came, at, 1)
    return (outs[0][None], outs[1][None], outs[2][None], grad_weight)


def solution(mesh):
    nodes, nx = mesh.shape["nodes"], mesh.shape["rep"]
    nc = 2
    nz = 8
    ny = nodes // (nz * nc)
    in_specs = (
        P("rep", "nodes", None),
        P("rep", "nodes", None),
        P("rep", "nodes", None),
        P("rep", "nodes", None),
        P(),
        P("rep", "nodes"),
    )
    out_specs = (
        P("rep", "nodes", None),
        P("rep", "nodes", None),
        P("rep", "nodes", None),
        P("nodes", None),
    )

    def body(*args):
        return local((ny, nz, nc, nx), *args)

    return jax.shard_map(
        body, mesh=mesh, in_specs=in_specs, out_specs=out_specs, check_vma=False
    )
```

profile of v0, /device:TPU:40, one launch (start us, length us, event | category | flops | bytes accessed | tf_op | source)
XLA Modules:
  0.0 250.0 jit_solution(7310239430187288612)
XLA Ops:
  6.2 3.7 %pack_first.1 = (bf16[512,2688]{1,0:T(8,128)(2,1)}, bf16[512,512]{1,0:T(8,128)(2,1)S(1)}) custom-call(s32[1,512]{1,0:T(1,128)S(1)} %copy-done.11, bf16[512,1024]{1,0:T(8,128)(2,1)S(1)} %bitcast.81, bf16[512,1024]{1,0:T(8,128)(2,1)S(1)} %bitcast.75, bf16[512,1024]{1,0:T(8,128)(2,1)S(1)} %bitcast.77, bf16[512,1024]{1,0:T(8,128)(2,1)S(1)} %bitcast.79), custom_call_target="tpu_custom_call" | custom-call | flops 1409286144 | bytes 5505024 | tf_op jit(solution)/shard_map/pack_first/pallas_call | solution.py:141
  9.9 12.0 %all-to-all-start = ((bf16[64,8,2688]{2,1,0:T(8,128)(2,1)}), bf16[64,8,2688]{2,1,0:T(8,128)(2,1)}, u32[]{:S(2)}, u32[]{:S(2)}) async-start(bf16[64,8,2688]{2,1,0:T(8,128)(2,1)} %bitcast.82), calls=%async_computation | async-start | bytes 5505024 | tf_op jit(solution)/shard_map/all_to_all | solution.py:134
  24.3 2.4 pack_rest.1
  26.7 58.3 %all-to-all-done = bf16[64,8,2688]{2,1,0:T(8,128)(2,1)} async-done(((bf16[64,8,2688]{2,1,0:T(8,128)(2,1)}), bf16[64,8,2688]{2,1,0:T(8,128)(2,1)}, u32[]{:S(2)}, u32[]{:S(2)}) %all-to-all-start) | async-done | bytes 2752544 | tf_op jit(solution)/shard_map/all_to_all | solution.py:134
  85.0 7.5 %all-to-all-start.1 = ((bf16[64,8,1536]{2,1,0:T(8,128)(2,1)}), bf16[64,8,1536]{2,1,0:T(8,128)(2,1)S(1)}, u32[]{:S(2)}, u32[]{:S(2)}) async-start(bf16[64,8,1536]{2,1,0:T(8,128)(2,1)} %bitcast.7), calls=%async_computation.1 | async-start | bytes 3145728 | tf_op jit(solution)/shard_map/all_to_all | solution.py:134
  92.6 1.6 copy-done
  94.2 8.1 %attend.3 = (bf16[512,1536]{1,0:T(8,128)(2,1)S(1)}, bf16[512,512]{1,0:T(8,128)(2,1)S(1)}) custom-call(bf16[512,2688]{1,0:T(8,128)(2,1)} %bitcast.6.refs_0_.refs_1_.refs_3_.refs_4_.refs_5_, bf16[512,2688]{1,0:T(8,128)(2,1)} %bitcast.6.refs_0_.refs_1_.refs_3_.refs_4_.refs_5_, bf16[1024,1024]{1,0:T(8,128)(2,1)S(1)} %copy-done, ...), custom_call_target="tpu_custom_call" | custom-call | flops 2147483648 | bytes 5767168 | tf_op jit(solution)/shard_map/attend/pallas_call | solution.py:171
  103.4 27.6 %all-to-all-done.1 = bf16[64,8,1536]{2,1,0:T(8,128)(2,1)S(1)} async-done(((bf16[64,8,1536]{2,1,0:T(8,128)(2,1)}), bf16[64,8,1536]{2,1,0:T(8,128)(2,1)S(1)}, u32[]{:S(2)}, u32[]{:S(2)}) %all-to-all-start.1) | async-done | bytes 1572896 | tf_op jit(solution)/shard_map/all_to_all | solution.py:134
  131.0 7.6 %all-to-all-start.3 = ((bf16[64,8,1536]{2,1,0:T(8,128)(2,1)}), bf16[64,8,1536]{2,1,0:T(8,128)(2,1)}, u32[]{:S(2)}, u32[]{:S(2)}) async-start(bf16[64,8,1536]{2,1,0:T(8,128)(2,1)} %bitcast.74), calls=%async_computation.3 | async-start | bytes 3145728 | tf_op jit(solution)/shard_map/all_to_all | solution.py:134
  138.6 1.6 copy-done.1
  140.2 7.9 %attend.2 = (bf16[512,1536]{1,0:T(8,128)(2,1)S(1)}, bf16[512,512]{1,0:T(8,128)(2,1)S(1)}) custom-call(bf16[512,2688]{1,0:T(8,128)(2,1)} %bitcast.6.refs_0_.refs_1_.refs_3_.refs_4_.refs_5_, bf16[512,2688]{1,0:T(8,128)(2,1)} %bitcast.6.refs_0_.refs_1_.refs_3_.refs_4_.refs_5_, bf16[1024,1024]{1,0:T(8,128)(2,1)S(1)} %copy-done.1, ...), custom_call_target="tpu_custom_call" | custom-call | flops 2147483648 | bytes 5767168 | tf_op jit(solution)/shard_map/attend/pallas_call | solution.py:171
  148.1 5.0 %fusion.1 = f32[1024,1024]{1,0:T(8,128)} fusion(bf16[512,2688]{1,0:T(8,128)(2,1)} %bitcast.6.refs_0_.refs_1_.refs_3_.refs_4_.refs_5_, bf16[512,512]{1,0:T(8,128)(2,1)S(1)} %get-tuple-element.27, bf16[512,512]{1,0:T(8,128)(2,1)S(1)} %get-tuple-element.26), kind=kOutput, calls=%fused_computation.3 | convolution fusion | flops 1075838976 | bytes 6291456 | tf_op jit(solution)/shard_map/dot_general | solution.py:21
  153.2 1.7 fusion
  155.1 21.8 %all-to-all-done.3 = bf16[64,8,1536]{2,1,0:T(8,128)(2,1)} async-done(((bf16[64,8,1536]{2,1,0:T(8,128)(2,1)}), bf16[64,8,1536]{2,1,0:T(8,128)(2,1)}, u32[]{:S(2)}, u32[]{:S(2)}) %all-to-all-start.3) | async-done | bytes 1572896 | tf_op jit(solution)/shard_map/all_to_all | solution.py:134
  176.9 7.5 %all-to-all-start.2 = ((bf16[64,8,1536]{2,1,0:T(8,128)(2,1)}), bf16[64,8,1536]{2,1,0:T(8,128)(2,1)S(1)}, u32[]{:S(2)}, u32[]{:S(2)}) async-start(bf16[64,8,1536]{2,1,0:T(8,128)(2,1)} %bitcast.73), calls=%async_computation.2 | async-start | bytes 3145728 | tf_op jit(solution)/shard_map/all_to_all | solution.py:134
  184.5 3.8 %bitcast_add_fusion = f32[32,16,1024]{2,1,0:T(8,128)} fusion(bf16[32,16,1024]{2,1,0:T(8,128)(2,1)} %collective-permute-done, f32[32,2,16,1024]{3,2,1,0:T(8,128)} %bitcast.16, s32[]{:T(128)S(6)} %select_n.142), kind=kLoop, calls=%fused_computation | loop fusion | flops 1048576 | bytes 5242884 | tf_op jit(solution)/shard_map/add | solution.py:247
  191.2 2.7 %collective-permute-start.2 = (bf16[512,256]{1,0:T(8,128)(2,1)S(1)}, bf16[512,256]{1,0:T(8,128)(2,1)S(1)}, u32[]{:S(2)}, u32[]{:S(2)}) collective-permute-start(bf16[512,256]{1,0:T(8,128)(2,1)S(1)} %get-tuple-element.32), channel_id=1, source_target_pairs={{0,2},{1,3},{2,0},{3,1},{4,6},{5,7},{6,4},{7,5},{8,10},{9,11},{10,... | collective-permute-start | bytes 786440 | tf_op jit(solution)/shard_map/ppermute | solution.py:253
  195.4 3.9 %collective-permute-done.1 = bf16[512,256]{1,0:T(8,128)(2,1)S(1)} collective-permute-done((bf16[512,256]{1,0:T(8,128)(2,1)S(1)}, bf16[512,256]{1,0:T(8,128)(2,1)S(1)}, u32[]{:S(2)}, u32[]{:S(2)}) %collective-permute-start.1) | collective-permute-done | bytes 262176 | tf_op jit(solution)/shard_map/ppermute | solution.py:253
  199.3 6.6 %collective-permute-done.2 = bf16[512,256]{1,0:T(8,128)(2,1)S(1)} collective-permute-done((bf16[512,256]{1,0:T(8,128)(2,1)S(1)}, bf16[512,256]{1,0:T(8,128)(2,1)S(1)}, u32[]{:S(2)}, u32[]{:S(2)}) %collective-permute-start.2) | collective-permute-done | bytes 262176 | tf_op jit(solution)/shard_map/ppermute | solution.py:253
  207.2 1.6 collective-permute-start.4
  209.9 2.3 collective-permute-start.6
  213.4 2.5 collective-permute-done.5
  216.9 6.2 %collective-permute-start.10 = (bf16[16,256]{1,0:T(8,128)(2,1)S(1)}, bf16[16,256]{1,0:T(8,128)(2,1)S(1)}, u32[]{:S(2)}, u32[]{:S(2)}) collective-permute-start(bf16[16,256]{1,0:T(8,128)(2,1)S(1)} %get-tuple-element.40), channel_id=1, source_target_pairs={{0,32},{4,36},{8,40},{12,44},{16,48},{20,52},{24,56},{28,60},{32,0... | collective-permute-start | bytes 24584 | tf_op jit(solution)/shard_map/ppermute | solution.py:263
  223.1 1.6 collective-permute-start.12
  225.2 1.6 collective-permute-start.7
  226.8 3.1 %collective-permute-start.8 = (bf16[16,256]{1,0:T(8,128)(2,1)S(1)}, bf16[16,256]{1,0:T(8,128)(2,1)S(1)}, u32[]{:S(2)}, u32[]{:S(2)}) collective-permute-start(bf16[16,256]{1,0:T(8,128)(2,1)S(1)} %get-tuple-element.42), channel_id=1, source_target_pairs={{0,16},{4,20},{8,24},{12,28},{16,32},{20,36},{24,40},{28,44},{32,4... | collective-permute-start | bytes 24584 | tf_op jit(solution)/shard_map/ppermute | solution.py:263
  229.9 3.2 %collective-permute-start.9 = (bf16[16,256]{1,0:T(8,128)(2,1)S(1)}, bf16[16,256]{1,0:T(8,128)(2,1)S(1)}, u32[]{:S(2)}, u32[]{:S(2)}) collective-permute-start(bf16[16,256]{1,0:T(8,128)(2,1)S(1)} %get-tuple-element.41), channel_id=1, source_target_pairs={{0,24},{4,28},{8,32},{12,36},{16,40},{20,44},{24,48},{28,52},{32,5... | collective-permute-start | bytes 24584 | tf_op jit(solution)/shard_map/ppermute | solution.py:263
  233.4 3.2 %collective-permute-done.9 = bf16[16,256]{1,0:T(8,128)(2,1)S(1)} collective-permute-done((bf16[16,256]{1,0:T(8,128)(2,1)S(1)}, bf16[16,256]{1,0:T(8,128)(2,1)S(1)}, u32[]{:S(2)}, u32[]{:S(2)}) %collective-permute-start.9) | collective-permute-done | bytes 8224 | tf_op jit(solution)/shard_map/ppermute | solution.py:263
  236.6 1.6 collective-permute-start.14
  238.2 3.0 %collective-permute-start.15 = (bf16[16,256]{1,0:T(8,128)(2,1)S(1)}, bf16[16,256]{1,0:T(8,128)(2,1)S(1)}, u32[]{:S(2)}, u32[]{:S(2)}) collective-permute-start(bf16[16,256]{1,0:T(8,128)(2,1)S(1)} %get-tuple-element.28), channel_id=1, source_target_pairs={{0,2},{1,3},{2,0},{3,1},{4,6},{5,7},{6,4},{7,5},{8,10},{9,11},{10,... | collective-permute-start | bytes 24584 | tf_op jit(solution)/shard_map/ppermute | solution.py:269
  244.8 3.1 %unpack_a.1 = (bf16[512,1024]{1,0:T(8,128)(2,1)}, bf16[512,1024]{1,0:T(8,128)(2,1)}, bf16[512,1024]{1,0:T(8,128)(2,1)}) custom-call(bf16[512,512]{1,0:T(8,128)(2,1)S(1)} %bitcast.71, bf16[512,1536]{1,0:T(8,128)(2,1)} %bitcast.12.refs_1_), custom_call_target="tpu_custom_call" | custom-call | flops 805306368 | bytes 3145728 | tf_op jit(solution)/shard_map/unpack_a/pallas_call | solution.py:203
  247.9 2.1 unpack_b.1
  (57 shorter events, 22.7 us)
Async XLA Ops:
  0.6 1.2 copy-start.4
  1.9 1.2 copy-start.6
  3.1 1.2 copy-start.8
  4.3 1.2 copy-start.10
  9.9 12.0 %copy-start.5 = (bf16[1,512,1024]{2,1,0:T(8,128)(2,1)S(1)}, bf16[1,512,1024]{2,1,0:T(8,128)(2,1)}, u32[]{:S(2)}) copy-start(bf16[1,512,1024]{2,1,0:T(8,128)(2,1)} %param.6) | copy-start | bytes 3145732
  9.9 75.2 %all-to-all-start = ((bf16[64,8,2688]{2,1,0:T(8,128)(2,1)}), bf16[64,8,2688]{2,1,0:T(8,128)(2,1)}, u32[]{:S(2)}, u32[]{:S(2)}) async-start(bf16[64,8,2688]{2,1,0:T(8,128)(2,1)} %bitcast.82), calls=%async_computation | async-start | bytes 5505024 | tf_op jit(solution)/shard_map/all_to_all | solution.py:134
  21.9 1.2 copy-start.7
  23.1 1.2 copy-start.9
  85.0 45.9 %all-to-all-start.1 = ((bf16[64,8,1536]{2,1,0:T(8,128)(2,1)}), bf16[64,8,1536]{2,1,0:T(8,128)(2,1)S(1)}, u32[]{:S(2)}, u32[]{:S(2)}) async-start(bf16[64,8,1536]{2,1,0:T(8,128)(2,1)} %bitcast.7), calls=%async_computation.1 | async-start | bytes 3145728 | tf_op jit(solution)/shard_map/all_to_all | solution.py:134
  92.6 1.6 copy-start
  131.0 46.0 %all-to-all-start.3 = ((bf16[64,8,1536]{2,1,0:T(8,128)(2,1)}), bf16[64,8,1536]{2,1,0:T(8,128)(2,1)}, u32[]{:S(2)}, u32[]{:S(2)}) async-start(bf16[64,8,1536]{2,1,0:T(8,128)(2,1)} %bitcast.74), calls=%async_computation.3 | async-start | bytes 3145728 | tf_op jit(solution)/shard_map/all_to_all | solution.py:134
  138.6 1.6 copy-start.1
  148.1 5.0 %copy-start.2 = (bf16[512,1536]{1,0:T(8,128)(2,1)}, bf16[512,1536]{1,0:T(8,128)(2,1)S(1)}, u32[]{:S(2)}) copy-start(bf16[512,1536]{1,0:T(8,128)(2,1)S(1)} %get-tuple-element.18) | copy-start | bytes 4718596
  154.9 29.5 %collective-permute-start = (bf16[32,16,1024]{2,1,0:T(8,128)(2,1)S(1)}, bf16[32,16,1024]{2,1,0:T(8,128)(2,1)}, u32[]{:S(2)}, u32[]{:S(2)}) collective-permute-start(bf16[32,16,1024]{2,1,0:T(8,128)(2,1)S(1)} %fusion), channel_id=1, source_target_pairs={{0,4},{4,0},{8,12},{12,8},{16,20},{20,16},{24,28},{28,24},{32,36},... | collective-permute-start | bytes 3145736 | tf_op jit(solution)/shard_map/ppermute | solution.py:247
  176.9 71.0 %all-to-all-start.2 = ((bf16[64,8,1536]{2,1,0:T(8,128)(2,1)}), bf16[64,8,1536]{2,1,0:T(8,128)(2,1)S(1)}, u32[]{:S(2)}, u32[]{:S(2)}) async-start(bf16[64,8,1536]{2,1,0:T(8,128)(2,1)} %bitcast.73), calls=%async_computation.2 | async-start | bytes 3145728 | tf_op jit(solution)/shard_map/all_to_all | solution.py:134
  189.7 9.6 %collective-permute-start.1 = (bf16[512,256]{1,0:T(8,128)(2,1)S(1)}, bf16[512,256]{1,0:T(8,128)(2,1)S(1)}, u32[]{:S(2)}, u32[]{:S(2)}) collective-permute-start(bf16[512,256]{1,0:T(8,128)(2,1)S(1)} %get-tuple-element.30), channel_id=1, source_target_pairs={{0,1},{1,2},{2,3},{3,0},{4,5},{5,6},{6,7},{7,4},{8,9},{9,10},{10,1... | collective-permute-start | bytes 786440 | tf_op jit(solution)/shard_map/ppermute | solution.py:253
  191.2 14.6 %collective-permute-start.2 = (bf16[512,256]{1,0:T(8,128)(2,1)S(1)}, bf16[512,256]{1,0:T(8,128)(2,1)S(1)}, u32[]{:S(2)}, u32[]{:S(2)}) collective-permute-start(bf16[512,256]{1,0:T(8,128)(2,1)S(1)} %get-tuple-element.32), channel_id=1, source_target_pairs={{0,2},{1,3},{2,0},{3,1},{4,6},{5,7},{6,4},{7,5},{8,10},{9,11},{10,... | collective-permute-start | bytes 786440 | tf_op jit(solution)/shard_map/ppermute | solution.py:253
  194.0 11.9 %collective-permute-start.3 = (bf16[512,256]{1,0:T(8,128)(2,1)S(1)}, bf16[512,256]{1,0:T(8,128)(2,1)}, u32[]{:S(2)}, u32[]{:S(2)}) collective-permute-start(bf16[512,256]{1,0:T(8,128)(2,1)S(1)} %get-tuple-element.31), channel_id=1, source_target_pairs={{0,3},{1,0},{2,1},{3,2},{4,7},{5,4},{6,5},{7,6},{8,11},{9,8},{10,9... | collective-permute-start | bytes 786440 | tf_op jit(solution)/shard_map/ppermute | solution.py:253
  207.2 6.3 %collective-permute-start.4 = (bf16[128,256]{1,0:T(8,128)(2,1)S(1)}, bf16[128,256]{1,0:T(8,128)(2,1)S(1)}, u32[]{:S(2)}, u32[]{:S(2)}) collective-permute-start(bf16[128,256]{1,0:T(8,128)(2,1)S(1)} %get-tuple-element.33), channel_id=1, source_target_pairs={{0,64},{4,68},{8,72},{12,76},{16,80},{20,84},{24,88},{28,92},{32,9... | collective-permute-start | bytes 196616 | tf_op jit(solution)/shard_map/ppermute | solution.py:258
  208.8 7.1 %collective-permute-start.5 = (bf16[128,256]{1,0:T(8,128)(2,1)S(1)}, bf16[128,256]{1,0:T(8,128)(2,1)S(1)}, u32[]{:S(2)}, u32[]{:S(2)}) collective-permute-start(bf16[128,256]{1,0:T(8,128)(2,1)S(1)} %get-tuple-element.35), channel_id=1, source_target_pairs={{0,128},{4,132},{8,136},{12,140},{16,144},{20,148},{24,152},{28,15... | collective-permute-start | bytes 196616 | tf_op jit(solution)/shard_map/ppermute | solution.py:258
  209.9 7.0 %collective-permute-start.6 = (bf16[128,256]{1,0:T(8,128)(2,1)S(1)}, bf16[128,256]{1,0:T(8,128)(2,1)S(1)}, u32[]{:S(2)}, u32[]{:S(2)}) collective-permute-start(bf16[128,256]{1,0:T(8,128)(2,1)S(1)} %get-tuple-element.34), channel_id=1, source_target_pairs={{0,192},{4,196},{8,200},{12,204},{16,208},{20,212},{24,216},{28,22... | collective-permute-start | bytes 196616 | tf_op jit(solution)/shard_map/ppermute | solution.py:258
  216.9 9.9 %collective-permute-start.10 = (bf16[16,256]{1,0:T(8,128)(2,1)S(1)}, bf16[16,256]{1,0:T(8,128)(2,1)S(1)}, u32[]{:S(2)}, u32[]{:S(2)}) collective-permute-start(bf16[16,256]{1,0:T(8,128)(2,1)S(1)} %get-tuple-element.40), channel_id=1, source_target_pairs={{0,32},{4,36},{8,40},{12,44},{16,48},{20,52},{24,56},{28,60},{32,0... | collective-permute-start | bytes 24584 | tf_op jit(solution)/shard_map/ppermute | solution.py:263
  223.1 6.8 %collective-permute-start.11 = (bf16[16,256]{1,0:T(8,128)(2,1)S(1)}, bf16[16,256]{1,0:T(8,128)(2,1)S(1)}, u32[]{:S(2)}, u32[]{:S(2)}) collective-permute-start(bf16[16,256]{1,0:T(8,128)(2,1)S(1)} %get-tuple-element.39), channel_id=1, source_target_pairs={{0,40},{4,44},{8,48},{12,52},{16,56},{20,60},{24,0},{28,4},{32,8},... | collective-permute-start | bytes 24584 | tf_op jit(solution)/shard_map/ppermute | solution.py:263
  223.1 10.2 %collective-permute-start.12 = (bf16[16,256]{1,0:T(8,128)(2,1)S(1)}, bf16[16,256]{1,0:T(8,128)(2,1)S(1)}, u32[]{:S(2)}, u32[]{:S(2)}) collective-permute-start(bf16[16,256]{1,0:T(8,128)(2,1)S(1)} %get-tuple-element.38), channel_id=1, source_target_pairs={{0,48},{4,52},{8,56},{12,60},{16,0},{20,4},{24,8},{28,12},{32,16},... | collective-permute-start | bytes 24584 | tf_op jit(solution)/shard_map/ppermute | solution.py:263
  224.7 8.6 %collective-permute-start.13 = (bf16[16,256]{1,0:T(8,128)(2,1)S(1)}, bf16[16,256]{1,0:T(8,128)(2,1)S(1)}, u32[]{:S(2)}, u32[]{:S(2)}) collective-permute-start(bf16[16,256]{1,0:T(8,128)(2,1)S(1)} %get-tuple-element.37), channel_id=1, source_target_pairs={{0,56},{4,60},{8,0},{12,4},{16,8},{20,12},{24,16},{28,20},{32,24},... | collective-permute-start | bytes 24584 | tf_op jit(solution)/shard_map/ppermute | solution.py:263
  225.2 8.2 %collective-permute-start.7 = (bf16[16,256]{1,0:T(8,128)(2,1)S(1)}, bf16[16,256]{1,0:T(8,128)(2,1)S(1)}, u32[]{:S(2)}, u32[]{:S(2)}) collective-permute-start(bf16[16,256]{1,0:T(8,128)(2,1)S(1)} %get-tuple-element.36), channel_id=1, source_target_pairs={{0,8},{4,12},{8,16},{12,20},{16,24},{20,28},{24,32},{28,36},{32,40... | collective-permute-start | bytes 24584 | tf_op jit(solution)/shard_map/ppermute | solution.py:263
  226.8 6.6 %collective-permute-start.8 = (bf16[16,256]{1,0:T(8,128)(2,1)S(1)}, bf16[16,256]{1,0:T(8,128)(2,1)S(1)}, u32[]{:S(2)}, u32[]{:S(2)}) collective-permute-start(bf16[16,256]{1,0:T(8,128)(2,1)S(1)} %get-tuple-element.42), channel_id=1, source_target_pairs={{0,16},{4,20},{8,24},{12,28},{16,32},{20,36},{24,40},{28,44},{32,4... | collective-permute-start | bytes 24584 | tf_op jit(solution)/shard_map/ppermute | solution.py:263
  229.9 6.7 %collective-permute-start.9 = (bf16[16,256]{1,0:T(8,128)(2,1)S(1)}, bf16[16,256]{1,0:T(8,128)(2,1)S(1)}, u32[]{:S(2)}, u32[]{:S(2)}) collective-permute-start(bf16[16,256]{1,0:T(8,128)(2,1)S(1)} %get-tuple-element.41), channel_id=1, source_target_pairs={{0,24},{4,28},{8,32},{12,36},{16,40},{20,44},{24,48},{28,52},{32,5... | collective-permute-start | bytes 24584 | tf_op jit(solution)/shard_map/ppermute | solution.py:263
  236.6 5.5 %collective-permute-start.14 = (bf16[16,256]{1,0:T(8,128)(2,1)S(1)}, bf16[16,256]{1,0:T(8,128)(2,1)S(1)}, u32[]{:S(2)}, u32[]{:S(2)}) collective-permute-start(bf16[16,256]{1,0:T(8,128)(2,1)S(1)} %get-tuple-element.28), channel_id=1, source_target_pairs={{0,1},{1,2},{2,3},{3,0},{4,5},{5,6},{6,7},{7,4},{8,9},{9,10},{10,1... | collective-permute-start | bytes 24584 | tf_op jit(solution)/shard_map/ppermute | solution.py:269
  238.2 5.2 %collective-permute-start.15 = (bf16[16,256]{1,0:T(8,128)(2,1)S(1)}, bf16[16,256]{1,0:T(8,128)(2,1)S(1)}, u32[]{:S(2)}, u32[]{:S(2)}) collective-permute-start(bf16[16,256]{1,0:T(8,128)(2,1)S(1)} %get-tuple-element.28), channel_id=1, source_target_pairs={{0,2},{1,3},{2,0},{3,1},{4,6},{5,7},{6,4},{7,5},{8,10},{9,11},{10,... | collective-permute-start | bytes 24584 | tf_op jit(solution)/shard_map/ppermute | solution.py:269
  241.1 3.7 %collective-permute-start.16 = (bf16[16,256]{1,0:T(8,128)(2,1)S(1)}, bf16[16,256]{1,0:T(8,128)(2,1)S(1)}, u32[]{:S(2)}, u32[]{:S(2)}) collective-permute-start(bf16[16,256]{1,0:T(8,128)(2,1)S(1)} %get-tuple-element.28), channel_id=1, source_target_pairs={{0,3},{1,0},{2,1},{3,2},{4,7},{5,4},{6,5},{7,6},{8,11},{9,8},{10,9... | collective-permute-start | bytes 24584 | tf_op jit(solution)/shard_map/ppermute | solution.py:269
  244.8 5.2 %copy-start.12 = (f32[16,1024]{1,0:T(8,128)}, f32[16,1024]{1,0:T(8,128)S(1)}, u32[]{:S(2)}) copy-start(f32[16,1024]{1,0:T(8,128)S(1)} %convert_dynamic-update-slice_fusion) | copy-start | bytes 196612
  (2 other events, 1.8 us)
where the time goes:
time: 251 us; the launch traced here: 250 us
  waiting for transfers between devices  129 us (51%)
  starting transfers between devices  67.2 us (27%)
  Pallas kernels  27.2 us (11%)
  local copies, waits for them, and re-layouts  15.8 us (6%)
  other arithmetic  5.04 us (2%)
  matrix products  5.03 us (2%)
    all_to_all x4, waiting for transfers between devices, exchange(): lax.all_to_all(rows_in.reshape(node_count, bucket, c), 'nodes', split_axi...  108 us
    all_to_all x4, starting transfers between devices, exchange(): lax.all_to_all(rows_in.reshape(node_count, bucket, c), 'nodes', split_axi...  34.6 us
    ppermute x7, starting transfers between devices, local(): total = total + lax.ppermute(sent, 'nodes', hop(0, s, 0))  16.2 us
    pallas_call x2, Pallas kernels, attention(): pl.pallas_call(lambda *refs: attend(scale, *refs), out_shape=(sds((rows,...  15.9 us
    unnamed x26, local copies, waits for them, and re-layouts  12.3 us
    ppermute x3, waiting for transfers between devices, local(): total = total + lax.ppermute(sent, 'rep', ring(nx, s))  10.5 us
    ppermute x3, starting transfers between devices, local(): total = total + lax.ppermute(sent, 'rep', ring(nx, s))  5.73 us
    ppermute x3, starting transfers between devices, local(): came = lax.ppermute(low, 'rep', ring(nx, s)).astype(F32)  5.52 us
  transfers between devices with their start and end apart: 21, of which 11 were waited for; matrix products, arithmetic and copies ran while one was open for 5% of the time, Pallas kernels for 9%

commit v1 on v0

--- a/solution.py
+++ b/solution.py
@@ -6,6 +6,7 @@
 from jax.experimental import pallas as pl
 from jax.experimental.pallas import tpu as pltpu
 from jax.sharding import PartitionSpec as P
+
 
 HEAD_DIM = 128
 CL_DEV = 4
@@ -68,8 +69,6 @@
 
 
 def attend(scale, g_ref, tag_ref, w_ref, q_ref, k_ref, v_ref, ret_ref, att_ref, bias_ref):
-    rows = g_ref.shape[0]
-
     @pl.when(pl.program_id(0) == 0)
     def _():
         tags = tag_ref[...].astype(F32)
@@ -99,12 +98,22 @@
         ref[...] = nn(back_ref[...], ret_ref[:, m * UNIT : (m + 1) * UNIT]).astype(BF)
 
 
+def spread(nx, at_ref, *refs):
+    ins, out_ref = refs[:nx], refs[nx]
+    half = ins[0].shape[1] // 2
+    for s, ref in enumerate(ins):
+        source = lax.rem(at_ref[0] + s, nx)
+        for m in range(2):
+            cols = pl.ds(pl.multiple_of((m * nx + source) * half, half), half)
+            out_ref[:, cols] = ref[:, m * half : (m + 1) * half].astype(F32)
+
+
 def cost(flops, nbytes, exps=0):
     return pl.CostEstimate(flops=flops, bytes_accessed=nbytes, transcendentals=exps)
 
 
 def params():
-    return pltpu.CompilerParams(vmem_limit_bytes=48 * 1024 * 1024)
+    return pltpu.CompilerParams(vmem_limit_bytes=67043328)
 
 
 def ring(size, shift):
@@ -132,7 +141,11 @@
     def exchange(rows_in):
         c = rows_in.shape[1]
         out = lax.all_to_all(
-            rows_in.reshape(node_count, bucket, c), "nodes", split_axis=0, concat_axis=0, tiled=True
+            rows_in.reshape(node_count, bucket, c),
+            "nodes",
+            split_axis=0,
+            concat_axis=0,
+            tiled=True,
         )
         return out.reshape(rows, c)
 
@@ -238,37 +251,56 @@
     def pick_of(array, index, axis):
         return lax.dynamic_index_in_dim(array, index, axis, keepdims=False)
 
-    att = jnp.concatenate([att_a, att_b], axis=1)
-    weight = tn(recv_a[:, :width], att)
-    weight = weight.reshape(ny * nz, nc, width // node_count, width)
-    total = pick_of(weight, ic, 1)
-    for s in range(1, nc):
-        sent = pick_of(weight, (ic + s) % nc, 1).astype(BF)
-        total = total + lax.ppermute(sent, "nodes", hop(0, 0, s))
     share = width // nx
-    weight = total.reshape(width // nc, width)
-    total = lax.dynamic_slice_in_dim(weight, ix * share, share, 1)
-    for s in range(1, nx):
-        sent = lax.dynamic_slice_in_dim(weight, ((ix + s) % nx) * share, share, 1).astype(BF)
-        total = total + lax.ppermute(sent, "rep", ring(nx, s))
-    weight = total.reshape(ny, width // nc // ny, share)
-    total = pick_of(weight, iy, 0)
+
+    def reduced_over_chip_and_x(att):
+        part = att.shape[1] // nx
+        weight = tn(recv_a[:, :width], att)
+        weight = weight.reshape(ny * nz, nc, width // node_count, att.shape[1])
+        total = pick_of(weight, ic, 1)
+        for s in range(1, nc):
+            sent = pick_of(weight, (ic + s) % nc, 1).astype(BF)
+            total = total + lax.ppermute(sent, "nodes", hop(0, 0, s))
+        weight = total.reshape(width // nc, att.shape[1])
+        came = []
+        for s in range(1, nx):
+            sent = lax.dynamic_slice_in_dim(weight, ((ix + s) % nx) * part, part, 1).astype(BF)
+            came.append(lax.ppermute(sent, "rep", ring(nx, s)))
+        total = lax.dynamic_slice_in_dim(weight, ix * part, part, 1)
+        for piece in came:
+            total = total + piece
+        return lax.optimization_barrier(total)
+
+    total_a = reduced_over_chip_and_x(att_a)
+    att_b, total_a = lax.optimization_barrier((att_b, total_a))
+    weight = jnp.concatenate([total_a, reduced_over_chip_and_x(att_b)], axis=1)
+    weight = weight.reshape(ny, width // nc // ny, share)
+    came = []
     for s in range(1, ny):
         sent = pick_of(weight, (iy + s) % ny, 0).astype(BF)
-        total = total + lax.ppermute(sent, "nodes", hop(s, 0, 0))
+        came.append(lax.ppermute(sent, "nodes", hop(s, 0, 0)))
+    total = pick_of(weight, iy, 0)
+    for piece in came:
+        total = total + piece
+    total = lax.optimization_barrier(total)
     weight = total.reshape(nz, width // node_count, share)
-    total = pick_of(weight, iz, 0)
+    came = []
     for s in range(1, nz):
         sent = pick_of(weight, (iz + s) % nz, 0).astype(BF)
-        total = total + lax.ppermute(sent, "nodes", hop(0, s, 0))
-    total = total * norm_factor
-    grad_weight = jnp.zeros((width // node_count, width), F32)
-    grad_weight = lax.dynamic_update_slice_in_dim(grad_weight, total, ix * share, 1)
-    low = total.astype(BF)
-    for s in range(1, nx):
-        came = lax.ppermute(low, "rep", ring(nx, s)).astype(F32)
-        at = ((ix + nx - s) % nx) * share
-        grad_weight = lax.dynamic_update_slice_in_dim(grad_weight, came, at, 1)
+        came.append(lax.ppermute(sent, "nodes", hop(0, s, 0)))
+    total = pick_of(weight, iz, 0)
+    for piece in came:
+        total = total + piece
+    low = (total * norm_factor).astype(BF)
+    pieces = [low] + [lax.ppermute(low, "rep", ring(nx, nx - s)) for s in range(1, nx)]
+    grad_weight = pl.pallas_call(
+        lambda *refs: spread(nx, *refs),
+        out_shape=sds((width // node_count, width), F32),
+        in_specs=[pl.BlockSpec(memory_space=pltpu.SMEM)]
+        + [pl.BlockSpec(memory_space=pltpu.VMEM)] * nx,
+        cost_estimate=cost(0, 6 * width // node_count * width),
+        name="spread",
+    )(ix.reshape(1), *pieces)
     return (outs[0][None], outs[1][None], outs[2][None], grad_weight)
 
 

time: 251 us -> 254 us (1.012)
  local copies, waits for them, and re-layouts: 15.8 us -> 4.19 us
  Pallas kernels: 27.2 us -> 34.9 us
  starting transfers between devices: 67.2 us -> 73.4 us
  other arithmetic: 5.04 us -> 2.02 us
  waiting for transfers between devices: 129 us -> 132 us
    unnamed x26 -> x16, local copies, waits for them, and re-layouts: 12.3 us -> 1.95 us
    ppermute x17 -> x21, starting transfers between devices: 32.6 us -> 38.5 us  [the longest x7 17.2 us: local(): came.append(lax.ppermute(sent, 'nodes', hop(0, s, 0)))]
    all_to_all x4, waiting for transfers between devices: 108 us -> 112 us  [exchange(): lax.all_to_all(rows_in.reshape(node_count, bucket, c), 'nodes', split_axi...]
    add x3 -> x5, other arithmetic: 5.01 us -> 1.93 us  [the longest x2 1.79 us: reduced_over_chip_and_x(): total = total + lax.ppermute(sent, 'nodes', hop(0, 0, s))]
    ppermute x17 -> x21, waiting for transfers between devices: 21 us -> 19.4 us  [the longest x6 9.72 us: reduced_over_chip_and_x(): came.append(lax.ppermute(sent, 'rep', ring(nx, s)))]
  transfers between devices with their start and end apart: 21 -> 25, of which waited for: 11 -> 14; matrix products, arithmetic and copies ran while one was open for 5% -> 3% of each run, Pallas kernels for 9% -> 10%
where the time goes in v1:
time: 254 us; the launch traced here: 251 us
  waiting for transfers between devices  132 us (52%)
  starting transfers between devices  73.4 us (29%)
  Pallas kernels  34.9 us (14%)
  local copies, waits for them, and re-layouts  4.19 us (2%)
  matrix products  3.94 us (2%)
    all_to_all x4, waiting for transfers between devices, exchange(): lax.all_to_all(rows_in.reshape(node_count, bucket, c), 'nodes', split_axi...  112 us
    all_to_all x4, starting transfers between devices, exchange(): lax.all_to_all(rows_in.reshape(node_count, bucket, c), 'nodes', split_axi...  34.9 us
    pallas_call x2, Pallas kernels, attention(): pl.pallas_call(lambda *refs: attend(scale, *refs), out_shape=(sds((rows,...  18.1 us
    ppermute x7, starting transfers between devices, local(): came.append(lax.ppermute(sent, 'nodes', hop(0, s, 0)))  17.2 us
    ppermute x6, starting transfers between devices, reduced_over_chip_and_x(): came.append(lax.ppermute(sent, 'rep', ring(nx, s)))  11.1 us
    ppermute x6, waiting for transfers between devices, reduced_over_chip_and_x(): came.append(lax.ppermute(sent, 'rep', ring(nx, s)))  9.72 us
    ppermute x3, starting transfers between devices, local(): came.append(lax.ppermute(sent, 'nodes', hop(s, 0, 0)))  5.6 us
    pallas_call x1, Pallas kernels, local(): pl.pallas_call(lambda *refs: pack_first(rows, bucket, *refs), out_shape=(...  5.39 us
  transfers between devices with their start and end apart: 25, of which 14 were waited for; matrix products, arithmetic and copies ran while one was open for 3% of the time, Pallas kernels for 10%

profile of v1, /device:TPU:40, one launch (start us, length us, event | category | flops | bytes accessed | tf_op | source)
XLA Modules:
  0.0 251.1 jit_solution(12751004374877009041)
XLA Ops:
  0.6 5.4 %pack_first.1 = (bf16[512,2688]{1,0:T(8,128)(2,1)}, bf16[512,512]{1,0:T(8,128)(2,1)}) custom-call(s32[1,512]{1,0:T(1,128)} %refs_0_.1, bf16[512,1024]{1,0:T(8,128)(2,1)} %bitcast.103, bf16[512,1024]{1,0:T(8,128)(2,1)} %bitcast.92, bf16[512,1024]{1,0:T(8,128)(2,1)} %bitcast.94, bf16[512,1024]{1,0:T(8,128)(2,1)} %bitcast.96), custom_call_target="tpu_custom_call" | custom-call | flops 1409286144 | bytes 5505024 | tf_op jit(solution)/shard_map/pack_first/pallas_call | solution.py:154
  6.0 11.8 %all-to-all-start = ((bf16[64,8,2688]{2,1,0:T(8,128)(2,1)}), bf16[64,8,2688]{2,1,0:T(8,128)(2,1)}, u32[]{:S(2)}, u32[]{:S(2)}) async-start(bf16[64,8,2688]{2,1,0:T(8,128)(2,1)} %bitcast.86), calls=%async_computation | async-start | bytes 5505024 | tf_op jit(solution)/shard_map/all_to_all | solution.py:143
  17.8 3.5 %pack_rest.1 = bf16[512,1536]{1,0:T(8,128)(2,1)} custom-call(bf16[512,512]{1,0:T(8,128)(2,1)} %get-tuple-element.18.pick_ref, bf16[512,1024]{1,0:T(8,128)(2,1)} %bitcast.93, bf16[512,1024]{1,0:T(8,128)(2,1)} %bitcast.95, bf16[512,1024]{1,0:T(8,128)(2,1)} %bitcast.97), custom_call_target="tpu_custom_call" | custom-call | flops 805306368 | bytes 3145728 | tf_op jit(solution)/shard_map/pack_rest/pallas_call | solution.py:167
  21.4 59.7 %all-to-all-done = bf16[64,8,2688]{2,1,0:T(8,128)(2,1)} async-done(((bf16[64,8,2688]{2,1,0:T(8,128)(2,1)}), bf16[64,8,2688]{2,1,0:T(8,128)(2,1)}, u32[]{:S(2)}, u32[]{:S(2)}) %all-to-all-start) | async-done | bytes 2752544 | tf_op jit(solution)/shard_map/all_to_all | solution.py:143
  81.0 7.7 %all-to-all-start.1 = ((bf16[64,8,1536]{2,1,0:T(8,128)(2,1)}), bf16[64,8,1536]{2,1,0:T(8,128)(2,1)}, u32[]{:S(2)}, u32[]{:S(2)}) async-start(bf16[64,8,1536]{2,1,0:T(8,128)(2,1)} %bitcast.81), calls=%async_computation.1 | async-start | bytes 3145728 | tf_op jit(solution)/shard_map/all_to_all | solution.py:143
  88.7 9.0 %attend.3 = (bf16[512,1536]{1,0:T(8,128)(2,1)}, bf16[512,512]{1,0:T(8,128)(2,1)}) custom-call(bf16[512,2688]{1,0:T(8,128)(2,1)} %bitcast.6.refs_0_.refs_1_.refs_3_.refs_4_.refs_5_, bf16[512,2688]{1,0:T(8,128)(2,1)} %bitcast.6.refs_0_.refs_1_.refs_3_.refs_4_.refs_5_, bf16[1024,1024]{1,0:T(8,128)(2,1)} %refs_2_.3, ...), custom_call_target="tpu_custom_call" | custom-call | flops 2147483648 | bytes 5767168 | tf_op jit(solution)/shard_map/attend/pallas_call | solution.py:184
  97.8 29.3 %all-to-all-done.1 = bf16[64,8,1536]{2,1,0:T(8,128)(2,1)} async-done(((bf16[64,8,1536]{2,1,0:T(8,128)(2,1)}), bf16[64,8,1536]{2,1,0:T(8,128)(2,1)}, u32[]{:S(2)}, u32[]{:S(2)}) %all-to-all-start.1) | async-done | bytes 1572896 | tf_op jit(solution)/shard_map/all_to_all | solution.py:143
  127.1 7.6 %all-to-all-start.3 = ((bf16[64,8,1536]{2,1,0:T(8,128)(2,1)}), bf16[64,8,1536]{2,1,0:T(8,128)(2,1)}, u32[]{:S(2)}, u32[]{:S(2)}) async-start(bf16[64,8,1536]{2,1,0:T(8,128)(2,1)} %bitcast.89), calls=%async_computation.3 | async-start | bytes 3145728 | tf_op jit(solution)/shard_map/all_to_all | solution.py:143
  134.7 2.0 fusion.2
  139.1 9.1 %attend.2 = (bf16[512,1536]{1,0:T(8,128)(2,1)}, bf16[512,512]{1,0:T(8,128)(2,1)}) custom-call(bf16[512,2688]{1,0:T(8,128)(2,1)} %bitcast.6.refs_0_.refs_1_.refs_3_.refs_4_.refs_5_, bf16[512,2688]{1,0:T(8,128)(2,1)} %bitcast.6.refs_0_.refs_1_.refs_3_.refs_4_.refs_5_, bf16[1024,1024]{1,0:T(8,128)(2,1)} %refs_2_.3, ...), custom_call_target="tpu_custom_call" | custom-call | flops 2147483648 | bytes 5767168 | tf_op jit(solution)/shard_map/attend/pallas_call | solution.py:184
  148.2 1.6 bitcast_add_fusion.1
  149.8 23.3 %all-to-all-done.3 = bf16[64,8,1536]{2,1,0:T(8,128)(2,1)} async-done(((bf16[64,8,1536]{2,1,0:T(8,128)(2,1)}), bf16[64,8,1536]{2,1,0:T(8,128)(2,1)}, u32[]{:S(2)}, u32[]{:S(2)}) %all-to-all-start.3) | async-done | bytes 1572896 | tf_op jit(solution)/shard_map/all_to_all | solution.py:143
  173.0 7.8 %all-to-all-start.2 = ((bf16[64,8,1536]{2,1,0:T(8,128)(2,1)}), bf16[64,8,1536]{2,1,0:T(8,128)(2,1)}, u32[]{:S(2)}, u32[]{:S(2)}) async-start(bf16[64,8,1536]{2,1,0:T(8,128)(2,1)} %bitcast.9), calls=%async_computation.2 | async-start | bytes 3145728 | tf_op jit(solution)/shard_map/all_to_all | solution.py:143
  180.9 1.6 collective-permute-start.1
  182.5 2.7 %collective-permute-start.2 = (bf16[512,128]{1,0:T(8,128)(2,1)S(1)}, bf16[512,128]{1,0:T(8,128)(2,1)S(1)}, u32[]{:S(2)}, u32[]{:S(2)}) collective-permute-start(bf16[512,128]{1,0:T(8,128)(2,1)S(1)} %get-tuple-element.37), channel_id=1, source_target_pairs={{0,2},{1,3},{2,0},{3,1},{4,6},{5,7},{6,4},{7,5},{8,10},{9,11},{10,... | collective-permute-start | bytes 393224 | tf_op jit(solution)/shard_map/ppermute | solution.py:268
  187.7 3.8 %collective-permute-done.2 = bf16[512,128]{1,0:T(8,128)(2,1)S(1)} collective-permute-done((bf16[512,128]{1,0:T(8,128)(2,1)S(1)}, bf16[512,128]{1,0:T(8,128)(2,1)S(1)}, u32[]{:S(2)}, u32[]{:S(2)}) %collective-permute-start.2) | collective-permute-done | bytes 131104 | tf_op jit(solution)/shard_map/ppermute | solution.py:268
  191.6 2.0 fusion
  193.8 1.9 collective-permute-done.4
  197.4 2.4 collective-permute-start.6
  201.4 1.8 collective-permute-done.5
  203.2 3.0 %collective-permute-done.6 = bf16[512,128]{1,0:T(8,128)(2,1)S(1)} collective-permute-done((bf16[512,128]{1,0:T(8,128)(2,1)S(1)}, bf16[512,128]{1,0:T(8,128)(2,1)S(1)}, u32[]{:S(2)}, u32[]{:S(2)}) %collective-permute-start.6) | collective-permute-done | bytes 131104 | tf_op jit(solution)/shard_map/ppermute | solution.py:268
  208.5 3.5 %collective-permute-start.9 = (bf16[128,256]{1,0:T(8,128)(2,1)S(1)}, bf16[128,256]{1,0:T(8,128)(2,1)S(1)}, u32[]{:S(2)}, u32[]{:S(2)}) collective-permute-start(bf16[128,256]{1,0:T(8,128)(2,1)S(1)} %get-tuple-element.40), channel_id=1, source_target_pairs={{0,128},{4,132},{8,136},{12,140},{16,144},{20,148},{24,152},{28,15... | collective-permute-start | bytes 196616 | tf_op jit(solution)/shard_map/ppermute | solution.py:281
  212.0 1.7 collective-permute-done.8
  216.1 5.2 %collective-permute-start.12 = (bf16[16,256]{1,0:T(8,128)(2,1)S(1)}, bf16[16,256]{1,0:T(8,128)(2,1)S(1)}, u32[]{:S(2)}, u32[]{:S(2)}) collective-permute-start(bf16[16,256]{1,0:T(8,128)(2,1)S(1)} %get-tuple-element.47), channel_id=1, source_target_pairs={{0,16},{4,20},{8,24},{12,28},{16,32},{20,36},{24,40},{28,44},{32,4... | collective-permute-start | bytes 24584 | tf_op jit(solution)/shard_map/ppermute | solution.py:290
  221.5 2.8 %collective-permute-start.14 = (bf16[16,256]{1,0:T(8,128)(2,1)S(1)}, bf16[16,256]{1,0:T(8,128)(2,1)S(1)}, u32[]{:S(2)}, u32[]{:S(2)}) collective-permute-start(bf16[16,256]{1,0:T(8,128)(2,1)S(1)} %get-tuple-element.45), channel_id=1, source_target_pairs={{0,32},{4,36},{8,40},{12,44},{16,48},{20,52},{24,56},{28,60},{32,0... | collective-permute-start | bytes 24584 | tf_op jit(solution)/shard_map/ppermute | solution.py:290
  224.3 2.2 collective-permute-start.15
  226.6 2.4 collective-permute-start.16
  229.0 3.1 %collective-permute-start.17 = (bf16[16,256]{1,0:T(8,128)(2,1)S(1)}, bf16[16,256]{1,0:T(8,128)(2,1)S(1)}, u32[]{:S(2)}, u32[]{:S(2)}) collective-permute-start(bf16[16,256]{1,0:T(8,128)(2,1)S(1)} %get-tuple-element.42), channel_id=1, source_target_pairs={{0,56},{4,60},{8,0},{12,4},{16,8},{20,12},{24,16},{28,20},{32,24},... | collective-permute-start | bytes 24584 | tf_op jit(solution)/shard_map/ppermute | solution.py:290
  233.6 3.0 %collective-permute-start.18 = (bf16[16,256]{1,0:T(8,128)(2,1)S(1)}, bf16[16,256]{1,0:T(8,128)(2,1)S(1)}, u32[]{:S(2)}, u32[]{:S(2)}) collective-permute-start(bf16[16,256]{1,0:T(8,128)(2,1)S(1)} %fusion.18.refs_1_), channel_id=1, source_target_pairs={{0,3},{1,0},{2,1},{3,2},{4,7},{5,4},{6,5},{7,6},{8,11},{9,8},{10,9... | collective-permute-start | bytes 24584 | tf_op jit(solution)/shard_map/ppermute | solution.py:295
  238.9 2.8 %collective-permute-done.19.refs_3_ = bf16[16,256]{1,0:T(8,128)(2,1)S(1)} collective-permute-done((bf16[16,256]{1,0:T(8,128)(2,1)S(1)}, bf16[16,256]{1,0:T(8,128)(2,1)S(1)}, u32[]{:S(2)}, u32[]{:S(2)}) %collective-permute-start.19) | collective-permute-done | bytes 8224 | tf_op jit(solution)/shard_map/ppermute | solution.py:295
  244.5 3.3 %unpack_a.1 = (bf16[512,1024]{1,0:T(8,128)(2,1)}, bf16[512,1024]{1,0:T(8,128)(2,1)}, bf16[512,1024]{1,0:T(8,128)(2,1)}) custom-call(bf16[512,512]{1,0:T(8,128)(2,1)} %bitcast.87, bf16[512,1536]{1,0:T(8,128)(2,1)} %bitcast.12.refs_1_), custom_call_target="tpu_custom_call" | custom-call | flops 805306368 | bytes 3145728 | tf_op jit(solution)/shard_map/unpack_a/pallas_call | solution.py:216
  247.8 3.3 %unpack_b.1 = (bf16[512,1024]{1,0:T(8,128)(2,1)}, bf16[512,1024]{1,0:T(8,128)(2,1)}, bf16[512,1024]{1,0:T(8,128)(2,1)}) custom-call(bf16[512,512]{1,0:T(8,128)(2,1)} %bitcast.88, bf16[512,1536]{1,0:T(8,128)(2,1)} %bitcast.10.refs_1_, bf16[512,1024]{1,0:T(8,128)(2,1)} %get-tuple-element.22.refs_2_, ...), custom_call_target="tpu_custom_call", output_to_operand_aliasing={{0}: (2, {}), {1}: (3, {}), {2}: (4, {})} | custom-call | flops 805306368 | bytes 3145728 | tf_op jit(solution)/shard_map/unpack_b/pallas_call | solution.py:226
  (57 shorter events, 19.9 us)
Async XLA Ops:
  6.0 75.0 %all-to-all-start = ((bf16[64,8,2688]{2,1,0:T(8,128)(2,1)}), bf16[64,8,2688]{2,1,0:T(8,128)(2,1)}, u32[]{:S(2)}, u32[]{:S(2)}) async-start(bf16[64,8,2688]{2,1,0:T(8,128)(2,1)} %bitcast.86), calls=%async_computation | async-start | bytes 5505024 | tf_op jit(solution)/shard_map/all_to_all | solution.py:143
  81.0 46.0 %all-to-all-start.1 = ((bf16[64,8,1536]{2,1,0:T(8,128)(2,1)}), bf16[64,8,1536]{2,1,0:T(8,128)(2,1)}, u32[]{:S(2)}, u32[]{:S(2)}) async-start(bf16[64,8,1536]{2,1,0:T(8,128)(2,1)} %bitcast.81), calls=%async_computation.1 | async-start | bytes 3145728 | tf_op jit(solution)/shard_map/all_to_all | solution.py:143
  97.8 37.0 %copy-start.2 = (bf16[512,512]{1,0:T(8,128)(2,1)S(1)}, bf16[512,512]{1,0:T(8,128)(2,1)}, u32[]{:S(2)}) copy-start(bf16[512,512]{1,0:T(8,128)(2,1)} %get-tuple-element.29) | copy-start | bytes 1572868
  127.1 46.0 %all-to-all-start.3 = ((bf16[64,8,1536]{2,1,0:T(8,128)(2,1)}), bf16[64,8,1536]{2,1,0:T(8,128)(2,1)}, u32[]{:S(2)}, u32[]{:S(2)}) async-start(bf16[64,8,1536]{2,1,0:T(8,128)(2,1)} %bitcast.89), calls=%async_computation.3 | async-start | bytes 3145728 | tf_op jit(solution)/shard_map/all_to_all | solution.py:143
  136.7 1.4 copy-start
  138.9 9.2 %collective-permute-start = (bf16[32,16,512]{2,1,0:T(8,128)(2,1)}, bf16[32,16,512]{2,1,0:T(8,128)(2,1)}, u32[]{:S(2)}, u32[]{:S(2)}) collective-permute-start(bf16[32,16,512]{2,1,0:T(8,128)(2,1)} %fusion.4), channel_id=1, source_target_pairs={{0,4},{4,0},{8,12},{12,8},{16,20},{20,16},{24,28},{28,24},{32,36},... | collective-permute-start | bytes 1572872 | tf_op jit(solution)/shard_map/ppermute | solution.py:263
  173.0 18.6 %copy-start.3 = (bf16[512,512]{1,0:T(8,128)(2,1)S(1)}, bf16[512,512]{1,0:T(8,128)(2,1)}, u32[]{:S(2)}) copy-start(bf16[512,512]{1,0:T(8,128)(2,1)} %get-tuple-element.31) | copy-start | bytes 1572868
  173.0 74.7 %all-to-all-start.2 = ((bf16[64,8,1536]{2,1,0:T(8,128)(2,1)}), bf16[64,8,1536]{2,1,0:T(8,128)(2,1)}, u32[]{:S(2)}, u32[]{:S(2)}) async-start(bf16[64,8,1536]{2,1,0:T(8,128)(2,1)} %bitcast.9), calls=%async_computation.2 | async-start | bytes 3145728 | tf_op jit(solution)/shard_map/all_to_all | solution.py:143
  180.9 6.8 %collective-permute-start.1 = (bf16[512,128]{1,0:T(8,128)(2,1)S(1)}, bf16[512,128]{1,0:T(8,128)(2,1)S(1)}, u32[]{:S(2)}, u32[]{:S(2)}) collective-permute-start(bf16[512,128]{1,0:T(8,128)(2,1)S(1)} %get-tuple-element.35), channel_id=1, source_target_pairs={{0,1},{1,2},{2,3},{3,0},{4,5},{5,6},{6,7},{7,4},{8,9},{9,10},{10,1... | collective-permute-start | bytes 393224 | tf_op jit(solution)/shard_map/ppermute | solution.py:268
  182.5 9.0 %collective-permute-start.2 = (bf16[512,128]{1,0:T(8,128)(2,1)S(1)}, bf16[512,128]{1,0:T(8,128)(2,1)S(1)}, u32[]{:S(2)}, u32[]{:S(2)}) collective-permute-start(bf16[512,128]{1,0:T(8,128)(2,1)S(1)} %get-tuple-element.37), channel_id=1, source_target_pairs={{0,2},{1,3},{2,0},{3,1},{4,6},{5,7},{6,4},{7,5},{8,10},{9,11},{10,... | collective-permute-start | bytes 393224 | tf_op jit(solution)/shard_map/ppermute | solution.py:268
  185.2 6.3 %collective-permute-start.3 = (bf16[512,128]{1,0:T(8,128)(2,1)S(1)}, bf16[512,128]{1,0:T(8,128)(2,1)S(1)}, u32[]{:S(2)}, u32[]{:S(2)}) collective-permute-start(bf16[512,128]{1,0:T(8,128)(2,1)S(1)} %get-tuple-element.36), channel_id=1, source_target_pairs={{0,3},{1,0},{2,1},{3,2},{4,7},{5,4},{6,5},{7,6},{8,11},{9,8},{10,9... | collective-permute-start | bytes 393224 | tf_op jit(solution)/shard_map/ppermute | solution.py:268
  193.7 2.0 collective-permute-start.4
  195.9 42.0 %copy-start.1 = (bf16[512,512]{1,0:T(8,128)(2,1)S(1)}, bf16[512,512]{1,0:T(8,128)(2,1)}, u32[]{:S(2)}) copy-start(bf16[512,512]{1,0:T(8,128)(2,1)} %get-tuple-element.18.pick_ref) | copy-start | bytes 1572868
  196.0 7.2 %collective-permute-start.5 = (bf16[512,128]{1,0:T(8,128)(2,1)S(1)}, bf16[512,128]{1,0:T(8,128)(2,1)S(1)}, u32[]{:S(2)}, u32[]{:S(2)}) collective-permute-start(bf16[512,128]{1,0:T(8,128)(2,1)S(1)} %get-tuple-element.32), channel_id=1, source_target_pairs={{0,1},{1,2},{2,3},{3,0},{4,5},{5,6},{6,7},{7,4},{8,9},{9,10},{10,1... | collective-permute-start | bytes 393224 | tf_op jit(solution)/shard_map/ppermute | solution.py:268
  197.4 8.7 %collective-permute-start.6 = (bf16[512,128]{1,0:T(8,128)(2,1)S(1)}, bf16[512,128]{1,0:T(8,128)(2,1)S(1)}, u32[]{:S(2)}, u32[]{:S(2)}) collective-permute-start(bf16[512,128]{1,0:T(8,128)(2,1)S(1)} %get-tuple-element.34), channel_id=1, source_target_pairs={{0,2},{1,3},{2,0},{3,1},{4,6},{5,7},{6,4},{7,5},{8,10},{9,11},{10,... | collective-permute-start | bytes 393224 | tf_op jit(solution)/shard_map/ppermute | solution.py:268
  199.8 6.4 %collective-permute-start.7 = (bf16[512,128]{1,0:T(8,128)(2,1)S(1)}, bf16[512,128]{1,0:T(8,128)(2,1)S(1)}, u32[]{:S(2)}, u32[]{:S(2)}) collective-permute-start(bf16[512,128]{1,0:T(8,128)(2,1)S(1)} %get-tuple-element.33), channel_id=1, source_target_pairs={{0,3},{1,0},{2,1},{3,2},{4,7},{5,4},{6,5},{7,6},{8,11},{9,8},{10,9... | collective-permute-start | bytes 393224 | tf_op jit(solution)/shard_map/ppermute | solution.py:268
  206.4 5.6 %collective-permute-start.10 = (bf16[128,256]{1,0:T(8,128)(2,1)S(1)}, bf16[128,256]{1,0:T(8,128)(2,1)S(1)}, u32[]{:S(2)}, u32[]{:S(2)}) collective-permute-start(bf16[128,256]{1,0:T(8,128)(2,1)S(1)} %get-tuple-element.39), channel_id=1, source_target_pairs={{0,192},{4,196},{8,200},{12,204},{16,208},{20,212},{24,216},{28,22... | collective-permute-start | bytes 196616 | tf_op jit(solution)/shard_map/ppermute | solution.py:281
  207.0 6.7 %collective-permute-start.8 = (bf16[128,256]{1,0:T(8,128)(2,1)S(1)}, bf16[128,256]{1,0:T(8,128)(2,1)S(1)}, u32[]{:S(2)}, u32[]{:S(2)}) collective-permute-start(bf16[128,256]{1,0:T(8,128)(2,1)S(1)} %get-tuple-element.38), channel_id=1, source_target_pairs={{0,64},{4,68},{8,72},{12,76},{16,80},{20,84},{24,88},{28,92},{32,9... | collective-permute-start | bytes 196616 | tf_op jit(solution)/shard_map/ppermute | solution.py:281
  208.5 6.4 %collective-permute-start.9 = (bf16[128,256]{1,0:T(8,128)(2,1)S(1)}, bf16[128,256]{1,0:T(8,128)(2,1)S(1)}, u32[]{:S(2)}, u32[]{:S(2)}) collective-permute-start(bf16[128,256]{1,0:T(8,128)(2,1)S(1)} %get-tuple-element.40), channel_id=1, source_target_pairs={{0,128},{4,132},{8,136},{12,140},{16,144},{20,148},{24,152},{28,15... | collective-permute-start | bytes 196616 | tf_op jit(solution)/shard_map/ppermute | solution.py:281
  214.9 11.6 %collective-permute-start.11 = (bf16[16,256]{1,0:T(8,128)(2,1)S(1)}, bf16[16,256]{1,0:T(8,128)(2,1)S(1)}, u32[]{:S(2)}, u32[]{:S(2)}) collective-permute-start(bf16[16,256]{1,0:T(8,128)(2,1)S(1)} %get-tuple-element.41), channel_id=1, source_target_pairs={{0,8},{4,12},{8,16},{12,20},{16,24},{20,28},{24,32},{28,36},{32,40... | collective-permute-start | bytes 24584 | tf_op jit(solution)/shard_map/ppermute | solution.py:290
  216.1 12.9 %collective-permute-start.12 = (bf16[16,256]{1,0:T(8,128)(2,1)S(1)}, bf16[16,256]{1,0:T(8,128)(2,1)S(1)}, u32[]{:S(2)}, u32[]{:S(2)}) collective-permute-start(bf16[16,256]{1,0:T(8,128)(2,1)S(1)} %get-tuple-element.47), channel_id=1, source_target_pairs={{0,16},{4,20},{8,24},{12,28},{16,32},{20,36},{24,40},{28,44},{32,4... | collective-permute-start | bytes 24584 | tf_op jit(solution)/shard_map/ppermute | solution.py:290
  221.3 10.8 %collective-permute-start.13 = (bf16[16,256]{1,0:T(8,128)(2,1)S(1)}, bf16[16,256]{1,0:T(8,128)(2,1)S(1)}, u32[]{:S(2)}, u32[]{:S(2)}) collective-permute-start(bf16[16,256]{1,0:T(8,128)(2,1)S(1)} %get-tuple-element.46), channel_id=1, source_target_pairs={{0,24},{4,28},{8,32},{12,36},{16,40},{20,44},{24,48},{28,52},{32,5... | collective-permute-start | bytes 24584 | tf_op jit(solution)/shard_map/ppermute | solution.py:290
  221.5 10.6 %collective-permute-start.14 = (bf16[16,256]{1,0:T(8,128)(2,1)S(1)}, bf16[16,256]{1,0:T(8,128)(2,1)S(1)}, u32[]{:S(2)}, u32[]{:S(2)}) collective-permute-start(bf16[16,256]{1,0:T(8,128)(2,1)S(1)} %get-tuple-element.45), channel_id=1, source_target_pairs={{0,32},{4,36},{8,40},{12,44},{16,48},{20,52},{24,56},{28,60},{32,0... | collective-permute-start | bytes 24584 | tf_op jit(solution)/shard_map/ppermute | solution.py:290
  224.3 7.8 %collective-permute-start.15 = (bf16[16,256]{1,0:T(8,128)(2,1)S(1)}, bf16[16,256]{1,0:T(8,128)(2,1)S(1)}, u32[]{:S(2)}, u32[]{:S(2)}) collective-permute-start(bf16[16,256]{1,0:T(8,128)(2,1)S(1)} %get-tuple-element.44), channel_id=1, source_target_pairs={{0,40},{4,44},{8,48},{12,52},{16,56},{20,60},{24,0},{28,4},{32,8},... | collective-permute-start | bytes 24584 | tf_op jit(solution)/shard_map/ppermute | solution.py:290
  226.6 5.6 %collective-permute-start.16 = (bf16[16,256]{1,0:T(8,128)(2,1)S(1)}, bf16[16,256]{1,0:T(8,128)(2,1)S(1)}, u32[]{:S(2)}, u32[]{:S(2)}) collective-permute-start(bf16[16,256]{1,0:T(8,128)(2,1)S(1)} %get-tuple-element.43), channel_id=1, source_target_pairs={{0,48},{4,52},{8,56},{12,60},{16,0},{20,4},{24,8},{28,12},{32,16},... | collective-permute-start | bytes 24584 | tf_op jit(solution)/shard_map/ppermute | solution.py:290
  229.0 4.5 %collective-permute-start.17 = (bf16[16,256]{1,0:T(8,128)(2,1)S(1)}, bf16[16,256]{1,0:T(8,128)(2,1)S(1)}, u32[]{:S(2)}, u32[]{:S(2)}) collective-permute-start(bf16[16,256]{1,0:T(8,128)(2,1)S(1)} %get-tuple-element.42), channel_id=1, source_target_pairs={{0,56},{4,60},{8,0},{12,4},{16,8},{20,12},{24,16},{28,20},{32,24},... | collective-permute-start | bytes 24584 | tf_op jit(solution)/shard_map/ppermute | solution.py:290
  233.5 9.0 %copy-start.4 = (bf16[16,256]{1,0:T(8,128)(2,1)}, bf16[16,256]{1,0:T(8,128)(2,1)S(1)}, u32[]{:S(2)}) copy-start(bf16[16,256]{1,0:T(8,128)(2,1)S(1)} %fusion.18.refs_1_) | copy-start | bytes 24580
  233.6 5.4 %collective-permute-start.18 = (bf16[16,256]{1,0:T(8,128)(2,1)S(1)}, bf16[16,256]{1,0:T(8,128)(2,1)S(1)}, u32[]{:S(2)}, u32[]{:S(2)}) collective-permute-start(bf16[16,256]{1,0:T(8,128)(2,1)S(1)} %fusion.18.refs_1_), channel_id=1, source_target_pairs={{0,3},{1,0},{2,1},{3,2},{4,7},{5,4},{6,5},{7,6},{8,11},{9,8},{10,9... | collective-permute-start | bytes 24584 | tf_op jit(solution)/shard_map/ppermute | solution.py:295
  236.6 5.2 %collective-permute-start.19 = (bf16[16,256]{1,0:T(8,128)(2,1)S(1)}, bf16[16,256]{1,0:T(8,128)(2,1)S(1)}, u32[]{:S(2)}, u32[]{:S(2)}) collective-permute-start(bf16[16,256]{1,0:T(8,128)(2,1)S(1)} %fusion.18.refs_1_), channel_id=1, source_target_pairs={{0,2},{1,3},{2,0},{3,1},{4,6},{5,7},{6,4},{7,5},{8,10},{9,11},{10,... | collective-permute-start | bytes 24584 | tf_op jit(solution)/shard_map/ppermute | solution.py:295
  237.7 4.9 %collective-permute-start.20 = (bf16[16,256]{1,0:T(8,128)(2,1)S(1)}, bf16[16,256]{1,0:T(8,128)(2,1)S(1)}, u32[]{:S(2)}, u32[]{:S(2)}) collective-permute-start(bf16[16,256]{1,0:T(8,128)(2,1)S(1)} %fusion.18.refs_1_), channel_id=1, source_target_pairs={{0,1},{1,2},{2,3},{3,0},{4,5},{5,6},{6,7},{7,4},{8,9},{9,10},{10,1... | collective-permute-start | bytes 24584 | tf_op jit(solution)/shard_map/ppermute | solution.py:295
  238.9 3.6 %copy-start.5 = (bf16[16,256]{1,0:T(8,128)(2,1)}, bf16[16,256]{1,0:T(8,128)(2,1)S(1)}, u32[]{:S(2)}) copy-start(bf16[16,256]{1,0:T(8,128)(2,1)S(1)} %collective-permute-done.18.refs_2_) | copy-start | bytes 24580
  241.7 0.8 copy-start.6
  (1 other events, 0.6 us)

commit v2 on v1

--- a/solution.py
+++ b/solution.py
@@ -98,14 +98,19 @@
         ref[...] = nn(back_ref[...], ret_ref[:, m * UNIT : (m + 1) * UNIT]).astype(BF)
 
 
-def spread(nx, at_ref, *refs):
-    ins, out_ref = refs[:nx], refs[nx]
-    half = ins[0].shape[1] // 2
-    for s, ref in enumerate(ins):
+def finish(factor, nx, at_ref, *refs):
+    ins, out_ref = refs[:-1], refs[-1]
+    total = ins[0][...].astype(F32)
+    for ref in ins[1:]:
+        total = total + ref[...].astype(F32)
+    total = total * factor
+    half = total.shape[1] // nx // 2
+    for s in range(nx):
         source = lax.rem(at_ref[0] + s, nx)
         for m in range(2):
             cols = pl.ds(pl.multiple_of((m * nx + source) * half, half), half)
-            out_ref[:, cols] = ref[:, m * half : (m + 1) * half].astype(F32)
+            base = (2 * s + m) * half
+            out_ref[:, cols] = total[:, base : base + half]
 
 
 def cost(flops, nbytes, exps=0):
@@ -282,25 +287,22 @@
     total = pick_of(weight, iy, 0)
     for piece in came:
         total = total + piece
-    total = lax.optimization_barrier(total)
-    weight = total.reshape(nz, width // node_count, share)
-    came = []
+    low = lax.optimization_barrier(total).astype(BF)
+    pieces = [low] + [lax.ppermute(low, "rep", ring(nx, nx - s)) for s in range(1, nx)]
+    weight = lax.optimization_barrier(jnp.concatenate(pieces, axis=1))
+    weight = weight.reshape(nz, width // node_count, width)
+    shares = [pick_of(weight, iz, 0)]
     for s in range(1, nz):
-        sent = pick_of(weight, (iz + s) % nz, 0).astype(BF)
-        came.append(lax.ppermute(sent, "nodes", hop(0, s, 0)))
-    total = pick_of(weight, iz, 0)
-    for piece in came:
-        total = total + piece
-    low = (total * norm_factor).astype(BF)
-    pieces = [low] + [lax.ppermute(low, "rep", ring(nx, nx - s)) for s in range(1, nx)]
+        sent = pick_of(weight, (iz + s) % nz, 0)
+        shares.append(lax.ppermute(sent, "nodes", hop(0, s, 0)))
     grad_weight = pl.pallas_call(
-        lambda *refs: spread(nx, *refs),
+        lambda *refs: finish(norm_factor, nx, *refs),
         out_shape=sds((width // node_count, width), F32),
         in_specs=[pl.BlockSpec(memory_space=pltpu.SMEM)]
-        + [pl.BlockSpec(memory_space=pltpu.VMEM)] * nx,
+        + [pl.BlockSpec(memory_space=pltpu.VMEM)] * nz,
         cost_estimate=cost(0, 6 * width // node_count * width),
-        name="spread",
-    )(ix.reshape(1), *pieces)
+        name="finish",
+    )(ix.reshape(1), *shares)
     return (outs[0][None], outs[1][None], outs[2][None], grad_weight)
 
 

time: 254 us -> 256 us (level)
  transfers between devices with their start and end apart: 25 -> 25, of which waited for: 14 -> 15; matrix products, arithmetic and copies ran while one was open for 3% -> 4% of each run, Pallas kernels for 10% -> 10%
where the time goes in v2:
time: 256 us; the launch traced here: 253 us
  waiting for transfers between devices  132 us (52%)
  starting transfers between devices  73.4 us (29%)
  Pallas kernels  35.1 us (14%)
  local copies, waits for them, and re-layouts  4.91 us (2%)
  matrix products  3.94 us (2%)
    all_to_all x4, waiting for transfers between devices, exchange(): lax.all_to_all(rows_in.reshape(node_count, bucket, c), 'nodes', split_axi...  112 us
    all_to_all x4, starting transfers between devices, exchange(): lax.all_to_all(rows_in.reshape(node_count, bucket, c), 'nodes', split_axi...  34.9 us
    pallas_call x2, Pallas kernels, attention(): pl.pallas_call(lambda *refs: attend(scale, *refs), out_shape=(sds((rows,...  18.1 us
    ppermute x7, starting transfers between devices, local(): shares.append(lax.ppermute(sent, 'nodes', hop(0, s, 0)))  17.2 us
    ppermute x6, starting transfers between devices, reduced_over_chip_and_x(): came.append(lax.ppermute(sent, 'rep', ring(nx, s)))  11.1 us
    ppermute x6, waiting for transfers between devices, reduced_over_chip_and_x(): came.append(lax.ppermute(sent, 'rep', ring(nx, s)))  9.71 us
    ppermute x3, starting transfers between devices, local(): came.append(lax.ppermute(sent, 'nodes', hop(s, 0, 0)))  5.6 us
    pallas_call x1, Pallas kernels, local(): pl.pallas_call(lambda *refs: pack_first(rows, bucket, *refs), out_shape=(...  5.39 us
  transfers between devices with their start and end apart: 25, of which 15 were waited for; matrix products, arithmetic and copies ran while one was open for 4% of the time, Pallas kernels for 10%

profile of v2, /device:TPU:40, one launch (start us, length us, event | category | flops | bytes accessed | tf_op | source)
XLA Modules:
  0.0 252.6 jit_solution(94798970603736734)
XLA Ops:
  0.6 5.4 %pack_first.1 = (bf16[512,2688]{1,0:T(8,128)(2,1)}, bf16[512,512]{1,0:T(8,128)(2,1)}) custom-call(s32[1,512]{1,0:T(1,128)} %refs_0_.1, bf16[512,1024]{1,0:T(8,128)(2,1)} %bitcast.86, bf16[512,1024]{1,0:T(8,128)(2,1)} %bitcast.76, bf16[512,1024]{1,0:T(8,128)(2,1)} %bitcast.78, bf16[512,1024]{1,0:T(8,128)(2,1)} %bitcast.80), custom_call_target="tpu_custom_call" | custom-call | flops 1409286144 | bytes 5505024 | tf_op jit(solution)/shard_map/pack_first/pallas_call | solution.py:159
  6.0 11.8 %all-to-all-start = ((bf16[64,8,2688]{2,1,0:T(8,128)(2,1)}), bf16[64,8,2688]{2,1,0:T(8,128)(2,1)}, u32[]{:S(2)}, u32[]{:S(2)}) async-start(bf16[64,8,2688]{2,1,0:T(8,128)(2,1)} %bitcast.70), calls=%async_computation | async-start | bytes 5505024 | tf_op jit(solution)/shard_map/all_to_all | solution.py:148
  17.9 3.5 %pack_rest.1 = bf16[512,1536]{1,0:T(8,128)(2,1)} custom-call(bf16[512,512]{1,0:T(8,128)(2,1)} %get-tuple-element.18.pick_ref, bf16[512,1024]{1,0:T(8,128)(2,1)} %bitcast.77, bf16[512,1024]{1,0:T(8,128)(2,1)} %bitcast.79, bf16[512,1024]{1,0:T(8,128)(2,1)} %bitcast.81), custom_call_target="tpu_custom_call" | custom-call | flops 805306368 | bytes 3145728 | tf_op jit(solution)/shard_map/pack_rest/pallas_call | solution.py:172
  21.4 59.7 %all-to-all-done = bf16[64,8,2688]{2,1,0:T(8,128)(2,1)} async-done(((bf16[64,8,2688]{2,1,0:T(8,128)(2,1)}), bf16[64,8,2688]{2,1,0:T(8,128)(2,1)}, u32[]{:S(2)}, u32[]{:S(2)}) %all-to-all-start) | async-done | bytes 2752544 | tf_op jit(solution)/shard_map/all_to_all | solution.py:148
  81.0 7.7 %all-to-all-start.1 = ((bf16[64,8,1536]{2,1,0:T(8,128)(2,1)}), bf16[64,8,1536]{2,1,0:T(8,128)(2,1)}, u32[]{:S(2)}, u32[]{:S(2)}) async-start(bf16[64,8,1536]{2,1,0:T(8,128)(2,1)} %bitcast.65), calls=%async_computation.1 | async-start | bytes 3145728 | tf_op jit(solution)/shard_map/all_to_all | solution.py:148
  88.7 9.0 %attend.3 = (bf16[512,1536]{1,0:T(8,128)(2,1)}, bf16[512,512]{1,0:T(8,128)(2,1)}) custom-call(bf16[512,2688]{1,0:T(8,128)(2,1)} %bitcast.6.refs_0_.refs_1_.refs_3_.refs_4_.refs_5_, bf16[512,2688]{1,0:T(8,128)(2,1)} %bitcast.6.refs_0_.refs_1_.refs_3_.refs_4_.refs_5_, bf16[1024,1024]{1,0:T(8,128)(2,1)} %refs_2_.3, ...), custom_call_target="tpu_custom_call" | custom-call | flops 2147483648 | bytes 5767168 | tf_op jit(solution)/shard_map/attend/pallas_call | solution.py:189
  97.8 29.3 %all-to-all-done.1 = bf16[64,8,1536]{2,1,0:T(8,128)(2,1)} async-done(((bf16[64,8,1536]{2,1,0:T(8,128)(2,1)}), bf16[64,8,1536]{2,1,0:T(8,128)(2,1)}, u32[]{:S(2)}, u32[]{:S(2)}) %all-to-all-start.1) | async-done | bytes 1572896 | tf_op jit(solution)/shard_map/all_to_all | solution.py:148
  127.1 7.6 %all-to-all-start.3 = ((bf16[64,8,1536]{2,1,0:T(8,128)(2,1)}), bf16[64,8,1536]{2,1,0:T(8,128)(2,1)}, u32[]{:S(2)}, u32[]{:S(2)}) async-start(bf16[64,8,1536]{2,1,0:T(8,128)(2,1)} %bitcast.73), calls=%async_computation.3 | async-start | bytes 3145728 | tf_op jit(solution)/shard_map/all_to_all | solution.py:148
  134.7 2.0 fusion.2
  139.1 9.1 %attend.2 = (bf16[512,1536]{1,0:T(8,128)(2,1)}, bf16[512,512]{1,0:T(8,128)(2,1)}) custom-call(bf16[512,2688]{1,0:T(8,128)(2,1)} %bitcast.6.refs_0_.refs_1_.refs_3_.refs_4_.refs_5_, bf16[512,2688]{1,0:T(8,128)(2,1)} %bitcast.6.refs_0_.refs_1_.refs_3_.refs_4_.refs_5_, bf16[1024,1024]{1,0:T(8,128)(2,1)} %refs_2_.3, ...), custom_call_target="tpu_custom_call" | custom-call | flops 2147483648 | bytes 5767168 | tf_op jit(solution)/shard_map/attend/pallas_call | solution.py:189
  148.2 1.6 bitcast_add_fusion.1
  149.8 23.2 %all-to-all-done.3 = bf16[64,8,1536]{2,1,0:T(8,128)(2,1)} async-done(((bf16[64,8,1536]{2,1,0:T(8,128)(2,1)}), bf16[64,8,1536]{2,1,0:T(8,128)(2,1)}, u32[]{:S(2)}, u32[]{:S(2)}) %all-to-all-start.3) | async-done | bytes 1572896 | tf_op jit(solution)/shard_map/all_to_all | solution.py:148
  173.0 7.8 %all-to-all-start.2 = ((bf16[64,8,1536]{2,1,0:T(8,128)(2,1)}), bf16[64,8,1536]{2,1,0:T(8,128)(2,1)}, u32[]{:S(2)}, u32[]{:S(2)}) async-start(bf16[64,8,1536]{2,1,0:T(8,128)(2,1)} %bitcast.9), calls=%async_computation.2 | async-start | bytes 3145728 | tf_op jit(solution)/shard_map/all_to_all | solution.py:148
  180.9 1.6 collective-permute-start.1
  182.5 2.7 %collective-permute-start.2 = (bf16[512,128]{1,0:T(8,128)(2,1)S(1)}, bf16[512,128]{1,0:T(8,128)(2,1)S(1)}, u32[]{:S(2)}, u32[]{:S(2)}) collective-permute-start(bf16[512,128]{1,0:T(8,128)(2,1)S(1)} %get-tuple-element.37), channel_id=1, source_target_pairs={{0,2},{1,3},{2,0},{3,1},{4,6},{5,7},{6,4},{7,5},{8,10},{9,11},{10,... | collective-permute-start | bytes 393224 | tf_op jit(solution)/shard_map/ppermute | solution.py:273
  187.7 3.8 %collective-permute-done.2 = bf16[512,128]{1,0:T(8,128)(2,1)S(1)} collective-permute-done((bf16[512,128]{1,0:T(8,128)(2,1)S(1)}, bf16[512,128]{1,0:T(8,128)(2,1)S(1)}, u32[]{:S(2)}, u32[]{:S(2)}) %collective-permute-start.2) | collective-permute-done | bytes 131104 | tf_op jit(solution)/shard_map/ppermute | solution.py:273
  191.6 2.0 fusion
  193.8 1.9 collective-permute-done.4
  197.4 2.4 collective-permute-start.6
  201.4 1.8 collective-permute-done.5
  203.2 3.0 %collective-permute-done.6 = bf16[512,128]{1,0:T(8,128)(2,1)S(1)} collective-permute-done((bf16[512,128]{1,0:T(8,128)(2,1)S(1)}, bf16[512,128]{1,0:T(8,128)(2,1)S(1)}, u32[]{:S(2)}, u32[]{:S(2)}) %collective-permute-start.6) | collective-permute-done | bytes 131104 | tf_op jit(solution)/shard_map/ppermute | solution.py:273
  208.5 3.5 %collective-permute-start.9 = (bf16[128,256]{1,0:T(8,128)(2,1)S(1)}, bf16[128,256]{1,0:T(8,128)(2,1)S(1)}, u32[]{:S(2)}, u32[]{:S(2)}) collective-permute-start(bf16[128,256]{1,0:T(8,128)(2,1)S(1)} %get-tuple-element.40), channel_id=1, source_target_pairs={{0,128},{4,132},{8,136},{12,140},{16,144},{20,148},{24,152},{28,15... | collective-permute-start | bytes 196616 | tf_op jit(solution)/shard_map/ppermute | solution.py:286
  212.0 1.7 collective-permute-done.8
  214.9 2.8 %collective-permute-start.11 = (bf16[128,256]{1,0:T(8,128)(2,1)S(1)}, bf16[128,256]{1,0:T(8,128)(2,1)S(1)}, u32[]{:S(2)}, u32[]{:S(2)}) collective-permute-start(bf16[128,256]{1,0:T(8,128)(2,1)S(1)} %fusion.7), channel_id=1, source_target_pairs={{0,3},{1,0},{2,1},{3,2},{4,7},{5,4},{6,5},{7,6},{8,11},{9,8},{10,9... | collective-permute-start | bytes 196616 | tf_op jit(solution)/shard_map/ppermute | solution.py:291
  219.8 3.7 %collective-permute-done.12 = bf16[128,256]{1,0:T(8,128)(2,1)S(1)} collective-permute-done((bf16[128,256]{1,0:T(8,128)(2,1)S(1)}, bf16[128,256]{1,0:T(8,128)(2,1)S(1)}, u32[]{:S(2)}, u32[]{:S(2)}) %collective-permute-start.12) | collective-permute-done | bytes 65568 | tf_op jit(solution)/shard_map/ppermute | solution.py:291
  226.6 4.5 %collective-permute-start.15 = (bf16[16,1024]{1,0:T(8,128)(2,1)S(1)}, bf16[16,1024]{1,0:T(8,128)(2,1)S(1)}, u32[]{:S(2)}, u32[]{:S(2)}) collective-permute-start(bf16[16,1024]{1,0:T(8,128)(2,1)S(1)} %get-tuple-element.46), channel_id=1, source_target_pairs={{0,16},{4,20},{8,24},{12,28},{16,32},{20,36},{24,40},{28,44},{32,4... | collective-permute-start | bytes 98312 | tf_op jit(solution)/shard_map/ppermute | solution.py:297
  231.7 2.5 collective-permute-start.17
  234.2 2.5 collective-permute-start.18
  236.7 2.4 collective-permute-start.19
  239.1 3.2 %collective-permute-start.20 = (bf16[16,1024]{1,0:T(8,128)(2,1)S(1)}, bf16[16,1024]{1,0:T(8,128)(2,1)S(1)}, u32[]{:S(2)}, u32[]{:S(2)}) collective-permute-start(bf16[16,1024]{1,0:T(8,128)(2,1)S(1)} %get-tuple-element.41), channel_id=1, source_target_pairs={{0,56},{4,60},{8,0},{12,4},{16,8},{20,12},{24,16},{28,20},{32,24},... | collective-permute-start | bytes 98312 | tf_op jit(solution)/shard_map/ppermute | solution.py:297
  246.1 3.3 %unpack_a.1 = (bf16[512,1024]{1,0:T(8,128)(2,1)}, bf16[512,1024]{1,0:T(8,128)(2,1)}, bf16[512,1024]{1,0:T(8,128)(2,1)}) custom-call(bf16[512,512]{1,0:T(8,128)(2,1)} %bitcast.71, bf16[512,1536]{1,0:T(8,128)(2,1)} %bitcast.12.refs_1_), custom_call_target="tpu_custom_call" | custom-call | flops 805306368 | bytes 3145728 | tf_op jit(solution)/shard_map/unpack_a/pallas_call | solution.py:221
  249.4 3.3 %unpack_b.1 = (bf16[512,1024]{1,0:T(8,128)(2,1)}, bf16[512,1024]{1,0:T(8,128)(2,1)}, bf16[512,1024]{1,0:T(8,128)(2,1)}) custom-call(bf16[512,512]{1,0:T(8,128)(2,1)} %bitcast.72, bf16[512,1536]{1,0:T(8,128)(2,1)} %bitcast.10.refs_1_, bf16[512,1024]{1,0:T(8,128)(2,1)} %get-tuple-element.22.refs_2_, ...), custom_call_target="tpu_custom_call", output_to_operand_aliasing={{0}: (2, {}), {1}: (3, {}), {2}: (4, {})} | custom-call | flops 805306368 | bytes 3145728 | tf_op jit(solution)/shard_map/unpack_b/pallas_call | solution.py:231
  (63 shorter events, 21.6 us)
Async XLA Ops:
  6.0 75.0 %all-to-all-start = ((bf16[64,8,2688]{2,1,0:T(8,128)(2,1)}), bf16[64,8,2688]{2,1,0:T(8,128)(2,1)}, u32[]{:S(2)}, u32[]{:S(2)}) async-start(bf16[64,8,2688]{2,1,0:T(8,128)(2,1)} %bitcast.70), calls=%async_computation | async-start | bytes 5505024 | tf_op jit(solution)/shard_map/all_to_all | solution.py:148
  81.0 46.0 %all-to-all-start.1 = ((bf16[64,8,1536]{2,1,0:T(8,128)(2,1)}), bf16[64,8,1536]{2,1,0:T(8,128)(2,1)}, u32[]{:S(2)}, u32[]{:S(2)}) async-start(bf16[64,8,1536]{2,1,0:T(8,128)(2,1)} %bitcast.65), calls=%async_computation.1 | async-start | bytes 3145728 | tf_op jit(solution)/shard_map/all_to_all | solution.py:148
  97.8 37.0 %copy-start.2 = (bf16[512,512]{1,0:T(8,128)(2,1)S(1)}, bf16[512,512]{1,0:T(8,128)(2,1)}, u32[]{:S(2)}) copy-start(bf16[512,512]{1,0:T(8,128)(2,1)} %get-tuple-element.29) | copy-start | bytes 1572868
  127.1 46.0 %all-to-all-start.3 = ((bf16[64,8,1536]{2,1,0:T(8,128)(2,1)}), bf16[64,8,1536]{2,1,0:T(8,128)(2,1)}, u32[]{:S(2)}, u32[]{:S(2)}) async-start(bf16[64,8,1536]{2,1,0:T(8,128)(2,1)} %bitcast.73), calls=%async_computation.3 | async-start | bytes 3145728 | tf_op jit(solution)/shard_map/all_to_all | solution.py:148
  136.7 1.4 copy-start
  139.0 9.2 %collective-permute-start = (bf16[32,16,512]{2,1,0:T(8,128)(2,1)}, bf16[32,16,512]{2,1,0:T(8,128)(2,1)}, u32[]{:S(2)}, u32[]{:S(2)}) collective-permute-start(bf16[32,16,512]{2,1,0:T(8,128)(2,1)} %fusion.4), channel_id=1, source_target_pairs={{0,4},{4,0},{8,12},{12,8},{16,20},{20,16},{24,28},{28,24},{32,36},... | collective-permute-start | bytes 1572872 | tf_op jit(solution)/shard_map/ppermute | solution.py:268
  173.0 18.6 %copy-start.3 = (bf16[512,512]{1,0:T(8,128)(2,1)S(1)}, bf16[512,512]{1,0:T(8,128)(2,1)}, u32[]{:S(2)}) copy-start(bf16[512,512]{1,0:T(8,128)(2,1)} %get-tuple-element.31) | copy-start | bytes 1572868
  173.0 76.3 %all-to-all-start.2 = ((bf16[64,8,1536]{2,1,0:T(8,128)(2,1)}), bf16[64,8,1536]{2,1,0:T(8,128)(2,1)}, u32[]{:S(2)}, u32[]{:S(2)}) async-start(bf16[64,8,1536]{2,1,0:T(8,128)(2,1)} %bitcast.9), calls=%async_computation.2 | async-start | bytes 3145728 | tf_op jit(solution)/shard_map/all_to_all | solution.py:148
  180.9 6.8 %collective-permute-start.1 = (bf16[512,128]{1,0:T(8,128)(2,1)S(1)}, bf16[512,128]{1,0:T(8,128)(2,1)S(1)}, u32[]{:S(2)}, u32[]{:S(2)}) collective-permute-start(bf16[512,128]{1,0:T(8,128)(2,1)S(1)} %get-tuple-element.35), channel_id=1, source_target_pairs={{0,1},{1,2},{2,3},{3,0},{4,5},{5,6},{6,7},{7,4},{8,9},{9,10},{10,1... | collective-permute-start | bytes 393224 | tf_op jit(solution)/shard_map/ppermute | solution.py:273
  182.5 9.0 %collective-permute-start.2 = (bf16[512,128]{1,0:T(8,128)(2,1)S(1)}, bf16[512,128]{1,0:T(8,128)(2,1)S(1)}, u32[]{:S(2)}, u32[]{:S(2)}) collective-permute-start(bf16[512,128]{1,0:T(8,128)(2,1)S(1)} %get-tuple-element.37), channel_id=1, source_target_pairs={{0,2},{1,3},{2,0},{3,1},{4,6},{5,7},{6,4},{7,5},{8,10},{9,11},{10,... | collective-permute-start | bytes 393224 | tf_op jit(solution)/shard_map/ppermute | solution.py:273
  185.2 6.3 %collective-permute-start.3 = (bf16[512,128]{1,0:T(8,128)(2,1)S(1)}, bf16[512,128]{1,0:T(8,128)(2,1)S(1)}, u32[]{:S(2)}, u32[]{:S(2)}) collective-permute-start(bf16[512,128]{1,0:T(8,128)(2,1)S(1)} %get-tuple-element.36), channel_id=1, source_target_pairs={{0,3},{1,0},{2,1},{3,2},{4,7},{5,4},{6,5},{7,6},{8,11},{9,8},{10,9... | collective-permute-start | bytes 393224 | tf_op jit(solution)/shard_map/ppermute | solution.py:273
  193.7 2.0 collective-permute-start.4
  196.0 7.2 %collective-permute-start.5 = (bf16[512,128]{1,0:T(8,128)(2,1)S(1)}, bf16[512,128]{1,0:T(8,128)(2,1)S(1)}, u32[]{:S(2)}, u32[]{:S(2)}) collective-permute-start(bf16[512,128]{1,0:T(8,128)(2,1)S(1)} %get-tuple-element.32), channel_id=1, source_target_pairs={{0,1},{1,2},{2,3},{3,0},{4,5},{5,6},{6,7},{7,4},{8,9},{9,10},{10,1... | collective-permute-start | bytes 393224 | tf_op jit(solution)/shard_map/ppermute | solution.py:273
  197.4 8.7 %collective-permute-start.6 = (bf16[512,128]{1,0:T(8,128)(2,1)S(1)}, bf16[512,128]{1,0:T(8,128)(2,1)S(1)}, u32[]{:S(2)}, u32[]{:S(2)}) collective-permute-start(bf16[512,128]{1,0:T(8,128)(2,1)S(1)} %get-tuple-element.34), channel_id=1, source_target_pairs={{0,2},{1,3},{2,0},{3,1},{4,6},{5,7},{6,4},{7,5},{8,10},{9,11},{10,... | collective-permute-start | bytes 393224 | tf_op jit(solution)/shard_map/ppermute | solution.py:273
  199.8 42.5 %copy-start.1 = (bf16[512,512]{1,0:T(8,128)(2,1)S(1)}, bf16[512,512]{1,0:T(8,128)(2,1)}, u32[]{:S(2)}) copy-start(bf16[512,512]{1,0:T(8,128)(2,1)} %get-tuple-element.18.pick_ref) | copy-start | bytes 1572868
  199.8 6.4 %collective-permute-start.7 = (bf16[512,128]{1,0:T(8,128)(2,1)S(1)}, bf16[512,128]{1,0:T(8,128)(2,1)S(1)}, u32[]{:S(2)}, u32[]{:S(2)}) collective-permute-start(bf16[512,128]{1,0:T(8,128)(2,1)S(1)} %get-tuple-element.33), channel_id=1, source_target_pairs={{0,3},{1,0},{2,1},{3,2},{4,7},{5,4},{6,5},{7,6},{8,11},{9,8},{10,9... | collective-permute-start | bytes 393224 | tf_op jit(solution)/shard_map/ppermute | solution.py:273
  206.4 5.6 %collective-permute-start.10 = (bf16[128,256]{1,0:T(8,128)(2,1)S(1)}, bf16[128,256]{1,0:T(8,128)(2,1)S(1)}, u32[]{:S(2)}, u32[]{:S(2)}) collective-permute-start(bf16[128,256]{1,0:T(8,128)(2,1)S(1)} %get-tuple-element.39), channel_id=1, source_target_pairs={{0,192},{4,196},{8,200},{12,204},{16,208},{20,212},{24,216},{28,22... | collective-permute-start | bytes 196616 | tf_op jit(solution)/shard_map/ppermute | solution.py:286
  207.0 6.7 %collective-permute-start.8 = (bf16[128,256]{1,0:T(8,128)(2,1)S(1)}, bf16[128,256]{1,0:T(8,128)(2,1)S(1)}, u32[]{:S(2)}, u32[]{:S(2)}) collective-permute-start(bf16[128,256]{1,0:T(8,128)(2,1)S(1)} %get-tuple-element.38), channel_id=1, source_target_pairs={{0,64},{4,68},{8,72},{12,76},{16,80},{20,84},{24,88},{28,92},{32,9... | collective-permute-start | bytes 196616 | tf_op jit(solution)/shard_map/ppermute | solution.py:286
  208.5 6.4 %collective-permute-start.9 = (bf16[128,256]{1,0:T(8,128)(2,1)S(1)}, bf16[128,256]{1,0:T(8,128)(2,1)S(1)}, u32[]{:S(2)}, u32[]{:S(2)}) collective-permute-start(bf16[128,256]{1,0:T(8,128)(2,1)S(1)} %get-tuple-element.40), channel_id=1, source_target_pairs={{0,128},{4,132},{8,136},{12,140},{16,144},{20,148},{24,152},{28,15... | collective-permute-start | bytes 196616 | tf_op jit(solution)/shard_map/ppermute | solution.py:286
  214.9 4.9 %collective-permute-start.11 = (bf16[128,256]{1,0:T(8,128)(2,1)S(1)}, bf16[128,256]{1,0:T(8,128)(2,1)S(1)}, u32[]{:S(2)}, u32[]{:S(2)}) collective-permute-start(bf16[128,256]{1,0:T(8,128)(2,1)S(1)} %fusion.7), channel_id=1, source_target_pairs={{0,3},{1,0},{2,1},{3,2},{4,7},{5,4},{6,5},{7,6},{8,11},{9,8},{10,9... | collective-permute-start | bytes 196616 | tf_op jit(solution)/shard_map/ppermute | solution.py:291
  217.7 5.8 %collective-permute-start.12 = (bf16[128,256]{1,0:T(8,128)(2,1)S(1)}, bf16[128,256]{1,0:T(8,128)(2,1)S(1)}, u32[]{:S(2)}, u32[]{:S(2)}) collective-permute-start(bf16[128,256]{1,0:T(8,128)(2,1)S(1)} %fusion.7), channel_id=1, source_target_pairs={{0,2},{1,3},{2,0},{3,1},{4,6},{5,7},{6,4},{7,5},{8,10},{9,11},{10,... | collective-permute-start | bytes 196616 | tf_op jit(solution)/shard_map/ppermute | solution.py:291
  218.9 5.5 %collective-permute-start.13 = (bf16[128,256]{1,0:T(8,128)(2,1)S(1)}, bf16[128,256]{1,0:T(8,128)(2,1)S(1)}, u32[]{:S(2)}, u32[]{:S(2)}) collective-permute-start(bf16[128,256]{1,0:T(8,128)(2,1)S(1)} %fusion.7), channel_id=1, source_target_pairs={{0,1},{1,2},{2,3},{3,0},{4,5},{5,6},{6,7},{7,4},{8,9},{9,10},{10,1... | collective-permute-start | bytes 196616 | tf_op jit(solution)/shard_map/ppermute | solution.py:291
  225.1 11.7 %collective-permute-start.14 = (bf16[16,1024]{1,0:T(8,128)(2,1)S(1)}, bf16[16,1024]{1,0:T(8,128)(2,1)S(1)}, u32[]{:S(2)}, u32[]{:S(2)}) collective-permute-start(bf16[16,1024]{1,0:T(8,128)(2,1)S(1)} %get-tuple-element.47), channel_id=1, source_target_pairs={{0,8},{4,12},{8,16},{12,20},{16,24},{20,28},{24,32},{28,36},{32,40... | collective-permute-start | bytes 98312 | tf_op jit(solution)/shard_map/ppermute | solution.py:297
  226.6 12.5 %collective-permute-start.15 = (bf16[16,1024]{1,0:T(8,128)(2,1)S(1)}, bf16[16,1024]{1,0:T(8,128)(2,1)S(1)}, u32[]{:S(2)}, u32[]{:S(2)}) collective-permute-start(bf16[16,1024]{1,0:T(8,128)(2,1)S(1)} %get-tuple-element.46), channel_id=1, source_target_pairs={{0,16},{4,20},{8,24},{12,28},{16,32},{20,36},{24,40},{28,44},{32,4... | collective-permute-start | bytes 98312 | tf_op jit(solution)/shard_map/ppermute | solution.py:297
  231.1 12.2 %collective-permute-start.16 = (bf16[16,1024]{1,0:T(8,128)(2,1)S(1)}, bf16[16,1024]{1,0:T(8,128)(2,1)S(1)}, u32[]{:S(2)}, u32[]{:S(2)}) collective-permute-start(bf16[16,1024]{1,0:T(8,128)(2,1)S(1)} %get-tuple-element.45), channel_id=1, source_target_pairs={{0,24},{4,28},{8,32},{12,36},{16,40},{20,44},{24,48},{28,52},{32,5... | collective-permute-start | bytes 98312 | tf_op jit(solution)/shard_map/ppermute | solution.py:297
  231.7 11.7 %collective-permute-start.17 = (bf16[16,1024]{1,0:T(8,128)(2,1)S(1)}, bf16[16,1024]{1,0:T(8,128)(2,1)S(1)}, u32[]{:S(2)}, u32[]{:S(2)}) collective-permute-start(bf16[16,1024]{1,0:T(8,128)(2,1)S(1)} %get-tuple-element.44), channel_id=1, source_target_pairs={{0,32},{4,36},{8,40},{12,44},{16,48},{20,52},{24,56},{28,60},{32,0... | collective-permute-start | bytes 98312 | tf_op jit(solution)/shard_map/ppermute | solution.py:297
  234.2 9.2 %collective-permute-start.18 = (bf16[16,1024]{1,0:T(8,128)(2,1)S(1)}, bf16[16,1024]{1,0:T(8,128)(2,1)S(1)}, u32[]{:S(2)}, u32[]{:S(2)}) collective-permute-start(bf16[16,1024]{1,0:T(8,128)(2,1)S(1)} %get-tuple-element.43), channel_id=1, source_target_pairs={{0,40},{4,44},{8,48},{12,52},{16,56},{20,60},{24,0},{28,4},{32,8},... | collective-permute-start | bytes 98312 | tf_op jit(solution)/shard_map/ppermute | solution.py:297
  236.7 7.2 %copy-start.4 = (bf16[16,1024]{1,0:T(8,128)(2,1)}, bf16[16,1024]{1,0:T(8,128)(2,1)S(1)}, u32[]{:S(2)}) copy-start(bf16[16,1024]{1,0:T(8,128)(2,1)S(1)} %collective-permute-done.14.refs_2_) | copy-start | bytes 98308
  236.7 6.7 %collective-permute-start.19 = (bf16[16,1024]{1,0:T(8,128)(2,1)S(1)}, bf16[16,1024]{1,0:T(8,128)(2,1)S(1)}, u32[]{:S(2)}, u32[]{:S(2)}) collective-permute-start(bf16[16,1024]{1,0:T(8,128)(2,1)S(1)} %get-tuple-element.42), channel_id=1, source_target_pairs={{0,48},{4,52},{8,56},{12,60},{16,0},{20,4},{24,8},{28,12},{32,16},... | collective-permute-start | bytes 98312 | tf_op jit(solution)/shard_map/ppermute | solution.py:297
  239.1 4.8 %copy-start.5 = (bf16[16,1024]{1,0:T(8,128)(2,1)}, bf16[16,1024]{1,0:T(8,128)(2,1)S(1)}, u32[]{:S(2)}) copy-start(bf16[16,1024]{1,0:T(8,128)(2,1)S(1)} %collective-permute-done.15.refs_3_) | copy-start | bytes 98308
  239.1 4.8 %collective-permute-start.20 = (bf16[16,1024]{1,0:T(8,128)(2,1)S(1)}, bf16[16,1024]{1,0:T(8,128)(2,1)S(1)}, u32[]{:S(2)}, u32[]{:S(2)}) collective-permute-start(bf16[16,1024]{1,0:T(8,128)(2,1)S(1)} %get-tuple-element.41), channel_id=1, source_target_pairs={{0,56},{4,60},{8,0},{12,4},{16,8},{20,12},{24,16},{28,20},{32,24},... | collective-permute-start | bytes 98312 | tf_op jit(solution)/shard_map/ppermute | solution.py:297
  243.4 0.6 copy-start.6
  (4 other events, 2.5 us)

commit v3 on v2

--- a/solution.py
+++ b/solution.py
@@ -13,6 +13,7 @@
 UNIT = 256
 UNITS_A = 2
 LANES = 128
+TAG_ROWS = 16
 big_negative = -1e30
 BF = jnp.bfloat16
 F32 = jnp.float32
@@ -38,28 +39,71 @@
     return jnp.transpose(jnp.broadcast_to(row, (LANES, rows)))[:, :1]
 
 
-def pack_first(rows, bucket, ids_ref, g_ref, q_ref, k_ref, v_ref, out_ref, pick_ref):
+def pack_first(rows, bucket, ids_ref, g_ref, q_ref, k_ref, v_ref, out_ref, pick_ref, tag_ref):
     ids_row = ids_ref[...].astype(F32)
     owner_row = jnp.floor(ids_row * (1.0 / CL_DEV))
     ids_col = column_of(ids_row, rows)
     owner_col = jnp.floor(ids_col * (1.0 / CL_DEV))
-    tag_col = ids_col - owner_col * CL_DEV + 1.0
-    down = lax.broadcasted_iota(jnp.int32, (rows, rows), 0)
-    across = lax.broadcasted_iota(jnp.int32, (rows, rows), 1)
-    same = (owner_col == owner_row) & (down < across)
-    rank = jnp.sum(jnp.where(same, 1.0, 0.0), axis=0, keepdims=True)
-    slot = (owner_row * bucket + rank).astype(jnp.int32)
-    pick = jnp.where(down == slot, 1.0, 0.0).astype(BF)
-    pick_ref[...] = pick
+    tag_row = ids_row - owner_row * CL_DEV + 1.0
+    down = lax.broadcasted_iota(jnp.int32, (rows, LANES), 0)
+    across = lax.broadcasted_iota(jnp.int32, (rows, LANES), 1)
+
+    @pl.loop(0, rows // LANES)
+    def _(j):
+        cols = pl.ds(pl.multiple_of(j * LANES, LANES), LANES)
+        owner = jnp.floor(ids_ref[:, cols].astype(F32) * (1.0 / CL_DEV))
+        same = (owner_col == owner) & (down < across + j * LANES)
+        rank = jnp.sum(jnp.where(same, 1.0, 0.0), axis=0, keepdims=True)
+        slot = (owner * bucket + rank).astype(jnp.int32)
+        pick_ref[:, cols] = jnp.where(down == slot, 1.0, 0.0).astype(BF)
+
     width = g_ref.shape[1]
-    out_ref[:, :width] = nn(pick, g_ref[...]).astype(BF)
-    for u in range(q_ref.shape[1] // UNIT):
+
+    def unit(n):
+        return pl.ds(pl.multiple_of(n * UNIT, UNIT), UNIT)
+
+    @pl.loop(0, width // UNIT)
+    def _(u):
+        out_ref[:, unit(u)] = nn(pick_ref[...], g_ref[:, unit(u)]).astype(BF)
+
+    @pl.loop(0, q_ref.shape[1] // UNIT)
+    def _(u):
         for m, ref in enumerate((q_ref, k_ref, v_ref)):
-            base = width + (3 * u + m) * UNIT
-            out_ref[:, base : base + UNIT] = nn(pick, ref[:, u * UNIT : (u + 1) * UNIT]).astype(BF)
-    base = out_ref.shape[1] - LANES
-    tags = jnp.broadcast_to(tag_col, (rows, LANES)).astype(BF)
-    out_ref[:, base:] = nn(pick, tags).astype(BF)
+            base = width // UNIT + 3 * u + m
+            out_ref[:, unit(base)] = nn(pick_ref[...], ref[:, unit(u)]).astype(BF)
+
+    tags = jnp.broadcast_to(tag_row, (TAG_ROWS, rows)).astype(BF)
+    tag_ref[...] = nt(tags, pick_ref[...])[:1].astype(BF)
+
+
+def tag_order(sizes, bucket, at_ref, *refs):
+    ny, nz, nc = sizes
+    nodes = ny * nz * nc
+    ins, out_ref = refs[:-1], refs[-1]
+    iy, iz, ic = at_ref[0], at_ref[1], at_ref[2]
+    table = jnp.concatenate([ref[...].astype(F32) for ref in ins], axis=0)
+    rows = table.shape[1]
+    lane = lax.broadcasted_iota(jnp.int32, (rows, LANES), 0)
+    k = lax.broadcasted_iota(jnp.int32, (rows, LANES), 1)
+    me = (iy * nz + iz) * nc + ic
+    mine = jnp.where((lane == me * bucket + k) & (k < bucket), 1.0, 0.0).astype(BF)
+    table = nn(table.astype(BF), mine)
+    n = lax.broadcasted_iota(jnp.int32, (nodes, nodes), 0)
+    at = lax.broadcasted_iota(jnp.int32, (nodes, nodes), 1)
+    bits_c, bits_z = nc.bit_length() - 1, nz.bit_length() - 1
+    dc = (ic - n) & (nc - 1)
+    dz = (iz - (n >> bits_c)) & (nz - 1)
+    dy = (iy - (n >> (bits_c + bits_z))) & (ny - 1)
+    turn = jnp.where(at == (dz * ny + dy) * nc + dc, 1.0, 0.0).astype(BF)
+    table = nn(turn, table.astype(BF)).astype(BF)
+    n = lax.broadcasted_iota(jnp.int32, (nodes, rows), 0)
+    slot = lax.broadcasted_iota(jnp.int32, (nodes, rows), 1)
+    bits_k = bucket.bit_length() - 1
+    spread = tn(table, jnp.where((slot >> bits_k) == n, 1.0, 0.0).astype(BF))
+    k = lax.broadcasted_iota(jnp.int32, spread.shape, 0)
+    slot = lax.broadcasted_iota(jnp.int32, spread.shape, 1)
+    kept = jnp.where((slot & (bucket - 1)) == k, spread, 0.0)
+    out_ref[...] = jnp.sum(kept, axis=0, keepdims=True)
 
 
 def pack_rest(pick_ref, q_ref, k_ref, v_ref, out_ref):
@@ -69,33 +113,39 @@
 
 
 def attend(scale, g_ref, tag_ref, w_ref, q_ref, k_ref, v_ref, ret_ref, att_ref, bias_ref):
+    rows = g_ref.shape[0]
+
     @pl.when(pl.program_id(0) == 0)
     def _():
-        tags = tag_ref[...].astype(F32)
-        same = tags[:, :1] == jnp.transpose(tags)[:1, :]
-        bias_ref[...] = jnp.where(same, 0.0, big_negative)
-
-    grad_all = nn(g_ref[...], w_ref[...]).astype(BF)
-    for h in range(UNIT // HEAD_DIM):
-        cols = slice(h * HEAD_DIM, (h + 1) * HEAD_DIM)
-        q, k, v, grad = q_ref[:, cols], k_ref[:, cols], v_ref[:, cols], grad_all[:, cols]
-        scores = nt(q, k) * scale + bias_ref[...]
-        weights = jnp.exp(scores - jnp.max(scores, axis=1, keepdims=True))
-        probs = weights * (1.0 / jnp.sum(weights, axis=1, keepdims=True))
-        low = probs.astype(BF)
-        attended = nn(low, v).astype(BF)
-        delta = jnp.sum(grad.astype(F32) * attended.astype(F32), axis=1, keepdims=True)
-        grad_scores = (probs * (nt(grad, v) - delta) * scale).astype(BF)
-        att_ref[:, cols] = attended
-        for m, part in enumerate((nn(grad_scores, k), tn(grad_scores, q), tn(low, grad))):
-            base = m * UNIT + h * HEAD_DIM
-            ret_ref[:, base : base + HEAD_DIM] = part.astype(BF)
+        tags = column_of(tag_ref[...], rows)
+
+        @pl.loop(0, rows // LANES)
+        def _(j):
+            cols = pl.ds(pl.multiple_of(j * LANES, LANES), LANES)
+            bias_ref[:, cols] = jnp.where(tags == tag_ref[:, cols], 0.0, big_negative)
+
+    q, k, v = q_ref[...], k_ref[...], v_ref[...]
+    grad = nn(g_ref[...], w_ref[...]).astype(BF)
+    scores = nt(q, k) * scale + bias_ref[...]
+    weights = jnp.exp(scores - jnp.max(scores, axis=1, keepdims=True))
+    probs = weights * (1.0 / jnp.sum(weights, axis=1, keepdims=True))
+    low = probs.astype(BF)
+    attended = nn(low, v).astype(BF)
+    delta = jnp.sum(grad.astype(F32) * attended.astype(F32), axis=1, keepdims=True)
+    grad_scores = (probs * (nt(grad, v) - delta) * scale).astype(BF)
+    att_ref[...] = attended
+    for m, part in enumerate((nn(grad_scores, k), tn(grad_scores, q), tn(low, grad))):
+        ret_ref[:, m * HEAD_DIM : (m + 1) * HEAD_DIM] = part.astype(BF)
 
 
 def unpack(held, back_ref, ret_ref, *refs):
     outs = refs[held:]
-    for m, ref in enumerate(outs):
-        ref[...] = nn(back_ref[...], ret_ref[:, m * UNIT : (m + 1) * UNIT]).astype(BF)
+    rows_out = nn(back_ref[...], ret_ref[...]).astype(BF)
+    for h in range(UNIT // HEAD_DIM):
+        for m, ref in enumerate(outs):
+            cols = slice(h * HEAD_DIM, (h + 1) * HEAD_DIM)
+            base = (h * len(outs) + m) * HEAD_DIM
+            ref[:, cols] = rows_out[:, base : base + HEAD_DIM]
 
 
 def finish(factor, nx, at_ref, *refs):
@@ -154,19 +204,52 @@
         )
         return out.reshape(rows, c)
 
-    wide_a = width + 3 * UNIT * ua + LANES
+    wide_a = width + 3 * UNIT * ua
     part_a = pl.BlockSpec((rows, UNIT * ua), lambda i: (0, 0))
-    send_a, pick = pl.pallas_call(
+    send_a, pick, tags = pl.pallas_call(
         lambda *refs: pack_first(rows, bucket, *refs),
-        out_shape=(sds((rows, wide_a)), sds((rows, rows))),
+        out_shape=(sds((rows, wide_a)), sds((rows, rows)), sds((1, rows))),
         grid=(1,),
         in_specs=[full((1, rows)), full((rows, width)), part_a, part_a, part_a],
-        out_specs=(full((rows, wide_a)), full((rows, rows))),
+        out_specs=(full((rows, wide_a)), full((rows, rows)), full((1, rows))),
         compiler_params=params(),
         cost_estimate=cost(2 * rows * rows * wide_a, 4 * rows * wide_a),
         name="pack_first",
     )(cluster_id, g, q, k, v)
     recv_a = exchange(send_a)
+
+    node = lax.axis_index("nodes")
+    ix = lax.axis_index("rep")
+    iy, iz, ic = node // (nz * nc), (node // nc) % nz, node % nc
+
+    def nid(y, z, c):
+        return ((y % ny) * nz + z % nz) * nc + c % nc
+
+    everyone = [(y, z, c) for y in range(ny) for z in range(nz) for c in range(nc)]
+
+    def hop(dy, dz, dc):
+        return [(nid(y, z, c), nid(y + dy, z + dz, c + dc)) for y, z, c in everyone]
+
+    def pick_of(array, index, axis):
+        return lax.dynamic_index_in_dim(array, index, axis, keepdims=False)
+
+    def around(line, count, step):
+        return [line] + [lax.ppermute(line, "nodes", hop(*step(s))) for s in range(1, count)]
+
+    line = jnp.concatenate(around(tags, nc, lambda s: (0, 0, s)), axis=0)
+    step = 1
+    while step < ny:
+        line = jnp.concatenate([line, lax.ppermute(line, "nodes", hop(step, 0, 0))], axis=0)
+        step *= 2
+    lines = around(line, nz, lambda s: (0, s, 0))
+    tag_line = pl.pallas_call(
+        lambda *refs: tag_order((ny, nz, nc), bucket, *refs),
+        out_shape=sds((1, rows), F32),
+        in_specs=[pl.BlockSpec(memory_space=pltpu.SMEM)]
+        + [pl.BlockSpec(memory_space=pltpu.VMEM)] * nz,
+        cost_estimate=cost(2 * rows * rows * LANES, 4 * rows * rows),
+        name="tag_order",
+    )(jnp.stack([iy, iz, ic]), *lines)
 
     part_b = pl.BlockSpec((rows, UNIT), lambda i: (0, i + ua))
     send_b = pl.pallas_call(
@@ -183,24 +266,28 @@
     back = jnp.transpose(pick)
 
     def attention(recv, first, unit0, n_units):
+        per = UNIT // HEAD_DIM
+
         def col(m):
-            return pl.BlockSpec((rows, UNIT), lambda i: (0, first + 3 * i + m))
+            return pl.BlockSpec(
+                (rows, HEAD_DIM), lambda i: (0, per * (first + 3 * (i // per) + m) + i % per)
+            )
 
         return pl.pallas_call(
             lambda *refs: attend(scale, *refs),
             out_shape=(sds((rows, 3 * UNIT * n_units)), sds((rows, UNIT * n_units))),
-            grid=(n_units,),
+            grid=(n_units * per,),
             in_specs=[
                 full((rows, width)),
-                pl.BlockSpec((rows, LANES), lambda i: (0, wide_a // LANES - 1)),
-                pl.BlockSpec((width, UNIT), lambda i: (0, i + unit0)),
+                full((1, rows)),
+                pl.BlockSpec((width, HEAD_DIM), lambda i: (0, i + unit0 * per)),
                 col(0),
                 col(1),
                 col(2),
             ],
             out_specs=(
-                pl.BlockSpec((rows, 3 * UNIT), lambda i: (0, i)),
-                pl.BlockSpec((rows, UNIT), lambda i: (0, i)),
+                pl.BlockSpec((rows, 3 * HEAD_DIM), lambda i: (0, i)),
+                pl.BlockSpec((rows, HEAD_DIM), lambda i: (0, i)),
             ),
             scratch_shapes=[pltpu.VMEM((rows, rows), F32)],
             compiler_params=params(),
@@ -210,7 +297,7 @@
                 rows * rows * n_units * UNIT // HEAD_DIM,
             ),
             name="attend",
-        )(recv_a, recv_a, w_out, recv, recv, recv)
+        )(recv_a, tag_line, w_out, recv, recv, recv)
 
     ret_a, att_a = attention(recv_a, width // UNIT, 0, ua)
     home_a = exchange(ret_a)
@@ -240,21 +327,6 @@
         cost_estimate=cost(2 * rows * rows * 3 * UNIT * ub, 4 * rows * 3 * UNIT * ub),
         name="unpack_b",
     )(back, home_b, *outs)
-
-    node = lax.axis_index("nodes")
-    ix = lax.axis_index("rep")
-    iy, iz, ic = node // (nz * nc), (node // nc) % nz, node % nc
-
-    def nid(y, z, c):
-        return ((y % ny) * nz + z % nz) * nc + c % nc
-
-    everyone = [(y, z, c) for y in range(ny) for z in range(nz) for c in range(nc)]
-
-    def hop(dy, dz, dc):
-        return [(nid(y, z, c), nid(y + dy, z + dz, c + dc)) for y, z, c in everyone]
-
-    def pick_of(array, index, axis):
-        return lax.dynamic_index_in_dim(array, index, axis, keepdims=False)
 
     share = width // nx
 

time: 256 us -> 273 us (1.066)
  starting transfers between devices: 73.4 us -> 93.7 us
  waiting for transfers between devices: 132 us -> 123 us
  Pallas kernels: 35.1 us -> 40.9 us
    all_to_all x4, waiting for transfers between devices: 112 us -> 79.2 us  [exchange(): lax.all_to_all(rows_in.reshape(node_count, bucket, c), 'nodes', split_axi...]
    ppermute x0 -> x10, waiting for transfers between devices: none -> 21.5 us  [the longest x8 16.5 us: around(): lax.ppermute(line, 'nodes', hop(*step(s)))]
    ppermute x0 -> x10, starting transfers between devices: none -> 20.3 us  [the longest x8 16.4 us: around(): lax.ppermute(line, 'nodes', hop(*step(s)))]
  transfers between devices with their start and end apart: 25 -> 35, of which waited for: 15 -> 19; matrix products, arithmetic and copies ran while one was open for 4% -> 3% of each run, Pallas kernels for 10% -> 11%
where the time goes in v3:
time: 273 us; the launch traced here: 270 us
  waiting for transfers between devices  123 us (45%)
  starting transfers between devices  93.7 us (34%)
  Pallas kernels  40.9 us (15%)
  local copies, waits for them, and re-layouts  5.42 us (2%)
  matrix products  3.94 us (1%)
    all_to_all x4, waiting for transfers between devices, exchange(): lax.all_to_all(rows_in.reshape(node_count, bucket, c), 'nodes', split_axi...  79.2 us
    all_to_all x4, starting transfers between devices, exchange(): lax.all_to_all(rows_in.reshape(node_count, bucket, c), 'nodes', split_axi...  36.3 us
    pallas_call x2, Pallas kernels, attention(): pl.pallas_call(lambda *refs: attend(scale, *refs), out_shape=(sds((rows,...  20.4 us
    ppermute x8, waiting for transfers between devices, around(): lax.ppermute(line, 'nodes', hop(*step(s)))  16.5 us
    ppermute x7, starting transfers between devices, local(): shares.append(lax.ppermute(sent, 'nodes', hop(0, s, 0)))  16.4 us
    ppermute x8, starting transfers between devices, around(): lax.ppermute(line, 'nodes', hop(*step(s)))  16.4 us
    ppermute x6, starting transfers between devices, reduced_over_chip_and_x(): came.append(lax.ppermute(sent, 'rep', ring(nx, s)))  11.1 us
    ppermute x6, waiting for transfers between devices, reduced_over_chip_and_x(): came.append(lax.ppermute(sent, 'rep', ring(nx, s)))  9.7 us
  transfers between devices with their start and end apart: 35, of which 19 were waited for; matrix products, arithmetic and copies ran while one was open for 3% of the time, Pallas kernels for 11%

profile of v3, /device:TPU:40, one launch (start us, length us, event | category | flops | bytes accessed | tf_op | source)
XLA Modules:
  0.0 270.1 jit_solution(2280014719886172318)
XLA Ops:
  0.6 6.6 %pack_first.1 = (bf16[512,2560]{1,0:T(8,128)(2,1)}, bf16[512,512]{1,0:T(8,128)(2,1)}, bf16[1,512]{1,0:T(2,128)(2,1)}) custom-call(s32[1,512]{1,0:T(1,128)} %refs_0_.1, bf16[512,1024]{1,0:T(8,128)(2,1)} %bitcast.89, bf16[512,1024]{1,0:T(8,128)(2,1)} %bitcast.79, bf16[512,1024]{1,0:T(8,128)(2,1)} %bitcast.81, bf16[512,1024]{1,0:T(8,128)(2,1)} %bitcast.83), custom_call_target="tpu_custom_call" | custom-call | flops 1342177280 | bytes 5242880 | tf_op jit(solution)/shard_map/pack_first/pallas_call | solution.py:209
  7.2 11.8 %all-to-all-start = ((bf16[64,8,2560]{2,1,0:T(8,128)(2,1)}), bf16[64,8,2560]{2,1,0:T(8,128)(2,1)}, u32[]{:S(2)}, u32[]{:S(2)}) async-start(bf16[64,8,2560]{2,1,0:T(8,128)(2,1)} %bitcast.73), calls=%async_computation | async-start | bytes 5242880 | tf_op jit(solution)/shard_map/all_to_all | solution.py:198
  19.0 3.5 %pack_rest.1 = bf16[512,1536]{1,0:T(8,128)(2,1)} custom-call(bf16[512,512]{1,0:T(8,128)(2,1)} %get-tuple-element.19.pick_ref, bf16[512,1024]{1,0:T(8,128)(2,1)} %bitcast.80, bf16[512,1024]{1,0:T(8,128)(2,1)} %bitcast.82, bf16[512,1024]{1,0:T(8,128)(2,1)} %bitcast.84), custom_call_target="tpu_custom_call" | custom-call | flops 805306368 | bytes 3145728 | tf_op jit(solution)/shard_map/pack_rest/pallas_call | solution.py:255
  22.6 56.9 %all-to-all-done = bf16[64,8,2560]{2,1,0:T(8,128)(2,1)} async-done(((bf16[64,8,2560]{2,1,0:T(8,128)(2,1)}), bf16[64,8,2560]{2,1,0:T(8,128)(2,1)}, u32[]{:S(2)}, u32[]{:S(2)}) %all-to-all-start) | async-done | bytes 2621472 | tf_op jit(solution)/shard_map/all_to_all | solution.py:198
  79.5 7.6 %all-to-all-start.1 = ((bf16[64,8,1536]{2,1,0:T(8,128)(2,1)}), bf16[64,8,1536]{2,1,0:T(8,128)(2,1)}, u32[]{:S(2)}, u32[]{:S(2)}) async-start(bf16[64,8,1536]{2,1,0:T(8,128)(2,1)} %bitcast.68), calls=%async_computation.1 | async-start | bytes 3145728 | tf_op jit(solution)/shard_map/all_to_all | solution.py:198
  92.1 2.3 collective-permute-start.2
  94.5 2.9 %collective-permute-done.2 = bf16[4,512]{1,0:T(4,128)(2,1)S(1)} collective-permute-done((bf16[4,512]{1,0:T(4,128)(2,1)S(1)}, bf16[4,512]{1,0:T(4,128)(2,1)S(1)}, u32[]{:S(2)}, u32[]{:S(2)}) %collective-permute-start.2) | collective-permute-done | bytes 4128 | tf_op jit(solution)/shard_map/ppermute | solution.py:242
  99.2 3.3 %collective-permute-start.4 = (bf16[8,512]{1,0:T(8,128)(2,1)S(1)}, bf16[8,512]{1,0:T(8,128)(2,1)S(1)}, u32[]{:S(2)}, u32[]{:S(2)}) collective-permute-start(bf16[8,512]{1,0:T(8,128)(2,1)S(1)} %pad_maximum_fusion.2.refs_1_), channel_id=1, source_target_pairs={{0,16},{4,20},{8,24},{12,28},{16,32},{20,36},{24,40},{28,44},{32,4... | collective-permute-start | bytes 24584 | tf_op jit(solution)/shard_map/ppermute | solution.py:237
  103.1 3.2 %collective-permute-start.6 = (bf16[8,512]{1,0:T(8,128)(2,1)S(1)}, bf16[8,512]{1,0:T(8,128)(2,1)S(1)}, u32[]{:S(2)}, u32[]{:S(2)}) collective-permute-start(bf16[8,512]{1,0:T(8,128)(2,1)S(1)} %pad_maximum_fusion.2.refs_1_), channel_id=1, source_target_pairs={{0,32},{4,36},{8,40},{12,44},{16,48},{20,52},{24,56},{28,60},{32,0... | collective-permute-start | bytes 24584 | tf_op jit(solution)/shard_map/ppermute | solution.py:237
  108.0 13.3 %collective-permute-done.3.refs_2_ = bf16[8,512]{1,0:T(8,128)(2,1)S(1)} collective-permute-done((bf16[8,512]{1,0:T(8,128)(2,1)S(1)}, bf16[8,512]{1,0:T(8,128)(2,1)S(1)}, u32[]{:S(2)}, u32[]{:S(2)}) %collective-permute-start.3) | collective-permute-done | bytes 8224 | tf_op jit(solution)/shard_map/ppermute | solution.py:237
  121.3 4.7 %collective-permute-start.8 = (bf16[8,512]{1,0:T(8,128)(2,1)S(1)}, bf16[8,512]{1,0:T(8,128)(2,1)S(1)}, u32[]{:S(2)}, u32[]{:S(2)}) collective-permute-start(bf16[8,512]{1,0:T(8,128)(2,1)S(1)} %pad_maximum_fusion.2.refs_1_), channel_id=1, source_target_pairs={{0,48},{4,52},{8,56},{12,60},{16,0},{20,4},{24,8},{28,12},{32,16},... | collective-permute-start | bytes 24584 | tf_op jit(solution)/shard_map/ppermute | solution.py:237
  127.5 2.2 collective-permute-done.9.refs_8_
  132.2 10.2 %attend.3 = (bf16[512,1536]{1,0:T(8,128)(2,1)}, bf16[512,512]{1,0:T(8,128)(2,1)}) custom-call(bf16[512,2560]{1,0:T(8,128)(2,1)} %bitcast.6.refs_0_.refs_3_.refs_4_.refs_5_, f32[1,512]{1,0:T(1,128)} %tag_order.1.refs_1_, bf16[1024,1024]{1,0:T(8,128)(2,1)} %refs_2_.3, bf16[512,2560]{1,0:T(8,128)(2,1)} %bitcast.6.refs_0_.refs_3_.refs_4_.refs_5_, ...), custom_call_target="tpu_custom_call" | custom-call | flops 2147483648 | bytes 5767168 | tf_op jit(solution)/shard_map/attend/pallas_call | solution.py:276
  142.5 9.1 %all-to-all-start.3 = ((bf16[64,8,1536]{2,1,0:T(8,128)(2,1)}), bf16[64,8,1536]{2,1,0:T(8,128)(2,1)}, u32[]{:S(2)}, u32[]{:S(2)}) async-start(bf16[64,8,1536]{2,1,0:T(8,128)(2,1)} %bitcast.76), calls=%async_computation.3 | async-start | bytes 3145728 | tf_op jit(solution)/shard_map/all_to_all | solution.py:198
  155.9 10.2 %attend.2 = (bf16[512,1536]{1,0:T(8,128)(2,1)}, bf16[512,512]{1,0:T(8,128)(2,1)}) custom-call(bf16[512,2560]{1,0:T(8,128)(2,1)} %bitcast.6.refs_0_.refs_3_.refs_4_.refs_5_, f32[1,512]{1,0:T(1,128)} %tag_order.1.refs_1_, bf16[1024,1024]{1,0:T(8,128)(2,1)} %refs_2_.3, bf16[512,1536]{1,0:T(8,128)(2,1)} %bitcast.11.refs_3_.refs_4_.refs_5_, ...), custom_call_target="tpu_custom_call" | custom-call | flops 2147483648 | bytes 5767168 | tf_op jit(solution)/shard_map/attend/pallas_call | solution.py:276
  167.7 22.3 %all-to-all-done.3 = bf16[64,8,1536]{2,1,0:T(8,128)(2,1)} async-done(((bf16[64,8,1536]{2,1,0:T(8,128)(2,1)}), bf16[64,8,1536]{2,1,0:T(8,128)(2,1)}, u32[]{:S(2)}, u32[]{:S(2)}) %all-to-all-start.3) | async-done | bytes 1572896 | tf_op jit(solution)/shard_map/all_to_all | solution.py:198
  189.9 7.8 %all-to-all-start.2 = ((bf16[64,8,1536]{2,1,0:T(8,128)(2,1)}), bf16[64,8,1536]{2,1,0:T(8,128)(2,1)}, u32[]{:S(2)}, u32[]{:S(2)}) async-start(bf16[64,8,1536]{2,1,0:T(8,128)(2,1)} %bitcast.12), calls=%async_computation.2 | async-start | bytes 3145728 | tf_op jit(solution)/shard_map/all_to_all | solution.py:198
  199.4 2.7 %collective-permute-start.12 = (bf16[512,128]{1,0:T(8,128)(2,1)S(1)}, bf16[512,128]{1,0:T(8,128)(2,1)S(1)}, u32[]{:S(2)}, u32[]{:S(2)}) collective-permute-start(bf16[512,128]{1,0:T(8,128)(2,1)S(1)} %get-tuple-element.39), channel_id=1, source_target_pairs={{0,2},{1,3},{2,0},{3,1},{4,6},{5,7},{6,4},{7,5},{8,10},{9,11},{10,... | collective-permute-start | bytes 393224 | tf_op jit(solution)/shard_map/ppermute | solution.py:345
  204.6 3.8 %collective-permute-done.12 = bf16[512,128]{1,0:T(8,128)(2,1)S(1)} collective-permute-done((bf16[512,128]{1,0:T(8,128)(2,1)S(1)}, bf16[512,128]{1,0:T(8,128)(2,1)S(1)}, u32[]{:S(2)}, u32[]{:S(2)}) %collective-permute-start.12) | collective-permute-done | bytes 131104 | tf_op jit(solution)/shard_map/ppermute | solution.py:345
  214.3 2.4 collective-permute-start.16
  220.1 3.0 %collective-permute-done.16 = bf16[512,128]{1,0:T(8,128)(2,1)S(1)} collective-permute-done((bf16[512,128]{1,0:T(8,128)(2,1)S(1)}, bf16[512,128]{1,0:T(8,128)(2,1)S(1)}, u32[]{:S(2)}, u32[]{:S(2)}) %collective-permute-start.16) | collective-permute-done | bytes 131104 | tf_op jit(solution)/shard_map/ppermute | solution.py:345
  226.0 2.3 collective-permute-start.20
  228.3 3.5 %collective-permute-done.19 = bf16[128,256]{1,0:T(8,128)(2,1)S(1)} collective-permute-done((bf16[128,256]{1,0:T(8,128)(2,1)S(1)}, bf16[128,256]{1,0:T(8,128)(2,1)S(1)}, u32[]{:S(2)}, u32[]{:S(2)}) %collective-permute-start.19) | collective-permute-done | bytes 65568 | tf_op jit(solution)/shard_map/ppermute | solution.py:358
  232.6 3.0 %collective-permute-start.21 = (bf16[128,256]{1,0:T(8,128)(2,1)S(1)}, bf16[128,256]{1,0:T(8,128)(2,1)S(1)}, u32[]{:S(2)}, u32[]{:S(2)}) collective-permute-start(bf16[128,256]{1,0:T(8,128)(2,1)S(1)} %fusion.7), channel_id=1, source_target_pairs={{0,3},{1,0},{2,1},{3,2},{4,7},{5,4},{6,5},{7,6},{8,11},{9,8},{10,9... | collective-permute-start | bytes 196616 | tf_op jit(solution)/shard_map/ppermute | solution.py:363
  238.2 3.2 %collective-permute-done.22 = bf16[128,256]{1,0:T(8,128)(2,1)S(1)} collective-permute-done((bf16[128,256]{1,0:T(8,128)(2,1)S(1)}, bf16[128,256]{1,0:T(8,128)(2,1)S(1)}, u32[]{:S(2)}, u32[]{:S(2)}) %collective-permute-start.22) | collective-permute-done | bytes 65568 | tf_op jit(solution)/shard_map/ppermute | solution.py:363
  244.2 4.2 %collective-permute-start.25 = (bf16[16,1024]{1,0:T(8,128)(2,1)S(1)}, bf16[16,1024]{1,0:T(8,128)(2,1)S(1)}, u32[]{:S(2)}, u32[]{:S(2)}) collective-permute-start(bf16[16,1024]{1,0:T(8,128)(2,1)S(1)} %get-tuple-element.48), channel_id=1, source_target_pairs={{0,16},{4,20},{8,24},{12,28},{16,32},{20,36},{24,40},{28,44},{32,4... | collective-permute-start | bytes 98312 | tf_op jit(solution)/shard_map/ppermute | solution.py:369
  249.0 2.5 collective-permute-start.27
  251.5 2.6 collective-permute-start.28
  254.0 2.9 %collective-permute-start.29 = (bf16[16,1024]{1,0:T(8,128)(2,1)S(1)}, bf16[16,1024]{1,0:T(8,128)(2,1)S(1)}, u32[]{:S(2)}, u32[]{:S(2)}) collective-permute-start(bf16[16,1024]{1,0:T(8,128)(2,1)S(1)} %get-tuple-element.44), channel_id=1, source_target_pairs={{0,48},{4,52},{8,56},{12,60},{16,0},{20,4},{24,8},{28,12},{32,16},... | collective-permute-start | bytes 98312 | tf_op jit(solution)/shard_map/ppermute | solution.py:369
  256.9 2.5 collective-permute-start.30
  263.2 3.6 %unpack_a.1 = (bf16[512,1024]{1,0:T(8,128)(2,1)}, bf16[512,1024]{1,0:T(8,128)(2,1)}, bf16[512,1024]{1,0:T(8,128)(2,1)}) custom-call(bf16[512,512]{1,0:T(8,128)(2,1)} %bitcast.74, bf16[512,1536]{1,0:T(8,128)(2,1)} %bitcast.15.refs_1_), custom_call_target="tpu_custom_call" | custom-call | flops 805306368 | bytes 3145728 | tf_op jit(solution)/shard_map/unpack_a/pallas_call | solution.py:308
  266.8 3.4 %unpack_b.1 = (bf16[512,1024]{1,0:T(8,128)(2,1)}, bf16[512,1024]{1,0:T(8,128)(2,1)}, bf16[512,1024]{1,0:T(8,128)(2,1)}) custom-call(bf16[512,512]{1,0:T(8,128)(2,1)} %bitcast.75, bf16[512,1536]{1,0:T(8,128)(2,1)} %bitcast.13.refs_1_, bf16[512,1024]{1,0:T(8,128)(2,1)} %get-tuple-element.24.refs_2_, ...), custom_call_target="tpu_custom_call", output_to_operand_aliasing={{0}: (2, {}), {1}: (3, {}), {2}: (4, {})} | custom-call | flops 805306368 | bytes 3145728 | tf_op jit(solution)/shard_map/unpack_b/pallas_call | solution.py:318
  (106 shorter events, 45.7 us)
Async XLA Ops:
  7.2 72.3 %all-to-all-start = ((bf16[64,8,2560]{2,1,0:T(8,128)(2,1)}), bf16[64,8,2560]{2,1,0:T(8,128)(2,1)}, u32[]{:S(2)}, u32[]{:S(2)}) async-start(bf16[64,8,2560]{2,1,0:T(8,128)(2,1)} %bitcast.73), calls=%async_computation | async-start | bytes 5242880 | tf_op jit(solution)/shard_map/all_to_all | solution.py:198
  79.5 63.0 %all-to-all-start.1 = ((bf16[64,8,1536]{2,1,0:T(8,128)(2,1)}), bf16[64,8,1536]{2,1,0:T(8,128)(2,1)}, u32[]{:S(2)}, u32[]{:S(2)}) async-start(bf16[64,8,1536]{2,1,0:T(8,128)(2,1)} %bitcast.68), calls=%async_computation.1 | async-start | bytes 3145728 | tf_op jit(solution)/shard_map/all_to_all | solution.py:198
  88.4 3.7 %collective-permute-start.1 = (bf16[2,512]{1,0:T(2,128)(2,1)S(1)}, bf16[2,512]{1,0:T(2,128)(2,1)S(1)}, u32[]{:S(2)}, u32[]{:S(2)}) collective-permute-start(bf16[2,512]{1,0:T(2,128)(2,1)S(1)} %pad_maximum_fusion.4), channel_id=1, source_target_pairs={{0,64},{4,68},{8,72},{12,76},{16,80},{20,84},{24,88},{28,92},{32,9... | collective-permute-start | bytes 6152 | tf_op jit(solution)/shard_map/ppermute | solution.py:242
  92.1 5.3 %collective-permute-start.2 = (bf16[4,512]{1,0:T(4,128)(2,1)S(1)}, bf16[4,512]{1,0:T(4,128)(2,1)S(1)}, u32[]{:S(2)}, u32[]{:S(2)}) collective-permute-start(bf16[4,512]{1,0:T(4,128)(2,1)S(1)} %pad_maximum_fusion.3), channel_id=1, source_target_pairs={{0,128},{4,132},{8,136},{12,140},{16,144},{20,148},{24,152},{28,15... | collective-permute-start | bytes 12296 | tf_op jit(solution)/shard_map/ppermute | solution.py:242
  97.4 23.9 %collective-permute-start.3 = (bf16[8,512]{1,0:T(8,128)(2,1)S(1)}, bf16[8,512]{1,0:T(8,128)(2,1)S(1)}, u32[]{:S(2)}, u32[]{:S(2)}) collective-permute-start(bf16[8,512]{1,0:T(8,128)(2,1)S(1)} %pad_maximum_fusion.2.refs_1_), channel_id=1, source_target_pairs={{0,8},{4,12},{8,16},{12,20},{16,24},{20,28},{24,32},{28,36},{32,40... | collective-permute-start | bytes 24584 | tf_op jit(solution)/shard_map/ppermute | solution.py:237
  99.2 26.8 %collective-permute-start.4 = (bf16[8,512]{1,0:T(8,128)(2,1)S(1)}, bf16[8,512]{1,0:T(8,128)(2,1)S(1)}, u32[]{:S(2)}, u32[]{:S(2)}) collective-permute-start(bf16[8,512]{1,0:T(8,128)(2,1)S(1)} %pad_maximum_fusion.2.refs_1_), channel_id=1, source_target_pairs={{0,16},{4,20},{8,24},{12,28},{16,32},{20,36},{24,40},{28,44},{32,4... | collective-permute-start | bytes 24584 | tf_op jit(solution)/shard_map/ppermute | solution.py:237
  102.5 24.9 %collective-permute-start.5 = (bf16[8,512]{1,0:T(8,128)(2,1)S(1)}, bf16[8,512]{1,0:T(8,128)(2,1)S(1)}, u32[]{:S(2)}, u32[]{:S(2)}) collective-permute-start(bf16[8,512]{1,0:T(8,128)(2,1)S(1)} %pad_maximum_fusion.2.refs_1_), channel_id=1, source_target_pairs={{0,24},{4,28},{8,32},{12,36},{16,40},{20,44},{24,48},{28,52},{32,5... | collective-permute-start | bytes 24584 | tf_op jit(solution)/shard_map/ppermute | solution.py:237
  103.1 24.3 %collective-permute-start.6 = (bf16[8,512]{1,0:T(8,128)(2,1)S(1)}, bf16[8,512]{1,0:T(8,128)(2,1)S(1)}, u32[]{:S(2)}, u32[]{:S(2)}) collective-permute-start(bf16[8,512]{1,0:T(8,128)(2,1)S(1)} %pad_maximum_fusion.2.refs_1_), channel_id=1, source_target_pairs={{0,32},{4,36},{8,40},{12,44},{16,48},{20,52},{24,56},{28,60},{32,0... | collective-permute-start | bytes 24584 | tf_op jit(solution)/shard_map/ppermute | solution.py:237
  106.3 21.2 %collective-permute-start.7 = (bf16[8,512]{1,0:T(8,128)(2,1)S(1)}, bf16[8,512]{1,0:T(8,128)(2,1)S(1)}, u32[]{:S(2)}, u32[]{:S(2)}) collective-permute-start(bf16[8,512]{1,0:T(8,128)(2,1)S(1)} %pad_maximum_fusion.2.refs_1_), channel_id=1, source_target_pairs={{0,40},{4,44},{8,48},{12,52},{16,56},{20,60},{24,0},{28,4},{32,8},... | collective-permute-start | bytes 24584 | tf_op jit(solution)/shard_map/ppermute | solution.py:237
  121.3 6.1 %collective-permute-start.8 = (bf16[8,512]{1,0:T(8,128)(2,1)S(1)}, bf16[8,512]{1,0:T(8,128)(2,1)S(1)}, u32[]{:S(2)}, u32[]{:S(2)}) collective-permute-start(bf16[8,512]{1,0:T(8,128)(2,1)S(1)} %pad_maximum_fusion.2.refs_1_), channel_id=1, source_target_pairs={{0,48},{4,52},{8,56},{12,60},{16,0},{20,4},{24,8},{28,12},{32,16},... | collective-permute-start | bytes 24584 | tf_op jit(solution)/shard_map/ppermute | solution.py:237
  142.5 47.4 %all-to-all-start.3 = ((bf16[64,8,1536]{2,1,0:T(8,128)(2,1)}), bf16[64,8,1536]{2,1,0:T(8,128)(2,1)}, u32[]{:S(2)}, u32[]{:S(2)}) async-start(bf16[64,8,1536]{2,1,0:T(8,128)(2,1)} %bitcast.76), calls=%async_computation.3 | async-start | bytes 3145728 | tf_op jit(solution)/shard_map/all_to_all | solution.py:198
  155.8 10.3 %collective-permute-start.10 = (bf16[32,16,512]{2,1,0:T(8,128)(2,1)}, bf16[32,16,512]{2,1,0:T(8,128)(2,1)}, u32[]{:S(2)}, u32[]{:S(2)}) collective-permute-start(bf16[32,16,512]{2,1,0:T(8,128)(2,1)} %fusion.4), channel_id=1, source_target_pairs={{0,4},{4,0},{8,12},{12,8},{16,20},{20,16},{24,28},{28,24},{32,36},... | collective-permute-start | bytes 1572872 | tf_op jit(solution)/shard_map/ppermute | solution.py:340
  189.9 76.9 %all-to-all-start.2 = ((bf16[64,8,1536]{2,1,0:T(8,128)(2,1)}), bf16[64,8,1536]{2,1,0:T(8,128)(2,1)}, u32[]{:S(2)}, u32[]{:S(2)}) async-start(bf16[64,8,1536]{2,1,0:T(8,128)(2,1)} %bitcast.12), calls=%async_computation.2 | async-start | bytes 3145728 | tf_op jit(solution)/shard_map/all_to_all | solution.py:198
  197.8 6.8 %collective-permute-start.11 = (bf16[512,128]{1,0:T(8,128)(2,1)S(1)}, bf16[512,128]{1,0:T(8,128)(2,1)S(1)}, u32[]{:S(2)}, u32[]{:S(2)}) collective-permute-start(bf16[512,128]{1,0:T(8,128)(2,1)S(1)} %get-tuple-element.37), channel_id=1, source_target_pairs={{0,1},{1,2},{2,3},{3,0},{4,5},{5,6},{6,7},{7,4},{8,9},{9,10},{10,1... | collective-permute-start | bytes 393224 | tf_op jit(solution)/shard_map/ppermute | solution.py:345
  199.4 9.0 %collective-permute-start.12 = (bf16[512,128]{1,0:T(8,128)(2,1)S(1)}, bf16[512,128]{1,0:T(8,128)(2,1)S(1)}, u32[]{:S(2)}, u32[]{:S(2)}) collective-permute-start(bf16[512,128]{1,0:T(8,128)(2,1)S(1)} %get-tuple-element.39), channel_id=1, source_target_pairs={{0,2},{1,3},{2,0},{3,1},{4,6},{5,7},{6,4},{7,5},{8,10},{9,11},{10,... | collective-permute-start | bytes 393224 | tf_op jit(solution)/shard_map/ppermute | solution.py:345
  202.1 6.3 %collective-permute-start.13 = (bf16[512,128]{1,0:T(8,128)(2,1)S(1)}, bf16[512,128]{1,0:T(8,128)(2,1)S(1)}, u32[]{:S(2)}, u32[]{:S(2)}) collective-permute-start(bf16[512,128]{1,0:T(8,128)(2,1)S(1)} %get-tuple-element.38), channel_id=1, source_target_pairs={{0,3},{1,0},{2,1},{3,2},{4,7},{5,4},{6,5},{7,6},{8,11},{9,8},{10,9... | collective-permute-start | bytes 393224 | tf_op jit(solution)/shard_map/ppermute | solution.py:345
  212.9 7.2 %collective-permute-start.15 = (bf16[512,128]{1,0:T(8,128)(2,1)S(1)}, bf16[512,128]{1,0:T(8,128)(2,1)S(1)}, u32[]{:S(2)}, u32[]{:S(2)}) collective-permute-start(bf16[512,128]{1,0:T(8,128)(2,1)S(1)} %get-tuple-element.34), channel_id=1, source_target_pairs={{0,1},{1,2},{2,3},{3,0},{4,5},{5,6},{6,7},{7,4},{8,9},{9,10},{10,1... | collective-permute-start | bytes 393224 | tf_op jit(solution)/shard_map/ppermute | solution.py:345
  214.3 8.7 %collective-permute-start.16 = (bf16[512,128]{1,0:T(8,128)(2,1)S(1)}, bf16[512,128]{1,0:T(8,128)(2,1)S(1)}, u32[]{:S(2)}, u32[]{:S(2)}) collective-permute-start(bf16[512,128]{1,0:T(8,128)(2,1)S(1)} %get-tuple-element.36), channel_id=1, source_target_pairs={{0,2},{1,3},{2,0},{3,1},{4,6},{5,7},{6,4},{7,5},{8,10},{9,11},{10,... | collective-permute-start | bytes 393224 | tf_op jit(solution)/shard_map/ppermute | solution.py:345
  216.7 6.4 %collective-permute-start.17 = (bf16[512,128]{1,0:T(8,128)(2,1)S(1)}, bf16[512,128]{1,0:T(8,128)(2,1)S(1)}, u32[]{:S(2)}, u32[]{:S(2)}) collective-permute-start(bf16[512,128]{1,0:T(8,128)(2,1)S(1)} %get-tuple-element.35), channel_id=1, source_target_pairs={{0,3},{1,0},{2,1},{3,2},{4,7},{5,4},{6,5},{7,6},{8,11},{9,8},{10,9... | collective-permute-start | bytes 393224 | tf_op jit(solution)/shard_map/ppermute | solution.py:345
  223.3 5.0 %collective-permute-start.18 = (bf16[128,256]{1,0:T(8,128)(2,1)S(1)}, bf16[128,256]{1,0:T(8,128)(2,1)S(1)}, u32[]{:S(2)}, u32[]{:S(2)}) collective-permute-start(bf16[128,256]{1,0:T(8,128)(2,1)S(1)} %get-tuple-element.40), channel_id=1, source_target_pairs={{0,64},{4,68},{8,72},{12,76},{16,80},{20,84},{24,88},{28,92},{32,9... | collective-permute-start | bytes 196616 | tf_op jit(solution)/shard_map/ppermute | solution.py:358
  224.9 6.9 %collective-permute-start.19 = (bf16[128,256]{1,0:T(8,128)(2,1)S(1)}, bf16[128,256]{1,0:T(8,128)(2,1)S(1)}, u32[]{:S(2)}, u32[]{:S(2)}) collective-permute-start(bf16[128,256]{1,0:T(8,128)(2,1)S(1)} %get-tuple-element.42), channel_id=1, source_target_pairs={{0,128},{4,132},{8,136},{12,140},{16,144},{20,148},{24,152},{28,15... | collective-permute-start | bytes 196616 | tf_op jit(solution)/shard_map/ppermute | solution.py:358
  226.0 6.6 %collective-permute-start.20 = (bf16[128,256]{1,0:T(8,128)(2,1)S(1)}, bf16[128,256]{1,0:T(8,128)(2,1)S(1)}, u32[]{:S(2)}, u32[]{:S(2)}) collective-permute-start(bf16[128,256]{1,0:T(8,128)(2,1)S(1)} %get-tuple-element.41), channel_id=1, source_target_pairs={{0,192},{4,196},{8,200},{12,204},{16,208},{20,212},{24,216},{28,22... | collective-permute-start | bytes 196616 | tf_op jit(solution)/shard_map/ppermute | solution.py:358
  232.6 5.6 %collective-permute-start.21 = (bf16[128,256]{1,0:T(8,128)(2,1)S(1)}, bf16[128,256]{1,0:T(8,128)(2,1)S(1)}, u32[]{:S(2)}, u32[]{:S(2)}) collective-permute-start(bf16[128,256]{1,0:T(8,128)(2,1)S(1)} %fusion.7), channel_id=1, source_target_pairs={{0,3},{1,0},{2,1},{3,2},{4,7},{5,4},{6,5},{7,6},{8,11},{9,8},{10,9... | collective-permute-start | bytes 196616 | tf_op jit(solution)/shard_map/ppermute | solution.py:363
  235.6 5.8 %collective-permute-start.22 = (bf16[128,256]{1,0:T(8,128)(2,1)S(1)}, bf16[128,256]{1,0:T(8,128)(2,1)S(1)}, u32[]{:S(2)}, u32[]{:S(2)}) collective-permute-start(bf16[128,256]{1,0:T(8,128)(2,1)S(1)} %fusion.7), channel_id=1, source_target_pairs={{0,2},{1,3},{2,0},{3,1},{4,6},{5,7},{6,4},{7,5},{8,10},{9,11},{10,... | collective-permute-start | bytes 196616 | tf_op jit(solution)/shard_map/ppermute | solution.py:363
  236.9 5.5 %collective-permute-start.23 = (bf16[128,256]{1,0:T(8,128)(2,1)S(1)}, bf16[128,256]{1,0:T(8,128)(2,1)S(1)}, u32[]{:S(2)}, u32[]{:S(2)}) collective-permute-start(bf16[128,256]{1,0:T(8,128)(2,1)S(1)} %fusion.7), channel_id=1, source_target_pairs={{0,1},{1,2},{2,3},{3,0},{4,5},{5,6},{6,7},{7,4},{8,9},{9,10},{10,1... | collective-permute-start | bytes 196616 | tf_op jit(solution)/shard_map/ppermute | solution.py:363
  243.1 10.9 %collective-permute-start.24 = (bf16[16,1024]{1,0:T(8,128)(2,1)S(1)}, bf16[16,1024]{1,0:T(8,128)(2,1)S(1)}, u32[]{:S(2)}, u32[]{:S(2)}) collective-permute-start(bf16[16,1024]{1,0:T(8,128)(2,1)S(1)} %get-tuple-element.49), channel_id=1, source_target_pairs={{0,8},{4,12},{8,16},{12,20},{16,24},{20,28},{24,32},{28,36},{32,40... | collective-permute-start | bytes 98312 | tf_op jit(solution)/shard_map/ppermute | solution.py:369
  244.2 12.8 %collective-permute-start.25 = (bf16[16,1024]{1,0:T(8,128)(2,1)S(1)}, bf16[16,1024]{1,0:T(8,128)(2,1)S(1)}, u32[]{:S(2)}, u32[]{:S(2)}) collective-permute-start(bf16[16,1024]{1,0:T(8,128)(2,1)S(1)} %get-tuple-element.48), channel_id=1, source_target_pairs={{0,16},{4,20},{8,24},{12,28},{16,32},{20,36},{24,40},{28,44},{32,4... | collective-permute-start | bytes 98312 | tf_op jit(solution)/shard_map/ppermute | solution.py:369
  248.4 12.1 %collective-permute-start.26 = (bf16[16,1024]{1,0:T(8,128)(2,1)S(1)}, bf16[16,1024]{1,0:T(8,128)(2,1)S(1)}, u32[]{:S(2)}, u32[]{:S(2)}) collective-permute-start(bf16[16,1024]{1,0:T(8,128)(2,1)S(1)} %get-tuple-element.47), channel_id=1, source_target_pairs={{0,24},{4,28},{8,32},{12,36},{16,40},{20,44},{24,48},{28,52},{32,5... | collective-permute-start | bytes 98312 | tf_op jit(solution)/shard_map/ppermute | solution.py:369
  249.0 11.5 %collective-permute-start.27 = (bf16[16,1024]{1,0:T(8,128)(2,1)S(1)}, bf16[16,1024]{1,0:T(8,128)(2,1)S(1)}, u32[]{:S(2)}, u32[]{:S(2)}) collective-permute-start(bf16[16,1024]{1,0:T(8,128)(2,1)S(1)} %get-tuple-element.46), channel_id=1, source_target_pairs={{0,32},{4,36},{8,40},{12,44},{16,48},{20,52},{24,56},{28,60},{32,0... | collective-permute-start | bytes 98312 | tf_op jit(solution)/shard_map/ppermute | solution.py:369
  251.5 9.1 %collective-permute-start.28 = (bf16[16,1024]{1,0:T(8,128)(2,1)S(1)}, bf16[16,1024]{1,0:T(8,128)(2,1)S(1)}, u32[]{:S(2)}, u32[]{:S(2)}) collective-permute-start(bf16[16,1024]{1,0:T(8,128)(2,1)S(1)} %get-tuple-element.45), channel_id=1, source_target_pairs={{0,40},{4,44},{8,48},{12,52},{16,56},{20,60},{24,0},{28,4},{32,8},... | collective-permute-start | bytes 98312 | tf_op jit(solution)/shard_map/ppermute | solution.py:369
  254.0 6.5 %collective-permute-start.29 = (bf16[16,1024]{1,0:T(8,128)(2,1)S(1)}, bf16[16,1024]{1,0:T(8,128)(2,1)S(1)}, u32[]{:S(2)}, u32[]{:S(2)}) collective-permute-start(bf16[16,1024]{1,0:T(8,128)(2,1)S(1)} %get-tuple-element.44), channel_id=1, source_target_pairs={{0,48},{4,52},{8,56},{12,60},{16,0},{20,4},{24,8},{28,12},{32,16},... | collective-permute-start | bytes 98312 | tf_op jit(solution)/shard_map/ppermute | solution.py:369
  256.9 4.1 %collective-permute-start.30 = (bf16[16,1024]{1,0:T(8,128)(2,1)S(1)}, bf16[16,1024]{1,0:T(8,128)(2,1)S(1)}, u32[]{:S(2)}, u32[]{:S(2)}) collective-permute-start(bf16[16,1024]{1,0:T(8,128)(2,1)S(1)} %get-tuple-element.43), channel_id=1, source_target_pairs={{0,56},{4,60},{8,0},{12,4},{16,8},{20,12},{24,16},{28,20},{32,24},... | collective-permute-start | bytes 98312 | tf_op jit(solution)/shard_map/ppermute | solution.py:369
  (23 other events, 215.2 us)

commit v4 on v3

--- a/solution.py
+++ b/solution.py
@@ -45,35 +45,21 @@
     ids_col = column_of(ids_row, rows)
     owner_col = jnp.floor(ids_col * (1.0 / CL_DEV))
     tag_row = ids_row - owner_row * CL_DEV + 1.0
-    down = lax.broadcasted_iota(jnp.int32, (rows, LANES), 0)
-    across = lax.broadcasted_iota(jnp.int32, (rows, LANES), 1)
-
-    @pl.loop(0, rows // LANES)
-    def _(j):
-        cols = pl.ds(pl.multiple_of(j * LANES, LANES), LANES)
-        owner = jnp.floor(ids_ref[:, cols].astype(F32) * (1.0 / CL_DEV))
-        same = (owner_col == owner) & (down < across + j * LANES)
-        rank = jnp.sum(jnp.where(same, 1.0, 0.0), axis=0, keepdims=True)
-        slot = (owner * bucket + rank).astype(jnp.int32)
-        pick_ref[:, cols] = jnp.where(down == slot, 1.0, 0.0).astype(BF)
-
+    down = lax.broadcasted_iota(jnp.int32, (rows, rows), 0)
+    across = lax.broadcasted_iota(jnp.int32, (rows, rows), 1)
+    same = (owner_col == owner_row) & (down < across)
+    rank = jnp.sum(jnp.where(same, 1.0, 0.0), axis=0, keepdims=True)
+    slot = (owner_row * bucket + rank).astype(jnp.int32)
+    pick = jnp.where(down == slot, 1.0, 0.0).astype(BF)
+    pick_ref[...] = pick
+    tags = jnp.broadcast_to(tag_row, (TAG_ROWS, rows)).astype(BF)
+    tag_ref[...] = nt(tags, pick)[:1].astype(BF)
     width = g_ref.shape[1]
-
-    def unit(n):
-        return pl.ds(pl.multiple_of(n * UNIT, UNIT), UNIT)
-
-    @pl.loop(0, width // UNIT)
-    def _(u):
-        out_ref[:, unit(u)] = nn(pick_ref[...], g_ref[:, unit(u)]).astype(BF)
-
-    @pl.loop(0, q_ref.shape[1] // UNIT)
-    def _(u):
+    out_ref[:, :width] = nn(pick, g_ref[...]).astype(BF)
+    for u in range(q_ref.shape[1] // UNIT):
         for m, ref in enumerate((q_ref, k_ref, v_ref)):
-            base = width // UNIT + 3 * u + m
-            out_ref[:, unit(base)] = nn(pick_ref[...], ref[:, unit(u)]).astype(BF)
-
-    tags = jnp.broadcast_to(tag_row, (TAG_ROWS, rows)).astype(BF)
-    tag_ref[...] = nt(tags, pick_ref[...])[:1].astype(BF)
+            base = width + (3 * u + m) * UNIT
+            out_ref[:, base : base + UNIT] = nn(pick, ref[:, u * UNIT : (u + 1) * UNIT]).astype(BF)
 
 
 def tag_order(sizes, bucket, at_ref, *refs):
@@ -156,7 +142,7 @@
     total = total * factor
     half = total.shape[1] // nx // 2
     for s in range(nx):
-        source = lax.rem(at_ref[0] + s, nx)
+        source = at_ref[0] ^ (s ^ (s >> 1))
         for m in range(2):
             cols = pl.ds(pl.multiple_of((m * nx + source) * half, half), half)
             base = (2 * s + m) * half
@@ -360,8 +346,13 @@
     for piece in came:
         total = total + piece
     low = lax.optimization_barrier(total).astype(BF)
-    pieces = [low] + [lax.ppermute(low, "rep", ring(nx, nx - s)) for s in range(1, nx)]
-    weight = lax.optimization_barrier(jnp.concatenate(pieces, axis=1))
+    held, turn = 1, low
+    while held < nx:
+        mask = 2 * held - 1
+        came = lax.ppermute(turn, "rep", [(i, i ^ mask) for i in range(nx)])
+        turn = jnp.concatenate([turn, came], axis=1)
+        held *= 2
+    weight = lax.optimization_barrier(turn)
     weight = weight.reshape(nz, width // node_count, width)
     shares = [pick_of(weight, iz, 0)]
     for s in range(1, nz):

time: 273 us -> 265 us (0.971)
  waiting for transfers between devices: 123 us -> 114 us
    all_to_all x4, waiting for transfers between devices: 79.2 us -> 73.3 us  [exchange(): lax.all_to_all(rows_in.reshape(node_count, bucket, c), 'nodes', split_axi...]
    ppermute x6, waiting for transfers between devices: 9.7 us -> 4.89 us  [reduced_over_chip_and_x(): came.append(lax.ppermute(sent, 'rep', ring(nx, s)))]
    ppermute x3 -> x2, waiting for transfers between devices: 5.47 us -> 6.51 us  [local(): came = lax.ppermute(turn, 'rep', [(i, i ^ mask) for i in range(nx)])]
  transfers between devices with their start and end apart: 35 -> 34, of which waited for: 19 -> 16; matrix products, arithmetic and copies ran while one was open for 3% -> 4% of each run, Pallas kernels for 11% -> 12%
where the time goes in v4:
time: 265 us; the launch traced here: 262 us
  waiting for transfers between devices  114 us (43%)
  starting transfers between devices  95.6 us (36%)
  Pallas kernels  39.6 us (15%)
  local copies, waits for them, and re-layouts  5.01 us (2%)
  matrix products  3.94 us (1%)
    all_to_all x4, waiting for transfers between devices, exchange(): lax.all_to_all(rows_in.reshape(node_count, bucket, c), 'nodes', split_axi...  73.3 us
    all_to_all x4, starting transfers between devices, exchange(): lax.all_to_all(rows_in.reshape(node_count, bucket, c), 'nodes', split_axi...  36.2 us
    pallas_call x2, Pallas kernels, attention(): pl.pallas_call(lambda *refs: attend(scale, *refs), out_shape=(sds((rows,...  20.4 us
    ppermute x7, starting transfers between devices, local(): shares.append(lax.ppermute(sent, 'nodes', hop(0, s, 0)))  18.1 us
    ppermute x8, waiting for transfers between devices, around(): lax.ppermute(line, 'nodes', hop(*step(s)))  16.4 us
    ppermute x8, starting transfers between devices, around(): lax.ppermute(line, 'nodes', hop(*step(s)))  16.4 us
    ppermute x6, starting transfers between devices, reduced_over_chip_and_x(): came.append(lax.ppermute(sent, 'rep', ring(nx, s)))  11.4 us
    ppermute x2, waiting for transfers between devices, local(): came = lax.ppermute(turn, 'rep', [(i, i ^ mask) for i in range(nx)])  6.51 us
  transfers between devices with their start and end apart: 34, of which 16 were waited for; matrix products, arithmetic and copies ran while one was open for 4% of the time, Pallas kernels for 12%

profile of v4, /device:TPU:40, one launch (start us, length us, event | category | flops | bytes accessed | tf_op | source)
XLA Modules:
  0.0 262.0 jit_solution(15723269042333531979)
XLA Ops:
  0.6 5.3 %pack_first.1 = (bf16[512,2560]{1,0:T(8,128)(2,1)}, bf16[512,512]{1,0:T(8,128)(2,1)}, bf16[1,512]{1,0:T(2,128)(2,1)}) custom-call(s32[1,512]{1,0:T(1,128)} %refs_0_.1, bf16[512,1024]{1,0:T(8,128)(2,1)} %bitcast.90, bf16[512,1024]{1,0:T(8,128)(2,1)} %bitcast.80, bf16[512,1024]{1,0:T(8,128)(2,1)} %bitcast.82, bf16[512,1024]{1,0:T(8,128)(2,1)} %bitcast.84), custom_call_target="tpu_custom_call" | custom-call | flops 1342177280 | bytes 5242880 | tf_op jit(solution)/shard_map/pack_first/pallas_call | solution.py:195
  6.0 11.8 %all-to-all-start = ((bf16[64,8,2560]{2,1,0:T(8,128)(2,1)}), bf16[64,8,2560]{2,1,0:T(8,128)(2,1)}, u32[]{:S(2)}, u32[]{:S(2)}) async-start(bf16[64,8,2560]{2,1,0:T(8,128)(2,1)} %bitcast.73), calls=%async_computation | async-start | bytes 5242880 | tf_op jit(solution)/shard_map/all_to_all | solution.py:184
  17.8 3.6 %pack_rest.1 = bf16[512,1536]{1,0:T(8,128)(2,1)} custom-call(bf16[512,512]{1,0:T(8,128)(2,1)} %get-tuple-element.19.pick_ref, bf16[512,1024]{1,0:T(8,128)(2,1)} %bitcast.81, bf16[512,1024]{1,0:T(8,128)(2,1)} %bitcast.83, bf16[512,1024]{1,0:T(8,128)(2,1)} %bitcast.85), custom_call_target="tpu_custom_call" | custom-call | flops 805306368 | bytes 3145728 | tf_op jit(solution)/shard_map/pack_rest/pallas_call | solution.py:241
  21.4 56.9 %all-to-all-done = bf16[64,8,2560]{2,1,0:T(8,128)(2,1)} async-done(((bf16[64,8,2560]{2,1,0:T(8,128)(2,1)}), bf16[64,8,2560]{2,1,0:T(8,128)(2,1)}, u32[]{:S(2)}, u32[]{:S(2)}) %all-to-all-start) | async-done | bytes 2621472 | tf_op jit(solution)/shard_map/all_to_all | solution.py:184
  78.2 7.6 %all-to-all-start.1 = ((bf16[64,8,1536]{2,1,0:T(8,128)(2,1)}), bf16[64,8,1536]{2,1,0:T(8,128)(2,1)}, u32[]{:S(2)}, u32[]{:S(2)}) async-start(bf16[64,8,1536]{2,1,0:T(8,128)(2,1)} %bitcast.68), calls=%async_computation.1 | async-start | bytes 3145728 | tf_op jit(solution)/shard_map/all_to_all | solution.py:184
  90.9 2.3 collective-permute-start.2
  93.2 2.9 %collective-permute-done.2 = bf16[4,512]{1,0:T(4,128)(2,1)S(1)} collective-permute-done((bf16[4,512]{1,0:T(4,128)(2,1)S(1)}, bf16[4,512]{1,0:T(4,128)(2,1)S(1)}, u32[]{:S(2)}, u32[]{:S(2)}) %collective-permute-start.2) | collective-permute-done | bytes 4128 | tf_op jit(solution)/shard_map/ppermute | solution.py:228
  98.0 3.3 %collective-permute-start.4 = (bf16[8,512]{1,0:T(8,128)(2,1)S(1)}, bf16[8,512]{1,0:T(8,128)(2,1)S(1)}, u32[]{:S(2)}, u32[]{:S(2)}) collective-permute-start(bf16[8,512]{1,0:T(8,128)(2,1)S(1)} %pad_maximum_fusion.3.refs_1_), channel_id=1, source_target_pairs={{0,16},{4,20},{8,24},{12,28},{16,32},{20,36},{24,40},{28,44},{32,4... | collective-permute-start | bytes 24584 | tf_op jit(solution)/shard_map/ppermute | solution.py:223
  101.9 3.2 %collective-permute-start.6 = (bf16[8,512]{1,0:T(8,128)(2,1)S(1)}, bf16[8,512]{1,0:T(8,128)(2,1)S(1)}, u32[]{:S(2)}, u32[]{:S(2)}) collective-permute-start(bf16[8,512]{1,0:T(8,128)(2,1)S(1)} %pad_maximum_fusion.3.refs_1_), channel_id=1, source_target_pairs={{0,32},{4,36},{8,40},{12,44},{16,48},{20,52},{24,56},{28,60},{32,0... | collective-permute-start | bytes 24584 | tf_op jit(solution)/shard_map/ppermute | solution.py:223
  106.8 13.3 %collective-permute-done.3.refs_2_ = bf16[8,512]{1,0:T(8,128)(2,1)S(1)} collective-permute-done((bf16[8,512]{1,0:T(8,128)(2,1)S(1)}, bf16[8,512]{1,0:T(8,128)(2,1)S(1)}, u32[]{:S(2)}, u32[]{:S(2)}) %collective-permute-start.3) | collective-permute-done | bytes 8224 | tf_op jit(solution)/shard_map/ppermute | solution.py:223
  120.1 4.7 %collective-permute-start.8 = (bf16[8,512]{1,0:T(8,128)(2,1)S(1)}, bf16[8,512]{1,0:T(8,128)(2,1)S(1)}, u32[]{:S(2)}, u32[]{:S(2)}) collective-permute-start(bf16[8,512]{1,0:T(8,128)(2,1)S(1)} %pad_maximum_fusion.3.refs_1_), channel_id=1, source_target_pairs={{0,48},{4,52},{8,56},{12,60},{16,0},{20,4},{24,8},{28,12},{32,16},... | collective-permute-start | bytes 24584 | tf_op jit(solution)/shard_map/ppermute | solution.py:223
  126.4 2.1 collective-permute-done.9.refs_8_
  131.0 10.2 %attend.3 = (bf16[512,1536]{1,0:T(8,128)(2,1)}, bf16[512,512]{1,0:T(8,128)(2,1)}) custom-call(bf16[512,2560]{1,0:T(8,128)(2,1)} %bitcast.6.refs_0_.refs_3_.refs_4_.refs_5_, f32[1,512]{1,0:T(1,128)} %tag_order.1.refs_1_, bf16[1024,1024]{1,0:T(8,128)(2,1)} %refs_2_.3, bf16[512,2560]{1,0:T(8,128)(2,1)} %bitcast.6.refs_0_.refs_3_.refs_4_.refs_5_, ...), custom_call_target="tpu_custom_call" | custom-call | flops 2147483648 | bytes 5767168 | tf_op jit(solution)/shard_map/attend/pallas_call | solution.py:262
  141.2 9.1 %all-to-all-start.3 = ((bf16[64,8,1536]{2,1,0:T(8,128)(2,1)}), bf16[64,8,1536]{2,1,0:T(8,128)(2,1)}, u32[]{:S(2)}, u32[]{:S(2)}) async-start(bf16[64,8,1536]{2,1,0:T(8,128)(2,1)} %bitcast.77), calls=%async_computation.3 | async-start | bytes 3145728 | tf_op jit(solution)/shard_map/all_to_all | solution.py:184
  157.9 2.7 %collective-permute-start.12 = (bf16[512,128]{1,0:T(8,128)(2,1)}, bf16[512,128]{1,0:T(8,128)(2,1)}, u32[]{:S(2)}, u32[]{:S(2)}) collective-permute-start(bf16[512,128]{1,0:T(8,128)(2,1)} %get-tuple-element.39), channel_id=1, source_target_pairs={{0,2},{1,3},{2,0},{3,1},{4,6},{5,7},{6,4},{7,5},{8,10},{9,11},{10,... | collective-permute-start | bytes 393224 | tf_op jit(solution)/shard_map/ppermute | solution.py:331
  162.1 10.2 %attend.2 = (bf16[512,1536]{1,0:T(8,128)(2,1)}, bf16[512,512]{1,0:T(8,128)(2,1)}) custom-call(bf16[512,2560]{1,0:T(8,128)(2,1)} %bitcast.6.refs_0_.refs_3_.refs_4_.refs_5_, f32[1,512]{1,0:T(1,128)} %tag_order.1.refs_1_, bf16[1024,1024]{1,0:T(8,128)(2,1)} %refs_2_.3, bf16[512,1536]{1,0:T(8,128)(2,1)} %bitcast.11.refs_3_.refs_4_.refs_5_, ...), custom_call_target="tpu_custom_call" | custom-call | flops 2147483648 | bytes 5767168 | tf_op jit(solution)/shard_map/attend/pallas_call | solution.py:262
  172.2 16.4 %all-to-all-done.3 = bf16[64,8,1536]{2,1,0:T(8,128)(2,1)} async-done(((bf16[64,8,1536]{2,1,0:T(8,128)(2,1)}), bf16[64,8,1536]{2,1,0:T(8,128)(2,1)}, u32[]{:S(2)}, u32[]{:S(2)}) %all-to-all-start.3) | async-done | bytes 1572896 | tf_op jit(solution)/shard_map/all_to_all | solution.py:184
  188.6 7.6 %all-to-all-start.2 = ((bf16[64,8,1536]{2,1,0:T(8,128)(2,1)}), bf16[64,8,1536]{2,1,0:T(8,128)(2,1)}, u32[]{:S(2)}, u32[]{:S(2)}) async-start(bf16[64,8,1536]{2,1,0:T(8,128)(2,1)} %bitcast.76), calls=%async_computation.2 | async-start | bytes 3145728 | tf_op jit(solution)/shard_map/all_to_all | solution.py:184
  203.5 2.7 %collective-permute-start.16 = (bf16[512,128]{1,0:T(8,128)(2,1)S(1)}, bf16[512,128]{1,0:T(8,128)(2,1)S(1)}, u32[]{:S(2)}, u32[]{:S(2)}) collective-permute-start(bf16[512,128]{1,0:T(8,128)(2,1)S(1)} %get-tuple-element.36), channel_id=1, source_target_pairs={{0,2},{1,3},{2,0},{3,1},{4,6},{5,7},{6,4},{7,5},{8,10},{9,11},{10,... | collective-permute-start | bytes 393224 | tf_op jit(solution)/shard_map/ppermute | solution.py:331
  208.8 3.8 %collective-permute-done.16 = bf16[512,128]{1,0:T(8,128)(2,1)S(1)} collective-permute-done((bf16[512,128]{1,0:T(8,128)(2,1)S(1)}, bf16[512,128]{1,0:T(8,128)(2,1)S(1)}, u32[]{:S(2)}, u32[]{:S(2)}) %collective-permute-start.16) | collective-permute-done | bytes 131104 | tf_op jit(solution)/shard_map/ppermute | solution.py:331
  215.4 2.3 collective-permute-start.20
  217.7 3.5 %collective-permute-done.19 = bf16[128,256]{1,0:T(8,128)(2,1)S(1)} collective-permute-done((bf16[128,256]{1,0:T(8,128)(2,1)S(1)}, bf16[128,256]{1,0:T(8,128)(2,1)S(1)}, u32[]{:S(2)}, u32[]{:S(2)}) %collective-permute-start.19) | collective-permute-done | bytes 65568 | tf_op jit(solution)/shard_map/ppermute | solution.py:344
  223.4 2.8 %collective-permute-done.21 = bf16[128,256]{1,0:T(8,128)(2,1)S(1)} collective-permute-done((bf16[128,256]{1,0:T(8,128)(2,1)S(1)}, bf16[128,256]{1,0:T(8,128)(2,1)S(1)}, u32[]{:S(2)}, u32[]{:S(2)}) %collective-permute-start.21) | collective-permute-done | bytes 65568 | tf_op jit(solution)/shard_map/ppermute | solution.py:352
  226.2 2.5 collective-permute-start.22
  228.7 3.7 %collective-permute-done.22 = bf16[128,512]{1,0:T(8,128)(2,1)S(1)} collective-permute-done((bf16[128,512]{1,0:T(8,128)(2,1)S(1)}, bf16[128,512]{1,0:T(8,128)(2,1)S(1)}, u32[]{:S(2)}, u32[]{:S(2)}) %collective-permute-start.22) | collective-permute-done | bytes 131104 | tf_op jit(solution)/shard_map/ppermute | solution.py:352
  234.3 6.9 %collective-permute-start.24 = (bf16[16,1024]{1,0:T(8,128)(2,1)S(1)}, bf16[16,1024]{1,0:T(8,128)(2,1)S(1)}, u32[]{:S(2)}, u32[]{:S(2)}) collective-permute-start(bf16[16,1024]{1,0:T(8,128)(2,1)S(1)} %get-tuple-element.48), channel_id=1, source_target_pairs={{0,16},{4,20},{8,24},{12,28},{16,32},{20,36},{24,40},{28,44},{32,4... | collective-permute-start | bytes 98312 | tf_op jit(solution)/shard_map/ppermute | solution.py:360
  241.2 2.5 collective-permute-start.26
  243.7 2.5 collective-permute-start.27
  246.2 2.4 collective-permute-start.28
  248.6 2.7 %collective-permute-start.29 = (bf16[16,1024]{1,0:T(8,128)(2,1)S(1)}, bf16[16,1024]{1,0:T(8,128)(2,1)S(1)}, u32[]{:S(2)}, u32[]{:S(2)}) collective-permute-start(bf16[16,1024]{1,0:T(8,128)(2,1)S(1)} %get-tuple-element.43), channel_id=1, source_target_pairs={{0,56},{4,60},{8,0},{12,4},{16,8},{20,12},{24,16},{28,20},{32,24},... | collective-permute-start | bytes 98312 | tf_op jit(solution)/shard_map/ppermute | solution.py:360
  255.0 3.6 %unpack_a.1 = (bf16[512,1024]{1,0:T(8,128)(2,1)}, bf16[512,1024]{1,0:T(8,128)(2,1)}, bf16[512,1024]{1,0:T(8,128)(2,1)}) custom-call(bf16[512,512]{1,0:T(8,128)(2,1)} %bitcast.74, bf16[512,1536]{1,0:T(8,128)(2,1)} %bitcast.15.refs_1_), custom_call_target="tpu_custom_call" | custom-call | flops 805306368 | bytes 3145728 | tf_op jit(solution)/shard_map/unpack_a/pallas_call | solution.py:294
  258.6 3.4 %unpack_b.1 = (bf16[512,1024]{1,0:T(8,128)(2,1)}, bf16[512,1024]{1,0:T(8,128)(2,1)}, bf16[512,1024]{1,0:T(8,128)(2,1)}) custom-call(bf16[512,512]{1,0:T(8,128)(2,1)} %bitcast.75, bf16[512,1536]{1,0:T(8,128)(2,1)} %bitcast.13.refs_1_, bf16[512,1024]{1,0:T(8,128)(2,1)} %get-tuple-element.24.refs_2_, ...), custom_call_target="tpu_custom_call", output_to_operand_aliasing={{0}: (2, {}), {1}: (3, {}), {2}: (4, {})} | custom-call | flops 805306368 | bytes 3145728 | tf_op jit(solution)/shard_map/unpack_b/pallas_call | solution.py:304
  (105 shorter events, 42.4 us)
Async XLA Ops:
  6.0 72.3 %all-to-all-start = ((bf16[64,8,2560]{2,1,0:T(8,128)(2,1)}), bf16[64,8,2560]{2,1,0:T(8,128)(2,1)}, u32[]{:S(2)}, u32[]{:S(2)}) async-start(bf16[64,8,2560]{2,1,0:T(8,128)(2,1)} %bitcast.73), calls=%async_computation | async-start | bytes 5242880 | tf_op jit(solution)/shard_map/all_to_all | solution.py:184
  78.2 62.9 %all-to-all-start.1 = ((bf16[64,8,1536]{2,1,0:T(8,128)(2,1)}), bf16[64,8,1536]{2,1,0:T(8,128)(2,1)}, u32[]{:S(2)}, u32[]{:S(2)}) async-start(bf16[64,8,1536]{2,1,0:T(8,128)(2,1)} %bitcast.68), calls=%async_computation.1 | async-start | bytes 3145728 | tf_op jit(solution)/shard_map/all_to_all | solution.py:184
  87.2 3.7 %collective-permute-start.1 = (bf16[2,512]{1,0:T(2,128)(2,1)S(1)}, bf16[2,512]{1,0:T(2,128)(2,1)S(1)}, u32[]{:S(2)}, u32[]{:S(2)}) collective-permute-start(bf16[2,512]{1,0:T(2,128)(2,1)S(1)} %pad_maximum_fusion.5), channel_id=1, source_target_pairs={{0,64},{4,68},{8,72},{12,76},{16,80},{20,84},{24,88},{28,92},{32,9... | collective-permute-start | bytes 6152 | tf_op jit(solution)/shard_map/ppermute | solution.py:228
  90.9 5.3 %collective-permute-start.2 = (bf16[4,512]{1,0:T(4,128)(2,1)S(1)}, bf16[4,512]{1,0:T(4,128)(2,1)S(1)}, u32[]{:S(2)}, u32[]{:S(2)}) collective-permute-start(bf16[4,512]{1,0:T(4,128)(2,1)S(1)} %pad_maximum_fusion.4), channel_id=1, source_target_pairs={{0,128},{4,132},{8,136},{12,140},{16,144},{20,148},{24,152},{28,15... | collective-permute-start | bytes 12296 | tf_op jit(solution)/shard_map/ppermute | solution.py:228
  96.2 23.9 %collective-permute-start.3 = (bf16[8,512]{1,0:T(8,128)(2,1)S(1)}, bf16[8,512]{1,0:T(8,128)(2,1)S(1)}, u32[]{:S(2)}, u32[]{:S(2)}) collective-permute-start(bf16[8,512]{1,0:T(8,128)(2,1)S(1)} %pad_maximum_fusion.3.refs_1_), channel_id=1, source_target_pairs={{0,8},{4,12},{8,16},{12,20},{16,24},{20,28},{24,32},{28,36},{32,40... | collective-permute-start | bytes 24584 | tf_op jit(solution)/shard_map/ppermute | solution.py:223
  98.0 26.8 %collective-permute-start.4 = (bf16[8,512]{1,0:T(8,128)(2,1)S(1)}, bf16[8,512]{1,0:T(8,128)(2,1)S(1)}, u32[]{:S(2)}, u32[]{:S(2)}) collective-permute-start(bf16[8,512]{1,0:T(8,128)(2,1)S(1)} %pad_maximum_fusion.3.refs_1_), channel_id=1, source_target_pairs={{0,16},{4,20},{8,24},{12,28},{16,32},{20,36},{24,40},{28,44},{32,4... | collective-permute-start | bytes 24584 | tf_op jit(solution)/shard_map/ppermute | solution.py:223
  101.3 25.0 %collective-permute-start.5 = (bf16[8,512]{1,0:T(8,128)(2,1)S(1)}, bf16[8,512]{1,0:T(8,128)(2,1)S(1)}, u32[]{:S(2)}, u32[]{:S(2)}) collective-permute-start(bf16[8,512]{1,0:T(8,128)(2,1)S(1)} %pad_maximum_fusion.3.refs_1_), channel_id=1, source_target_pairs={{0,24},{4,28},{8,32},{12,36},{16,40},{20,44},{24,48},{28,52},{32,5... | collective-permute-start | bytes 24584 | tf_op jit(solution)/shard_map/ppermute | solution.py:223
  101.9 24.4 %collective-permute-start.6 = (bf16[8,512]{1,0:T(8,128)(2,1)S(1)}, bf16[8,512]{1,0:T(8,128)(2,1)S(1)}, u32[]{:S(2)}, u32[]{:S(2)}) collective-permute-start(bf16[8,512]{1,0:T(8,128)(2,1)S(1)} %pad_maximum_fusion.3.refs_1_), channel_id=1, source_target_pairs={{0,32},{4,36},{8,40},{12,44},{16,48},{20,52},{24,56},{28,60},{32,0... | collective-permute-start | bytes 24584 | tf_op jit(solution)/shard_map/ppermute | solution.py:223
  105.0 21.3 %collective-permute-start.7 = (bf16[8,512]{1,0:T(8,128)(2,1)S(1)}, bf16[8,512]{1,0:T(8,128)(2,1)S(1)}, u32[]{:S(2)}, u32[]{:S(2)}) collective-permute-start(bf16[8,512]{1,0:T(8,128)(2,1)S(1)} %pad_maximum_fusion.3.refs_1_), channel_id=1, source_target_pairs={{0,40},{4,44},{8,48},{12,52},{16,56},{20,60},{24,0},{28,4},{32,8},... | collective-permute-start | bytes 24584 | tf_op jit(solution)/shard_map/ppermute | solution.py:223
  120.1 6.2 %collective-permute-start.8 = (bf16[8,512]{1,0:T(8,128)(2,1)S(1)}, bf16[8,512]{1,0:T(8,128)(2,1)S(1)}, u32[]{:S(2)}, u32[]{:S(2)}) collective-permute-start(bf16[8,512]{1,0:T(8,128)(2,1)S(1)} %pad_maximum_fusion.3.refs_1_), channel_id=1, source_target_pairs={{0,48},{4,52},{8,56},{12,60},{16,0},{20,4},{24,8},{28,12},{32,16},... | collective-permute-start | bytes 24584 | tf_op jit(solution)/shard_map/ppermute | solution.py:223
  124.8 3.7 %collective-permute-start.9 = (bf16[8,512]{1,0:T(8,128)(2,1)S(1)}, bf16[8,512]{1,0:T(8,128)(2,1)S(1)}, u32[]{:S(2)}, u32[]{:S(2)}) collective-permute-start(bf16[8,512]{1,0:T(8,128)(2,1)S(1)} %pad_maximum_fusion.3.refs_1_), channel_id=1, source_target_pairs={{0,56},{4,60},{8,0},{12,4},{16,8},{20,12},{24,16},{28,20},{32,24},... | collective-permute-start | bytes 24584 | tf_op jit(solution)/shard_map/ppermute | solution.py:223
  141.2 47.4 %all-to-all-start.3 = ((bf16[64,8,1536]{2,1,0:T(8,128)(2,1)}), bf16[64,8,1536]{2,1,0:T(8,128)(2,1)}, u32[]{:S(2)}, u32[]{:S(2)}) async-start(bf16[64,8,1536]{2,1,0:T(8,128)(2,1)} %bitcast.77), calls=%async_computation.3 | async-start | bytes 3145728 | tf_op jit(solution)/shard_map/all_to_all | solution.py:184
  152.4 2.0 collective-permute-start.10
  156.4 39.9 %collective-permute-start.11 = (bf16[512,128]{1,0:T(8,128)(2,1)}, bf16[512,128]{1,0:T(8,128)(2,1)}, u32[]{:S(2)}, u32[]{:S(2)}) collective-permute-start(bf16[512,128]{1,0:T(8,128)(2,1)} %get-tuple-element.37), channel_id=1, source_target_pairs={{0,1},{1,2},{2,3},{3,0},{4,5},{5,6},{6,7},{7,4},{8,9},{9,10},{10,1... | collective-permute-start | bytes 393224 | tf_op jit(solution)/shard_map/ppermute | solution.py:331
  157.9 38.4 %collective-permute-start.12 = (bf16[512,128]{1,0:T(8,128)(2,1)}, bf16[512,128]{1,0:T(8,128)(2,1)}, u32[]{:S(2)}, u32[]{:S(2)}) collective-permute-start(bf16[512,128]{1,0:T(8,128)(2,1)} %get-tuple-element.39), channel_id=1, source_target_pairs={{0,2},{1,3},{2,0},{3,1},{4,6},{5,7},{6,4},{7,5},{8,10},{9,11},{10,... | collective-permute-start | bytes 393224 | tf_op jit(solution)/shard_map/ppermute | solution.py:331
  160.6 35.7 %collective-permute-start.13 = (bf16[512,128]{1,0:T(8,128)(2,1)}, bf16[512,128]{1,0:T(8,128)(2,1)}, u32[]{:S(2)}, u32[]{:S(2)}) collective-permute-start(bf16[512,128]{1,0:T(8,128)(2,1)} %get-tuple-element.38), channel_id=1, source_target_pairs={{0,3},{1,0},{2,1},{3,2},{4,7},{5,4},{6,5},{7,6},{8,11},{9,8},{10,9... | collective-permute-start | bytes 393224 | tf_op jit(solution)/shard_map/ppermute | solution.py:331
  188.6 70.0 %all-to-all-start.2 = ((bf16[64,8,1536]{2,1,0:T(8,128)(2,1)}), bf16[64,8,1536]{2,1,0:T(8,128)(2,1)}, u32[]{:S(2)}, u32[]{:S(2)}) async-start(bf16[64,8,1536]{2,1,0:T(8,128)(2,1)} %bitcast.76), calls=%async_computation.2 | async-start | bytes 3145728 | tf_op jit(solution)/shard_map/all_to_all | solution.py:184
  201.9 6.8 %collective-permute-start.15 = (bf16[512,128]{1,0:T(8,128)(2,1)S(1)}, bf16[512,128]{1,0:T(8,128)(2,1)S(1)}, u32[]{:S(2)}, u32[]{:S(2)}) collective-permute-start(bf16[512,128]{1,0:T(8,128)(2,1)S(1)} %get-tuple-element.34), channel_id=1, source_target_pairs={{0,1},{1,2},{2,3},{3,0},{4,5},{5,6},{6,7},{7,4},{8,9},{9,10},{10,1... | collective-permute-start | bytes 393224 | tf_op jit(solution)/shard_map/ppermute | solution.py:331
  203.5 9.0 %collective-permute-start.16 = (bf16[512,128]{1,0:T(8,128)(2,1)S(1)}, bf16[512,128]{1,0:T(8,128)(2,1)S(1)}, u32[]{:S(2)}, u32[]{:S(2)}) collective-permute-start(bf16[512,128]{1,0:T(8,128)(2,1)S(1)} %get-tuple-element.36), channel_id=1, source_target_pairs={{0,2},{1,3},{2,0},{3,1},{4,6},{5,7},{6,4},{7,5},{8,10},{9,11},{10,... | collective-permute-start | bytes 393224 | tf_op jit(solution)/shard_map/ppermute | solution.py:331
  206.2 6.3 %collective-permute-start.17 = (bf16[512,128]{1,0:T(8,128)(2,1)S(1)}, bf16[512,128]{1,0:T(8,128)(2,1)S(1)}, u32[]{:S(2)}, u32[]{:S(2)}) collective-permute-start(bf16[512,128]{1,0:T(8,128)(2,1)S(1)} %get-tuple-element.35), channel_id=1, source_target_pairs={{0,3},{1,0},{2,1},{3,2},{4,7},{5,4},{6,5},{7,6},{8,11},{9,8},{10,9... | collective-permute-start | bytes 393224 | tf_op jit(solution)/shard_map/ppermute | solution.py:331
  212.7 5.0 %collective-permute-start.18 = (bf16[128,256]{1,0:T(8,128)(2,1)S(1)}, bf16[128,256]{1,0:T(8,128)(2,1)S(1)}, u32[]{:S(2)}, u32[]{:S(2)}) collective-permute-start(bf16[128,256]{1,0:T(8,128)(2,1)S(1)} %get-tuple-element.40), channel_id=1, source_target_pairs={{0,64},{4,68},{8,72},{12,76},{16,80},{20,84},{24,88},{28,92},{32,9... | collective-permute-start | bytes 196616 | tf_op jit(solution)/shard_map/ppermute | solution.py:344
  214.4 6.9 %collective-permute-start.19 = (bf16[128,256]{1,0:T(8,128)(2,1)S(1)}, bf16[128,256]{1,0:T(8,128)(2,1)S(1)}, u32[]{:S(2)}, u32[]{:S(2)}) collective-permute-start(bf16[128,256]{1,0:T(8,128)(2,1)S(1)} %get-tuple-element.42), channel_id=1, source_target_pairs={{0,128},{4,132},{8,136},{12,140},{16,144},{20,148},{24,152},{28,15... | collective-permute-start | bytes 196616 | tf_op jit(solution)/shard_map/ppermute | solution.py:344
  215.4 6.4 %collective-permute-start.20 = (bf16[128,256]{1,0:T(8,128)(2,1)S(1)}, bf16[128,256]{1,0:T(8,128)(2,1)S(1)}, u32[]{:S(2)}, u32[]{:S(2)}) collective-permute-start(bf16[128,256]{1,0:T(8,128)(2,1)S(1)} %get-tuple-element.41), channel_id=1, source_target_pairs={{0,192},{4,196},{8,200},{12,204},{16,208},{20,212},{24,216},{28,22... | collective-permute-start | bytes 196616 | tf_op jit(solution)/shard_map/ppermute | solution.py:344
  221.8 4.4 %collective-permute-start.21 = (bf16[128,256]{1,0:T(8,128)(2,1)S(1)}, bf16[128,256]{1,0:T(8,128)(2,1)S(1)}, u32[]{:S(2)}, u32[]{:S(2)}) collective-permute-start(bf16[128,256]{1,0:T(8,128)(2,1)S(1)} %fusion.7), channel_id=1, source_target_pairs={{0,1},{1,0},{2,3},{3,2},{4,5},{5,4},{6,7},{7,6},{8,9},{9,8},{10,11... | collective-permute-start | bytes 196616 | tf_op jit(solution)/shard_map/ppermute | solution.py:352
  226.2 6.3 %collective-permute-start.22 = (bf16[128,512]{1,0:T(8,128)(2,1)S(1)}, bf16[128,512]{1,0:T(8,128)(2,1)S(1)}, u32[]{:S(2)}, u32[]{:S(2)}) collective-permute-start(bf16[128,512]{1,0:T(8,128)(2,1)S(1)} %pad_maximum_fusion.2), channel_id=1, source_target_pairs={{0,3},{1,2},{2,1},{3,0},{4,7},{5,6},{6,5},{7,4},{8,11},{9,10},{10,... | collective-permute-start | bytes 393224 | tf_op jit(solution)/shard_map/ppermute | solution.py:352
  233.1 13.1 %collective-permute-start.23 = (bf16[16,1024]{1,0:T(8,128)(2,1)S(1)}, bf16[16,1024]{1,0:T(8,128)(2,1)S(1)}, u32[]{:S(2)}, u32[]{:S(2)}) collective-permute-start(bf16[16,1024]{1,0:T(8,128)(2,1)S(1)} %get-tuple-element.49), channel_id=1, source_target_pairs={{0,8},{4,12},{8,16},{12,20},{16,24},{20,28},{24,32},{28,36},{32,40... | collective-permute-start | bytes 98312 | tf_op jit(solution)/shard_map/ppermute | solution.py:360
  234.3 14.3 %collective-permute-start.24 = (bf16[16,1024]{1,0:T(8,128)(2,1)S(1)}, bf16[16,1024]{1,0:T(8,128)(2,1)S(1)}, u32[]{:S(2)}, u32[]{:S(2)}) collective-permute-start(bf16[16,1024]{1,0:T(8,128)(2,1)S(1)} %get-tuple-element.48), channel_id=1, source_target_pairs={{0,16},{4,20},{8,24},{12,28},{16,32},{20,36},{24,40},{28,44},{32,4... | collective-permute-start | bytes 98312 | tf_op jit(solution)/shard_map/ppermute | solution.py:360
  241.2 11.1 %collective-permute-start.25 = (bf16[16,1024]{1,0:T(8,128)(2,1)S(1)}, bf16[16,1024]{1,0:T(8,128)(2,1)S(1)}, u32[]{:S(2)}, u32[]{:S(2)}) collective-permute-start(bf16[16,1024]{1,0:T(8,128)(2,1)S(1)} %get-tuple-element.47), channel_id=1, source_target_pairs={{0,24},{4,28},{8,32},{12,36},{16,40},{20,44},{24,48},{28,52},{32,5... | collective-permute-start | bytes 98312 | tf_op jit(solution)/shard_map/ppermute | solution.py:360
  241.2 11.1 %collective-permute-start.26 = (bf16[16,1024]{1,0:T(8,128)(2,1)S(1)}, bf16[16,1024]{1,0:T(8,128)(2,1)S(1)}, u32[]{:S(2)}, u32[]{:S(2)}) collective-permute-start(bf16[16,1024]{1,0:T(8,128)(2,1)S(1)} %get-tuple-element.46), channel_id=1, source_target_pairs={{0,32},{4,36},{8,40},{12,44},{16,48},{20,52},{24,56},{28,60},{32,0... | collective-permute-start | bytes 98312 | tf_op jit(solution)/shard_map/ppermute | solution.py:360
  243.7 8.6 %collective-permute-start.27 = (bf16[16,1024]{1,0:T(8,128)(2,1)S(1)}, bf16[16,1024]{1,0:T(8,128)(2,1)S(1)}, u32[]{:S(2)}, u32[]{:S(2)}) collective-permute-start(bf16[16,1024]{1,0:T(8,128)(2,1)S(1)} %get-tuple-element.45), channel_id=1, source_target_pairs={{0,40},{4,44},{8,48},{12,52},{16,56},{20,60},{24,0},{28,4},{32,8},... | collective-permute-start | bytes 98312 | tf_op jit(solution)/shard_map/ppermute | solution.py:360
  246.2 6.1 %collective-permute-start.28 = (bf16[16,1024]{1,0:T(8,128)(2,1)S(1)}, bf16[16,1024]{1,0:T(8,128)(2,1)S(1)}, u32[]{:S(2)}, u32[]{:S(2)}) collective-permute-start(bf16[16,1024]{1,0:T(8,128)(2,1)S(1)} %get-tuple-element.44), channel_id=1, source_target_pairs={{0,48},{4,52},{8,56},{12,60},{16,0},{20,4},{24,8},{28,12},{32,16},... | collective-permute-start | bytes 98312 | tf_op jit(solution)/shard_map/ppermute | solution.py:360
  248.6 4.3 %collective-permute-start.29 = (bf16[16,1024]{1,0:T(8,128)(2,1)S(1)}, bf16[16,1024]{1,0:T(8,128)(2,1)S(1)}, u32[]{:S(2)}, u32[]{:S(2)}) collective-permute-start(bf16[16,1024]{1,0:T(8,128)(2,1)S(1)} %get-tuple-element.43), channel_id=1, source_target_pairs={{0,56},{4,60},{8,0},{12,4},{16,8},{20,12},{24,16},{28,20},{32,24},... | collective-permute-start | bytes 98312 | tf_op jit(solution)/shard_map/ppermute | solution.py:360
  (22 other events, 214.3 us)

commit v5 on v4

--- a/solution.py
+++ b/solution.py
@@ -11,7 +11,7 @@
 HEAD_DIM = 128
 CL_DEV = 4
 UNIT = 256
-UNITS_A = 2
+UNITS_A = 3
 LANES = 128
 TAG_ROWS = 16
 big_negative = -1e30
@@ -98,7 +98,8 @@
         out_ref[:, m * UNIT : (m + 1) * UNIT] = nn(pick, ref[...]).astype(BF)
 
 
-def attend(scale, g_ref, tag_ref, w_ref, q_ref, k_ref, v_ref, ret_ref, att_ref, bias_ref):
+def attend(scale, g_ref, tag_ref, w_ref, q_ref, k_ref, v_ref, *refs):
+    ret_ref, att_ref, bias_ref = refs[-3:]
     rows = g_ref.shape[0]
 
     @pl.when(pl.program_id(0) == 0)
@@ -124,8 +125,11 @@
         ret_ref[:, m * HEAD_DIM : (m + 1) * HEAD_DIM] = part.astype(BF)
 
 
-def unpack(held, back_ref, ret_ref, *refs):
-    outs = refs[held:]
+def flip(in_ref, out_ref):
+    out_ref[...] = jnp.transpose(in_ref[...].astype(F32)).astype(BF)
+
+
+def unpack(back_ref, ret_ref, *outs):
     rows_out = nn(back_ref[...], ret_ref[...]).astype(BF)
     for h in range(UNIT // HEAD_DIM):
         for m, ref in enumerate(outs):
@@ -140,13 +144,11 @@
     for ref in ins[1:]:
         total = total + ref[...].astype(F32)
     total = total * factor
-    half = total.shape[1] // nx // 2
+    share = total.shape[1] // nx
     for s in range(nx):
         source = at_ref[0] ^ (s ^ (s >> 1))
-        for m in range(2):
-            cols = pl.ds(pl.multiple_of((m * nx + source) * half, half), half)
-            base = (2 * s + m) * half
-            out_ref[:, cols] = total[:, base : base + half]
+        cols = pl.ds(pl.multiple_of(source * share, share), share)
+        out_ref[:, cols] = total[:, s * share : (s + 1) * share]
 
 
 def cost(flops, nbytes, exps=0):
@@ -249,11 +251,10 @@
         name="pack_rest",
     )(pick, q, k, v)
     recv_b = exchange(send_b)
-    back = jnp.transpose(pick)
-
-    def attention(recv, first, unit0, n_units):
-        per = UNIT // HEAD_DIM
-
+
+    per = UNIT // HEAD_DIM
+
+    def attention(recv, first, unit0, n_units, made):
         def col(m):
             return pl.BlockSpec(
                 (rows, HEAD_DIM), lambda i: (0, per * (first + 3 * (i // per) + m) + i % per)
@@ -261,7 +262,7 @@
 
         return pl.pallas_call(
             lambda *refs: attend(scale, *refs),
-            out_shape=(sds((rows, 3 * UNIT * n_units)), sds((rows, UNIT * n_units))),
+            out_shape=(sds((rows, 3 * width)), sds((rows, width))),
             grid=(n_units * per,),
             in_specs=[
                 full((rows, width)),
@@ -270,12 +271,14 @@
                 col(0),
                 col(1),
                 col(2),
-            ],
+            ]
+            + [pl.BlockSpec(memory_space=pl.ANY)] * len(made),
             out_specs=(
-                pl.BlockSpec((rows, 3 * HEAD_DIM), lambda i: (0, i)),
-                pl.BlockSpec((rows, HEAD_DIM), lambda i: (0, i)),
+                pl.BlockSpec((rows, 3 * HEAD_DIM), lambda i: (0, i + unit0 * per)),
+                pl.BlockSpec((rows, HEAD_DIM), lambda i: (0, i + unit0 * per)),
             ),
             scratch_shapes=[pltpu.VMEM((rows, rows), F32)],
+            input_output_aliases={6 + m: m for m in range(len(made))},
             compiler_params=params(),
             cost_estimate=cost(
                 2 * rows * UNIT * n_units * (6 * rows + width),
@@ -283,60 +286,47 @@
                 rows * rows * n_units * UNIT // HEAD_DIM,
             ),
             name="attend",
-        )(recv_a, tag_line, w_out, recv, recv, recv)
-
-    ret_a, att_a = attention(recv_a, width // UNIT, 0, ua)
-    home_a = exchange(ret_a)
-    ret_b, att_b = attention(recv_b, 0, ua, ub)
-    home_b = exchange(ret_b)
-
-    out_sds = (sds((rows, width)),) * 3
+        )(recv_a, tag_line, w_out, recv, recv, recv, *made)
+
+    made = attention(recv_a, width // UNIT, 0, ua, ())
+    ret, att = attention(recv_b, 0, ua, ub, made)
+    home = exchange(ret)
+    turned = pl.pallas_call(
+        flip,
+        out_shape=sds((rows, rows)),
+        compiler_params=params(),
+        cost_estimate=cost(0, 4 * rows * rows),
+        name="flip",
+    )(pick)
     outs = pl.pallas_call(
-        lambda *refs: unpack(0, *refs),
-        out_shape=out_sds,
-        grid=(ua,),
+        unpack,
+        out_shape=(sds((rows, width)),) * 3,
+        grid=(units,),
         in_specs=[full((rows, rows)), pl.BlockSpec((rows, 3 * UNIT), lambda i: (0, i))],
         out_specs=(pl.BlockSpec((rows, UNIT), lambda i: (0, i)),) * 3,
         compiler_params=params(),
-        cost_estimate=cost(2 * rows * rows * 3 * UNIT * ua, 4 * rows * 3 * UNIT * ua),
-        name="unpack_a",
-    )(back, home_a)
-    outs = pl.pallas_call(
-        lambda *refs: unpack(3, *refs),
-        out_shape=out_sds,
-        grid=(ub,),
-        in_specs=[full((rows, rows)), pl.BlockSpec((rows, 3 * UNIT), lambda i: (0, i))]
-        + [pl.BlockSpec(memory_space=pl.ANY)] * 3,
-        out_specs=(pl.BlockSpec((rows, UNIT), lambda i: (0, i + ua)),) * 3,
-        input_output_aliases={2: 0, 3: 1, 4: 2},
-        compiler_params=params(),
-        cost_estimate=cost(2 * rows * rows * 3 * UNIT * ub, 4 * rows * 3 * UNIT * ub),
-        name="unpack_b",
-    )(back, home_b, *outs)
+        cost_estimate=cost(2 * rows * rows * 3 * width, 12 * rows * width),
+        name="unpack",
+    )(turned, home)
 
     share = width // nx
 
-    def reduced_over_chip_and_x(att):
-        part = att.shape[1] // nx
-        weight = tn(recv_a[:, :width], att)
-        weight = weight.reshape(ny * nz, nc, width // node_count, att.shape[1])
-        total = pick_of(weight, ic, 1)
-        for s in range(1, nc):
-            sent = pick_of(weight, (ic + s) % nc, 1).astype(BF)
-            total = total + lax.ppermute(sent, "nodes", hop(0, 0, s))
-        weight = total.reshape(width // nc, att.shape[1])
-        came = []
-        for s in range(1, nx):
-            sent = lax.dynamic_slice_in_dim(weight, ((ix + s) % nx) * part, part, 1).astype(BF)
-            came.append(lax.ppermute(sent, "rep", ring(nx, s)))
-        total = lax.dynamic_slice_in_dim(weight, ix * part, part, 1)
-        for piece in came:
-            total = total + piece
-        return lax.optimization_barrier(total)
-
-    total_a = reduced_over_chip_and_x(att_a)
-    att_b, total_a = lax.optimization_barrier((att_b, total_a))
-    weight = jnp.concatenate([total_a, reduced_over_chip_and_x(att_b)], axis=1)
+    weight = tn(recv_a[:, :width], att)
+    weight = weight.reshape(ny * nz, nc, width // node_count, width)
+    total = pick_of(weight, ic, 1)
+    for s in range(1, nc):
+        sent = pick_of(weight, (ic + s) % nc, 1).astype(BF)
+        came = lax.ppermute(sent, "nodes", hop(0, 0, s))
+        total = total + came
+    weight = total.reshape(width // nc, width)
+    came = []
+    for s in range(1, nx):
+        sent = lax.dynamic_slice_in_dim(weight, ((ix + s) % nx) * share, share, 1).astype(BF)
+        came.append(lax.ppermute(sent, "rep", ring(nx, s)))
+    total = lax.dynamic_slice_in_dim(weight, ix * share, share, 1)
+    for piece in came:
+        total = total + piece
+    weight = lax.optimization_barrier(total)
     weight = weight.reshape(ny, width // nc // ny, share)
     came = []
     for s in range(1, ny):

time: 265 us -> 254 us (0.958)
  starting transfers between devices: 95.6 us -> 78.2 us
  waiting for transfers between devices: 114 us -> 120 us
  other arithmetic: 2.51 us -> 5.7 us
    ppermute x8, waiting for transfers between devices: 16.4 us -> 1.97 us  [around(): lax.ppermute(line, 'nodes', hop(*step(s)))]
    ppermute x8 -> x4, waiting for transfers between devices: 8.48 us -> 16.2 us  [the longest x3 13.6 us: local(): came.append(lax.ppermute(sent, 'rep', ring(nx, s)))]
    ppermute x7, waiting for transfers between devices: 0.54 us -> 7.85 us  [local(): shares.append(lax.ppermute(sent, 'nodes', hop(0, s, 0)))]
    ppermute x8 -> x4, starting transfers between devices: 11.8 us -> 4.72 us  [the longest x3 4.52 us: local(): came.append(lax.ppermute(sent, 'rep', ring(nx, s)))]
    all_to_all x4 -> x3, starting transfers between devices: 36.2 us -> 29.5 us  [exchange(): lax.all_to_all(rows_in.reshape(node_count, bucket, c), 'nodes', split_axi...]
    ppermute x2, waiting for transfers between devices: 6.51 us -> 10.2 us  [local(): came = lax.ppermute(turn, 'rep', [(i, i ^ mask) for i in range(nx)])]
    ppermute x2, starting transfers between devices: 4.11 us -> 0.62 us  [local(): came = lax.ppermute(turn, 'rep', [(i, i ^ mask) for i in range(nx)])]
    all_to_all x4 -> x3, waiting for transfers between devices: 73.3 us -> 74.2 us  [exchange(): lax.all_to_all(rows_in.reshape(node_count, bucket, c), 'nodes', split_axi...]
  transfers between devices with their start and end apart: 34 -> 29, of which waited for: 16 -> 14; matrix products, arithmetic and copies ran while one was open for 4% -> 4% of each run, Pallas kernels for 12% -> 9%
where the time goes in v5:
time: 254 us; the launch traced here: 251 us
  waiting for transfers between devices  120 us (47%)
  starting transfers between devices  78.2 us (31%)
  Pallas kernels  40.5 us (16%)
  other arithmetic  5.7 us (2%)
  local copies, waits for them, and re-layouts  3.57 us (1%)
    all_to_all x3, waiting for transfers between devices, exchange(): lax.all_to_all(rows_in.reshape(node_count, bucket, c), 'nodes', split_axi...  74.2 us
    all_to_all x3, starting transfers between devices, exchange(): lax.all_to_all(rows_in.reshape(node_count, bucket, c), 'nodes', split_axi...  29.5 us
    pallas_call x2, Pallas kernels, attention(): pl.pallas_call(lambda *refs: attend(scale, *refs), out_shape=(sds((rows,...  20.5 us
    ppermute x7, starting transfers between devices, local(): shares.append(lax.ppermute(sent, 'nodes', hop(0, s, 0)))  18.2 us
    ppermute x8, starting transfers between devices, around(): lax.ppermute(line, 'nodes', hop(*step(s)))  16.1 us
    ppermute x3, waiting for transfers between devices, local(): came.append(lax.ppermute(sent, 'rep', ring(nx, s)))  13.6 us
    ppermute x2, waiting for transfers between devices, local(): came = lax.ppermute(turn, 'rep', [(i, i ^ mask) for i in range(nx)])  10.2 us
    ppermute x7, waiting for transfers between devices, local(): shares.append(lax.ppermute(sent, 'nodes', hop(0, s, 0)))  7.85 us
  transfers between devices with their start and end apart: 29, of which 14 were waited for; matrix products, arithmetic and copies ran while one was open for 4% of the time, Pallas kernels for 9%

profile of v5, /device:TPU:40, one launch (start us, length us, event | category | flops | bytes accessed | tf_op | source)
XLA Modules:
  0.0 251.1 jit_solution(3168502310363051281)
XLA Ops:
  0.6 6.4 %pack_first.1 = (bf16[512,3328]{1,0:T(8,128)(2,1)}, bf16[512,512]{1,0:T(8,128)(2,1)}, bf16[1,512]{1,0:T(2,128)(2,1)}) custom-call(s32[1,512]{1,0:T(1,128)} %refs_0_.1, bf16[512,1024]{1,0:T(8,128)(2,1)} %bitcast.70, bf16[512,1024]{1,0:T(8,128)(2,1)} %bitcast.63, bf16[512,1024]{1,0:T(8,128)(2,1)} %bitcast.65, bf16[512,1024]{1,0:T(8,128)(2,1)} %bitcast.67), custom_call_target="tpu_custom_call" | custom-call | flops 1744830464 | bytes 6815744 | tf_op jit(solution)/shard_map/pack_first/pallas_call | solution.py:197
  7.0 11.8 %all-to-all-start = ((bf16[64,8,3328]{2,1,0:T(8,128)(2,1)}), bf16[64,8,3328]{2,1,0:T(8,128)(2,1)}, u32[]{:S(2)}, u32[]{:S(2)}) async-start(bf16[64,8,3328]{2,1,0:T(8,128)(2,1)} %bitcast.59), calls=%async_computation | async-start | bytes 6815744 | tf_op jit(solution)/shard_map/all_to_all | solution.py:186
  18.8 2.7 %pack_rest.1 = bf16[512,768]{1,0:T(8,128)(2,1)} custom-call(bf16[512,512]{1,0:T(8,128)(2,1)} %get-tuple-element.14.in_ref.pick_ref, bf16[512,1024]{1,0:T(8,128)(2,1)} %bitcast.64, bf16[512,1024]{1,0:T(8,128)(2,1)} %bitcast.66, bf16[512,1024]{1,0:T(8,128)(2,1)} %bitcast.68), custom_call_target="tpu_custom_call" | custom-call | flops 402653184 | bytes 1572864 | tf_op jit(solution)/shard_map/pack_rest/pallas_call | solution.py:243
  21.6 74.2 %all-to-all-done = bf16[64,8,3328]{2,1,0:T(8,128)(2,1)} async-done(((bf16[64,8,3328]{2,1,0:T(8,128)(2,1)}), bf16[64,8,3328]{2,1,0:T(8,128)(2,1)}, u32[]{:S(2)}, u32[]{:S(2)}) %all-to-all-start) | async-done | bytes 3407904 | tf_op jit(solution)/shard_map/all_to_all | solution.py:186
  95.8 8.0 %all-to-all-start.1 = ((bf16[64,8,768]{2,1,0:T(8,128)(2,1)}), bf16[64,8,768]{2,1,0:T(8,128)(2,1)}, u32[]{:S(2)}, u32[]{:S(2)}) async-start(bf16[64,8,768]{2,1,0:T(8,128)(2,1)} %bitcast.60), calls=%async_computation.1 | async-start | bytes 1572864 | tf_op jit(solution)/shard_map/all_to_all | solution.py:186
  107.6 2.0 collective-permute-done.1
  110.3 2.4 collective-permute-start.2
  112.7 2.8 %collective-permute-done.2 = bf16[4,512]{1,0:T(4,128)(2,1)S(1)} collective-permute-done((bf16[4,512]{1,0:T(4,128)(2,1)S(1)}, bf16[4,512]{1,0:T(4,128)(2,1)S(1)}, u32[]{:S(2)}, u32[]{:S(2)}) %collective-permute-start.2) | collective-permute-done | bytes 4128 | tf_op jit(solution)/shard_map/ppermute | solution.py:230
  117.8 4.0 %collective-permute-start.4 = (bf16[8,512]{1,0:T(8,128)(2,1)S(1)}, bf16[8,512]{1,0:T(8,128)(2,1)S(1)}, u32[]{:S(2)}, u32[]{:S(2)}) collective-permute-start(bf16[8,512]{1,0:T(8,128)(2,1)S(1)} %pad_maximum_fusion.2.refs_1_), channel_id=1, source_target_pairs={{0,16},{4,20},{8,24},{12,28},{16,32},{20,36},{24,40},{28,44},{32,4... | collective-permute-start | bytes 24584 | tf_op jit(solution)/shard_map/ppermute | solution.py:225
  122.0 3.6 %collective-permute-start.6 = (bf16[8,512]{1,0:T(8,128)(2,1)S(1)}, bf16[8,512]{1,0:T(8,128)(2,1)S(1)}, u32[]{:S(2)}, u32[]{:S(2)}) collective-permute-start(bf16[8,512]{1,0:T(8,128)(2,1)S(1)} %pad_maximum_fusion.2.refs_1_), channel_id=1, source_target_pairs={{0,32},{4,36},{8,40},{12,44},{16,48},{20,52},{24,56},{28,60},{32,0... | collective-permute-start | bytes 24584 | tf_op jit(solution)/shard_map/ppermute | solution.py:225
  127.2 2.2 collective-permute-start.8
  129.4 2.7 %collective-permute-start.9 = (bf16[8,512]{1,0:T(8,128)(2,1)S(1)}, bf16[8,512]{1,0:T(8,128)(2,1)S(1)}, u32[]{:S(2)}, u32[]{:S(2)}) collective-permute-start(bf16[8,512]{1,0:T(8,128)(2,1)S(1)} %pad_maximum_fusion.2.refs_1_), channel_id=1, source_target_pairs={{0,56},{4,60},{8,0},{12,4},{16,8},{20,12},{24,16},{28,20},{32,24},... | collective-permute-start | bytes 24584 | tf_op jit(solution)/shard_map/ppermute | solution.py:225
  136.0 13.9 %attend.2 = (bf16[512,3072]{1,0:T(8,128)(2,1)}, bf16[512,1024]{1,0:T(8,128)(2,1)}) custom-call(bf16[512,3328]{1,0:T(8,128)(2,1)} %bitcast.5.refs_0_.refs_3_.refs_4_.refs_5_, f32[1,512]{1,0:T(1,128)} %tag_order.1.refs_1_, bf16[1024,1024]{1,0:T(8,128)(2,1)} %refs_2_.3, bf16[512,3328]{1,0:T(8,128)(2,1)} %bitcast.5.refs_0_.refs_3_.refs_4_.refs_5_, ...), custom_call_target="tpu_custom_call" | custom-call | flops 3221225472 | bytes 7602176 | tf_op jit(solution)/shard_map/attend/pallas_call | solution.py:263
  149.9 6.6 %attend.3 = (bf16[512,3072]{1,0:T(8,128)(2,1)}, bf16[512,1024]{1,0:T(8,128)(2,1)}) custom-call(bf16[512,3328]{1,0:T(8,128)(2,1)} %bitcast.5.refs_0_.refs_3_.refs_4_.refs_5_, f32[1,512]{1,0:T(1,128)} %tag_order.1.refs_1_, bf16[1024,1024]{1,0:T(8,128)(2,1)} %refs_2_.3, ...), custom_call_target="tpu_custom_call", output_to_operand_aliasing={{0}: (6, {}), {1}: (7, {})} | custom-call | flops 1073741824 | bytes 3932160 | tf_op jit(solution)/shard_map/attend/pallas_call | solution.py:263
  156.5 9.7 %all-to-all-start.2 = ((bf16[64,8,3072]{2,1,0:T(8,128)(2,1)}), bf16[64,8,3072]{2,1,0:T(8,128)(2,1)}, u32[]{:S(2)}, u32[]{:S(2)}) async-start(bf16[64,8,3072]{2,1,0:T(8,128)(2,1)} %bitcast.56), calls=%async_computation.2 | async-start | bytes 6291456 | tf_op jit(solution)/shard_map/all_to_all | solution.py:186
  166.3 2.5 %fusion.1 = f32[1024,1024]{1,0:T(8,128)S(1)} fusion(bf16[512,1024]{1,0:T(8,128)(2,1)S(1)} %copy-done.1, bf16[512,3328]{1,0:T(8,128)(2,1)} %bitcast.5.refs_0_.refs_3_.refs_4_.refs_5_), kind=kOutput, calls=%fused_computation.3 | convolution fusion | flops 1073741824 | bytes 6291456 | tf_op jit(solution)/shard_map/dot_general | solution.py:23
  168.8 2.0 copy-done
  171.1 2.5 %collective-permute-done.10 = bf16[32,16,1024]{2,1,0:T(8,128)(2,1)S(1)} collective-permute-done((bf16[32,16,1024]{2,1,0:T(8,128)(2,1)S(1)}, bf16[32,16,1024]{2,1,0:T(8,128)(2,1)S(1)}, u32[]{:S(2)}, u32[]{:S(2)}) %collective-permute-start.10) | collective-permute-done | bytes 1048608 | tf_op jit(solution)/shard_map/ppermute | solution.py:319
  175.7 2.8 %collective-permute-start.13 = (bf16[512,256]{1,0:T(8,128)(2,1)S(1)}, bf16[512,256]{1,0:T(8,128)(2,1)S(1)}, u32[]{:S(2)}, u32[]{:S(2)}) collective-permute-start(bf16[512,256]{1,0:T(8,128)(2,1)S(1)} %get-tuple-element.25), channel_id=1, source_target_pairs={{0,3},{1,0},{2,1},{3,2},{4,7},{5,4},{6,5},{7,6},{8,11},{9,8},{10,9... | collective-permute-start | bytes 786440 | tf_op jit(solution)/shard_map/ppermute | solution.py:325
  180.2 9.8 %collective-permute-done.13 = bf16[512,256]{1,0:T(8,128)(2,1)S(1)} collective-permute-done((bf16[512,256]{1,0:T(8,128)(2,1)S(1)}, bf16[512,256]{1,0:T(8,128)(2,1)S(1)}, u32[]{:S(2)}, u32[]{:S(2)}) %collective-permute-start.13) | collective-permute-done | bytes 262176 | tf_op jit(solution)/shard_map/ppermute | solution.py:325
  190.0 3.8 %collective-permute-done.11 = bf16[512,256]{1,0:T(8,128)(2,1)} collective-permute-done((bf16[512,256]{1,0:T(8,128)(2,1)S(1)}, bf16[512,256]{1,0:T(8,128)(2,1)}, u32[]{:S(2)}, u32[]{:S(2)}) %collective-permute-start.11) | collective-permute-done | bytes 262176 | tf_op jit(solution)/shard_map/ppermute | solution.py:325
  195.6 2.5 collective-permute-start.15
  201.3 3.1 %collective-permute-done.15 = bf16[128,256]{1,0:T(8,128)(2,1)S(1)} collective-permute-done((bf16[128,256]{1,0:T(8,128)(2,1)S(1)}, bf16[128,256]{1,0:T(8,128)(2,1)S(1)}, u32[]{:S(2)}, u32[]{:S(2)}) %collective-permute-start.15) | collective-permute-done | bytes 65568 | tf_op jit(solution)/shard_map/ppermute | solution.py:334
  204.6 4.3 %collective-permute-done.17 = bf16[128,256]{1,0:T(8,128)(2,1)S(1)} collective-permute-done((bf16[128,256]{1,0:T(8,128)(2,1)S(1)}, bf16[128,256]{1,0:T(8,128)(2,1)S(1)}, u32[]{:S(2)}, u32[]{:S(2)}) %collective-permute-start.17) | collective-permute-done | bytes 65568 | tf_op jit(solution)/shard_map/ppermute | solution.py:342
  209.4 6.0 %collective-permute-done.18 = bf16[128,512]{1,0:T(8,128)(2,1)S(1)} collective-permute-done((bf16[128,512]{1,0:T(8,128)(2,1)S(1)}, bf16[128,512]{1,0:T(8,128)(2,1)S(1)}, u32[]{:S(2)}, u32[]{:S(2)}) %collective-permute-start.18) | collective-permute-done | bytes 131104 | tf_op jit(solution)/shard_map/ppermute | solution.py:342
  217.5 4.7 %collective-permute-start.20 = (bf16[16,1024]{1,0:T(8,128)(2,1)S(1)}, bf16[16,1024]{1,0:T(8,128)(2,1)}, u32[]{:S(2)}, u32[]{:S(2)}) collective-permute-start(bf16[16,1024]{1,0:T(8,128)(2,1)S(1)} %get-tuple-element.35), channel_id=1, source_target_pairs={{0,16},{4,20},{8,24},{12,28},{16,32},{20,36},{24,40},{28,44},{32,4... | collective-permute-start | bytes 98312 | tf_op jit(solution)/shard_map/ppermute | solution.py:350
  222.4 3.7 %collective-permute-start.22 = (bf16[16,1024]{1,0:T(8,128)(2,1)}, bf16[16,1024]{1,0:T(8,128)(2,1)}, u32[]{:S(2)}, u32[]{:S(2)}) collective-permute-start(bf16[16,1024]{1,0:T(8,128)(2,1)} %get-tuple-element.33), channel_id=1, source_target_pairs={{0,32},{4,36},{8,40},{12,44},{16,48},{20,52},{24,56},{28,60},{32,0... | collective-permute-start | bytes 98312 | tf_op jit(solution)/shard_map/ppermute | solution.py:350
  227.9 7.8 %collective-permute-done.19.refs_2_ = bf16[16,1024]{1,0:T(8,128)(2,1)} collective-permute-done((bf16[16,1024]{1,0:T(8,128)(2,1)S(1)}, bf16[16,1024]{1,0:T(8,128)(2,1)}, u32[]{:S(2)}, u32[]{:S(2)}) %collective-permute-start.19) | collective-permute-done | bytes 32800 | tf_op jit(solution)/shard_map/ppermute | solution.py:350
  235.7 4.2 %collective-permute-start.24 = (bf16[16,1024]{1,0:T(8,128)(2,1)}, bf16[16,1024]{1,0:T(8,128)(2,1)}, u32[]{:S(2)}, u32[]{:S(2)}) collective-permute-start(bf16[16,1024]{1,0:T(8,128)(2,1)} %get-tuple-element.31), channel_id=1, source_target_pairs={{0,48},{4,52},{8,56},{12,60},{16,0},{20,4},{24,8},{28,12},{32,16},... | collective-permute-start | bytes 98312 | tf_op jit(solution)/shard_map/ppermute | solution.py:350
  240.0 2.1 collective-permute-start.25
  242.1 2.0 flip.1.back_ref
  245.7 5.4 %unpack.1 = (bf16[512,1024]{1,0:T(8,128)(2,1)}, bf16[512,1024]{1,0:T(8,128)(2,1)}, bf16[512,1024]{1,0:T(8,128)(2,1)}) custom-call(bf16[512,512]{1,0:T(8,128)(2,1)} %flip.1.back_ref, bf16[512,3072]{1,0:T(8,128)(2,1)} %bitcast.12.ret_ref), custom_call_target="tpu_custom_call" | custom-call | flops 1610612736 | bytes 6291456 | tf_op jit(solution)/shard_map/unpack/pallas_call | solution.py:301
  (68 shorter events, 27.9 us)
Async XLA Ops:
  7.0 88.8 %all-to-all-start = ((bf16[64,8,3328]{2,1,0:T(8,128)(2,1)}), bf16[64,8,3328]{2,1,0:T(8,128)(2,1)}, u32[]{:S(2)}, u32[]{:S(2)}) async-start(bf16[64,8,3328]{2,1,0:T(8,128)(2,1)} %bitcast.59), calls=%async_computation | async-start | bytes 6815744 | tf_op jit(solution)/shard_map/all_to_all | solution.py:186
  95.8 54.1 %all-to-all-start.1 = ((bf16[64,8,768]{2,1,0:T(8,128)(2,1)}), bf16[64,8,768]{2,1,0:T(8,128)(2,1)}, u32[]{:S(2)}, u32[]{:S(2)}) async-start(bf16[64,8,768]{2,1,0:T(8,128)(2,1)} %bitcast.60), calls=%async_computation.1 | async-start | bytes 1572864 | tf_op jit(solution)/shard_map/all_to_all | solution.py:186
  103.8 1.5 collective-permute-start
  105.9 3.7 %collective-permute-start.1 = (bf16[2,512]{1,0:T(2,128)(2,1)S(1)}, bf16[2,512]{1,0:T(2,128)(2,1)S(1)}, u32[]{:S(2)}, u32[]{:S(2)}) collective-permute-start(bf16[2,512]{1,0:T(2,128)(2,1)S(1)} %pad_maximum_fusion.4), channel_id=1, source_target_pairs={{0,64},{4,68},{8,72},{12,76},{16,80},{20,84},{24,88},{28,92},{32,9... | collective-permute-start | bytes 6152 | tf_op jit(solution)/shard_map/ppermute | solution.py:230
  110.3 5.2 %collective-permute-start.2 = (bf16[4,512]{1,0:T(4,128)(2,1)S(1)}, bf16[4,512]{1,0:T(4,128)(2,1)S(1)}, u32[]{:S(2)}, u32[]{:S(2)}) collective-permute-start(bf16[4,512]{1,0:T(4,128)(2,1)S(1)} %pad_maximum_fusion.3), channel_id=1, source_target_pairs={{0,128},{4,132},{8,136},{12,140},{16,144},{20,148},{24,152},{28,15... | collective-permute-start | bytes 12296 | tf_op jit(solution)/shard_map/ppermute | solution.py:230
  116.2 17.3 %copy-start.2 = (bf16[8,512]{1,0:T(8,128)(2,1)}, bf16[8,512]{1,0:T(8,128)(2,1)S(1)}, u32[]{:S(2)}) copy-start(bf16[8,512]{1,0:T(8,128)(2,1)S(1)} %pad_maximum_fusion.2.refs_1_) | copy-start | bytes 24580
  116.2 11.0 %collective-permute-start.3 = (bf16[8,512]{1,0:T(8,128)(2,1)S(1)}, bf16[8,512]{1,0:T(8,128)(2,1)S(1)}, u32[]{:S(2)}, u32[]{:S(2)}) collective-permute-start(bf16[8,512]{1,0:T(8,128)(2,1)S(1)} %pad_maximum_fusion.2.refs_1_), channel_id=1, source_target_pairs={{0,8},{4,12},{8,16},{12,20},{16,24},{20,28},{24,32},{28,36},{32,40... | collective-permute-start | bytes 24584 | tf_op jit(solution)/shard_map/ppermute | solution.py:225
  117.8 11.6 %collective-permute-start.4 = (bf16[8,512]{1,0:T(8,128)(2,1)S(1)}, bf16[8,512]{1,0:T(8,128)(2,1)S(1)}, u32[]{:S(2)}, u32[]{:S(2)}) collective-permute-start(bf16[8,512]{1,0:T(8,128)(2,1)S(1)} %pad_maximum_fusion.2.refs_1_), channel_id=1, source_target_pairs={{0,16},{4,20},{8,24},{12,28},{16,32},{20,36},{24,40},{28,44},{32,4... | collective-permute-start | bytes 24584 | tf_op jit(solution)/shard_map/ppermute | solution.py:225
  121.8 10.9 %collective-permute-start.5 = (bf16[8,512]{1,0:T(8,128)(2,1)S(1)}, bf16[8,512]{1,0:T(8,128)(2,1)S(1)}, u32[]{:S(2)}, u32[]{:S(2)}) collective-permute-start(bf16[8,512]{1,0:T(8,128)(2,1)S(1)} %pad_maximum_fusion.2.refs_1_), channel_id=1, source_target_pairs={{0,24},{4,28},{8,32},{12,36},{16,40},{20,44},{24,48},{28,52},{32,5... | collective-permute-start | bytes 24584 | tf_op jit(solution)/shard_map/ppermute | solution.py:225
  122.0 10.7 %collective-permute-start.6 = (bf16[8,512]{1,0:T(8,128)(2,1)S(1)}, bf16[8,512]{1,0:T(8,128)(2,1)S(1)}, u32[]{:S(2)}, u32[]{:S(2)}) collective-permute-start(bf16[8,512]{1,0:T(8,128)(2,1)S(1)} %pad_maximum_fusion.2.refs_1_), channel_id=1, source_target_pairs={{0,32},{4,36},{8,40},{12,44},{16,48},{20,52},{24,56},{28,60},{32,0... | collective-permute-start | bytes 24584 | tf_op jit(solution)/shard_map/ppermute | solution.py:225
  125.6 7.1 %collective-permute-start.7 = (bf16[8,512]{1,0:T(8,128)(2,1)S(1)}, bf16[8,512]{1,0:T(8,128)(2,1)S(1)}, u32[]{:S(2)}, u32[]{:S(2)}) collective-permute-start(bf16[8,512]{1,0:T(8,128)(2,1)S(1)} %pad_maximum_fusion.2.refs_1_), channel_id=1, source_target_pairs={{0,40},{4,44},{8,48},{12,52},{16,56},{20,60},{24,0},{28,4},{32,8},... | collective-permute-start | bytes 24584 | tf_op jit(solution)/shard_map/ppermute | solution.py:225
  127.2 6.3 %copy-start.3 = (bf16[8,512]{1,0:T(8,128)(2,1)}, bf16[8,512]{1,0:T(8,128)(2,1)S(1)}, u32[]{:S(2)}) copy-start(bf16[8,512]{1,0:T(8,128)(2,1)S(1)} %collective-permute-done.3.refs_2_) | copy-start | bytes 24580
  127.2 5.6 %collective-permute-start.8 = (bf16[8,512]{1,0:T(8,128)(2,1)S(1)}, bf16[8,512]{1,0:T(8,128)(2,1)S(1)}, u32[]{:S(2)}, u32[]{:S(2)}) collective-permute-start(bf16[8,512]{1,0:T(8,128)(2,1)S(1)} %pad_maximum_fusion.2.refs_1_), channel_id=1, source_target_pairs={{0,48},{4,52},{8,56},{12,60},{16,0},{20,4},{24,8},{28,12},{32,16},... | collective-permute-start | bytes 24584 | tf_op jit(solution)/shard_map/ppermute | solution.py:225
  129.4 4.0 %collective-permute-start.9 = (bf16[8,512]{1,0:T(8,128)(2,1)S(1)}, bf16[8,512]{1,0:T(8,128)(2,1)S(1)}, u32[]{:S(2)}, u32[]{:S(2)}) collective-permute-start(bf16[8,512]{1,0:T(8,128)(2,1)S(1)} %pad_maximum_fusion.2.refs_1_), channel_id=1, source_target_pairs={{0,56},{4,60},{8,0},{12,4},{16,8},{20,12},{24,16},{28,20},{32,24},... | collective-permute-start | bytes 24584 | tf_op jit(solution)/shard_map/ppermute | solution.py:225
  156.5 9.8 %copy-start.1 = (bf16[512,1024]{1,0:T(8,128)(2,1)S(1)}, bf16[512,1024]{1,0:T(8,128)(2,1)}, u32[]{:S(2)}) copy-start(bf16[512,1024]{1,0:T(8,128)(2,1)} %get-tuple-element.23) | copy-start | bytes 3145732
  156.5 89.2 %all-to-all-start.2 = ((bf16[64,8,3072]{2,1,0:T(8,128)(2,1)}), bf16[64,8,3072]{2,1,0:T(8,128)(2,1)}, u32[]{:S(2)}, u32[]{:S(2)}) async-start(bf16[64,8,3072]{2,1,0:T(8,128)(2,1)} %bitcast.56), calls=%async_computation.2 | async-start | bytes 6291456 | tf_op jit(solution)/shard_map/all_to_all | solution.py:186
  170.9 2.7 %collective-permute-start.10 = (bf16[32,16,1024]{2,1,0:T(8,128)(2,1)S(1)}, bf16[32,16,1024]{2,1,0:T(8,128)(2,1)S(1)}, u32[]{:S(2)}, u32[]{:S(2)}) collective-permute-start(bf16[32,16,1024]{2,1,0:T(8,128)(2,1)S(1)} %fusion), channel_id=1, source_target_pairs={{0,4},{4,0},{8,12},{12,8},{16,20},{20,16},{24,28},{28,24},{32,36},... | collective-permute-start | bytes 3145736 | tf_op jit(solution)/shard_map/ppermute | solution.py:319
  175.7 14.4 %collective-permute-start.13 = (bf16[512,256]{1,0:T(8,128)(2,1)S(1)}, bf16[512,256]{1,0:T(8,128)(2,1)S(1)}, u32[]{:S(2)}, u32[]{:S(2)}) collective-permute-start(bf16[512,256]{1,0:T(8,128)(2,1)S(1)} %get-tuple-element.25), channel_id=1, source_target_pairs={{0,3},{1,0},{2,1},{3,2},{4,7},{5,4},{6,5},{7,6},{8,11},{9,8},{10,9... | collective-permute-start | bytes 786440 | tf_op jit(solution)/shard_map/ppermute | solution.py:325
  178.5 11.5 %collective-permute-start.12 = (bf16[512,256]{1,0:T(8,128)(2,1)S(1)}, bf16[512,256]{1,0:T(8,128)(2,1)S(1)}, u32[]{:S(2)}, u32[]{:S(2)}) collective-permute-start(bf16[512,256]{1,0:T(8,128)(2,1)S(1)} %get-tuple-element.26), channel_id=1, source_target_pairs={{0,2},{1,3},{2,0},{3,1},{4,6},{5,7},{6,4},{7,5},{8,10},{9,11},{10,... | collective-permute-start | bytes 786440 | tf_op jit(solution)/shard_map/ppermute | solution.py:325
  179.3 14.5 %collective-permute-start.11 = (bf16[512,256]{1,0:T(8,128)(2,1)S(1)}, bf16[512,256]{1,0:T(8,128)(2,1)}, u32[]{:S(2)}, u32[]{:S(2)}) collective-permute-start(bf16[512,256]{1,0:T(8,128)(2,1)S(1)} %get-tuple-element.24), channel_id=1, source_target_pairs={{0,1},{1,2},{2,3},{3,0},{4,5},{5,6},{6,7},{7,4},{8,9},{9,10},{10,1... | collective-permute-start | bytes 786440 | tf_op jit(solution)/shard_map/ppermute | solution.py:325
  194.9 6.4 %collective-permute-start.16 = (bf16[128,256]{1,0:T(8,128)(2,1)S(1)}, bf16[128,256]{1,0:T(8,128)(2,1)S(1)}, u32[]{:S(2)}, u32[]{:S(2)}) collective-permute-start(bf16[128,256]{1,0:T(8,128)(2,1)S(1)} %get-tuple-element.28), channel_id=1, source_target_pairs={{0,192},{4,196},{8,200},{12,204},{16,208},{20,212},{24,216},{28,22... | collective-permute-start | bytes 196616 | tf_op jit(solution)/shard_map/ppermute | solution.py:334
  195.6 8.9 %collective-permute-start.15 = (bf16[128,256]{1,0:T(8,128)(2,1)S(1)}, bf16[128,256]{1,0:T(8,128)(2,1)S(1)}, u32[]{:S(2)}, u32[]{:S(2)}) collective-permute-start(bf16[128,256]{1,0:T(8,128)(2,1)S(1)} %get-tuple-element.29), channel_id=1, source_target_pairs={{0,128},{4,132},{8,136},{12,140},{16,144},{20,148},{24,152},{28,15... | collective-permute-start | bytes 196616 | tf_op jit(solution)/shard_map/ppermute | solution.py:334
  198.0 6.4 %collective-permute-start.14 = (bf16[128,256]{1,0:T(8,128)(2,1)S(1)}, bf16[128,256]{1,0:T(8,128)(2,1)S(1)}, u32[]{:S(2)}, u32[]{:S(2)}) collective-permute-start(bf16[128,256]{1,0:T(8,128)(2,1)S(1)} %get-tuple-element.27), channel_id=1, source_target_pairs={{0,64},{4,68},{8,72},{12,76},{16,80},{20,84},{24,88},{28,92},{32,9... | collective-permute-start | bytes 196616 | tf_op jit(solution)/shard_map/ppermute | solution.py:334
  204.5 4.4 %collective-permute-start.17 = (bf16[128,256]{1,0:T(8,128)(2,1)S(1)}, bf16[128,256]{1,0:T(8,128)(2,1)S(1)}, u32[]{:S(2)}, u32[]{:S(2)}) collective-permute-start(bf16[128,256]{1,0:T(8,128)(2,1)S(1)} %fusion.4), channel_id=1, source_target_pairs={{0,1},{1,0},{2,3},{3,2},{4,5},{5,4},{6,7},{7,6},{8,9},{9,8},{10,11... | collective-permute-start | bytes 196616 | tf_op jit(solution)/shard_map/ppermute | solution.py:342
  208.8 6.5 %collective-permute-start.18 = (bf16[128,512]{1,0:T(8,128)(2,1)S(1)}, bf16[128,512]{1,0:T(8,128)(2,1)S(1)}, u32[]{:S(2)}, u32[]{:S(2)}) collective-permute-start(bf16[128,512]{1,0:T(8,128)(2,1)S(1)} %pad_maximum_fusion.1), channel_id=1, source_target_pairs={{0,3},{1,2},{2,1},{3,0},{4,7},{5,6},{6,5},{7,4},{8,11},{9,10},{10,... | collective-permute-start | bytes 393224 | tf_op jit(solution)/shard_map/ppermute | solution.py:342
  216.0 19.7 %collective-permute-start.19 = (bf16[16,1024]{1,0:T(8,128)(2,1)S(1)}, bf16[16,1024]{1,0:T(8,128)(2,1)}, u32[]{:S(2)}, u32[]{:S(2)}) collective-permute-start(bf16[16,1024]{1,0:T(8,128)(2,1)S(1)} %get-tuple-element.36), channel_id=1, source_target_pairs={{0,8},{4,12},{8,16},{12,20},{16,24},{20,28},{24,32},{28,36},{32,40... | collective-permute-start | bytes 98312 | tf_op jit(solution)/shard_map/ppermute | solution.py:350
  217.5 22.5 %collective-permute-start.20 = (bf16[16,1024]{1,0:T(8,128)(2,1)S(1)}, bf16[16,1024]{1,0:T(8,128)(2,1)}, u32[]{:S(2)}, u32[]{:S(2)}) collective-permute-start(bf16[16,1024]{1,0:T(8,128)(2,1)S(1)} %get-tuple-element.35), channel_id=1, source_target_pairs={{0,16},{4,20},{8,24},{12,28},{16,32},{20,36},{24,40},{28,44},{32,4... | collective-permute-start | bytes 98312 | tf_op jit(solution)/shard_map/ppermute | solution.py:350
  222.2 21.9 %collective-permute-start.21 = (bf16[16,1024]{1,0:T(8,128)(2,1)}, bf16[16,1024]{1,0:T(8,128)(2,1)}, u32[]{:S(2)}, u32[]{:S(2)}) collective-permute-start(bf16[16,1024]{1,0:T(8,128)(2,1)} %get-tuple-element.34), channel_id=1, source_target_pairs={{0,24},{4,28},{8,32},{12,36},{16,40},{20,44},{24,48},{28,52},{32,5... | collective-permute-start | bytes 98312 | tf_op jit(solution)/shard_map/ppermute | solution.py:350
  222.4 21.7 %collective-permute-start.22 = (bf16[16,1024]{1,0:T(8,128)(2,1)}, bf16[16,1024]{1,0:T(8,128)(2,1)}, u32[]{:S(2)}, u32[]{:S(2)}) collective-permute-start(bf16[16,1024]{1,0:T(8,128)(2,1)} %get-tuple-element.33), channel_id=1, source_target_pairs={{0,32},{4,36},{8,40},{12,44},{16,48},{20,52},{24,56},{28,60},{32,0... | collective-permute-start | bytes 98312 | tf_op jit(solution)/shard_map/ppermute | solution.py:350
  226.2 18.0 %collective-permute-start.23 = (bf16[16,1024]{1,0:T(8,128)(2,1)}, bf16[16,1024]{1,0:T(8,128)(2,1)}, u32[]{:S(2)}, u32[]{:S(2)}) collective-permute-start(bf16[16,1024]{1,0:T(8,128)(2,1)} %get-tuple-element.32), channel_id=1, source_target_pairs={{0,40},{4,44},{8,48},{12,52},{16,56},{20,60},{24,0},{28,4},{32,8},... | collective-permute-start | bytes 98312 | tf_op jit(solution)/shard_map/ppermute | solution.py:350
  235.7 8.4 %collective-permute-start.24 = (bf16[16,1024]{1,0:T(8,128)(2,1)}, bf16[16,1024]{1,0:T(8,128)(2,1)}, u32[]{:S(2)}, u32[]{:S(2)}) collective-permute-start(bf16[16,1024]{1,0:T(8,128)(2,1)} %get-tuple-element.31), channel_id=1, source_target_pairs={{0,48},{4,52},{8,56},{12,60},{16,0},{20,4},{24,8},{28,12},{32,16},... | collective-permute-start | bytes 98312 | tf_op jit(solution)/shard_map/ppermute | solution.py:350
  240.0 4.2 %collective-permute-start.25 = (bf16[16,1024]{1,0:T(8,128)(2,1)}, bf16[16,1024]{1,0:T(8,128)(2,1)}, u32[]{:S(2)}, u32[]{:S(2)}) collective-permute-start(bf16[16,1024]{1,0:T(8,128)(2,1)} %get-tuple-element.30), channel_id=1, source_target_pairs={{0,56},{4,60},{8,0},{12,4},{16,8},{20,12},{24,16},{28,20},{32,24},... | collective-permute-start | bytes 98312 | tf_op jit(solution)/shard_map/ppermute | solution.py:350
  (7 other events, 9.6 us)

commit v6 on v5

--- a/solution.py
+++ b/solution.py
@@ -98,9 +98,9 @@
         out_ref[:, m * UNIT : (m + 1) * UNIT] = nn(pick, ref[...]).astype(BF)
 
 
-def attend(scale, g_ref, tag_ref, w_ref, q_ref, k_ref, v_ref, *refs):
+def attend(scale, tag_ref, grad_ref, q_ref, k_ref, v_ref, *refs):
     ret_ref, att_ref, bias_ref = refs[-3:]
-    rows = g_ref.shape[0]
+    rows = q_ref.shape[0]
 
     @pl.when(pl.program_id(0) == 0)
     def _():
@@ -111,18 +111,20 @@
             cols = pl.ds(pl.multiple_of(j * LANES, LANES), LANES)
             bias_ref[:, cols] = jnp.where(tags == tag_ref[:, cols], 0.0, big_negative)
 
-    q, k, v = q_ref[...], k_ref[...], v_ref[...]
-    grad = nn(g_ref[...], w_ref[...]).astype(BF)
-    scores = nt(q, k) * scale + bias_ref[...]
-    weights = jnp.exp(scores - jnp.max(scores, axis=1, keepdims=True))
-    probs = weights * (1.0 / jnp.sum(weights, axis=1, keepdims=True))
-    low = probs.astype(BF)
-    attended = nn(low, v).astype(BF)
-    delta = jnp.sum(grad.astype(F32) * attended.astype(F32), axis=1, keepdims=True)
-    grad_scores = (probs * (nt(grad, v) - delta) * scale).astype(BF)
-    att_ref[...] = attended
-    for m, part in enumerate((nn(grad_scores, k), tn(grad_scores, q), tn(low, grad))):
-        ret_ref[:, m * HEAD_DIM : (m + 1) * HEAD_DIM] = part.astype(BF)
+    for h in range(UNIT // HEAD_DIM):
+        cols = slice(h * HEAD_DIM, (h + 1) * HEAD_DIM)
+        q, k, v, grad = q_ref[:, cols], k_ref[:, cols], v_ref[:, cols], grad_ref[:, cols]
+        scores = nt(q, k) * scale + bias_ref[...]
+        weights = jnp.exp(scores - jnp.max(scores, axis=1, keepdims=True))
+        probs = weights * (1.0 / jnp.sum(weights, axis=1, keepdims=True))
+        low = probs.astype(BF)
+        attended = nn(low, v).astype(BF)
+        delta = jnp.sum(grad.astype(F32) * attended.astype(F32), axis=1, keepdims=True)
+        grad_scores = (probs * (nt(grad, v) - delta) * scale).astype(BF)
+        att_ref[:, cols] = attended
+        for m, part in enumerate((nn(grad_scores, k), tn(grad_scores, q), tn(low, grad))):
+            base = m * UNIT + h * HEAD_DIM
+            ret_ref[:, base : base + HEAD_DIM] = part.astype(BF)
 
 
 def flip(in_ref, out_ref):
@@ -130,12 +132,8 @@
 
 
 def unpack(back_ref, ret_ref, *outs):
-    rows_out = nn(back_ref[...], ret_ref[...]).astype(BF)
-    for h in range(UNIT // HEAD_DIM):
-        for m, ref in enumerate(outs):
-            cols = slice(h * HEAD_DIM, (h + 1) * HEAD_DIM)
-            base = (h * len(outs) + m) * HEAD_DIM
-            ref[:, cols] = rows_out[:, base : base + HEAD_DIM]
+    for m, ref in enumerate(outs):
+        ref[...] = nn(back_ref[...], ret_ref[:, m * UNIT : (m + 1) * UNIT]).astype(BF)
 
 
 def finish(factor, nx, at_ref, *refs):
@@ -252,41 +250,38 @@
     )(pick, q, k, v)
     recv_b = exchange(send_b)
 
-    per = UNIT // HEAD_DIM
+    grad_attended = nn(recv_a[:, :width], w_out).astype(BF)
 
     def attention(recv, first, unit0, n_units, made):
         def col(m):
-            return pl.BlockSpec(
-                (rows, HEAD_DIM), lambda i: (0, per * (first + 3 * (i // per) + m) + i % per)
-            )
+            return pl.BlockSpec((rows, UNIT), lambda i: (0, first + 3 * i + m))
 
         return pl.pallas_call(
             lambda *refs: attend(scale, *refs),
             out_shape=(sds((rows, 3 * width)), sds((rows, width))),
-            grid=(n_units * per,),
+            grid=(n_units,),
             in_specs=[
-                full((rows, width)),
                 full((1, rows)),
-                pl.BlockSpec((width, HEAD_DIM), lambda i: (0, i + unit0 * per)),
+                pl.BlockSpec((rows, UNIT), lambda i: (0, i + unit0)),
                 col(0),
                 col(1),
                 col(2),
             ]
             + [pl.BlockSpec(memory_space=pl.ANY)] * len(made),
             out_specs=(
-                pl.BlockSpec((rows, 3 * HEAD_DIM), lambda i: (0, i + unit0 * per)),
-                pl.BlockSpec((rows, HEAD_DIM), lambda i: (0, i + unit0 * per)),
+                pl.BlockSpec((rows, 3 * UNIT), lambda i: (0, i + unit0)),
+                pl.BlockSpec((rows, UNIT), lambda i: (0, i + unit0)),
             ),
             scratch_shapes=[pltpu.VMEM((rows, rows), F32)],
-            input_output_aliases={6 + m: m for m in range(len(made))},
+            input_output_aliases={5 + m: m for m in range(len(made))},
             compiler_params=params(),
             cost_estimate=cost(
-                2 * rows * UNIT * n_units * (6 * rows + width),
-                2 * rows * UNIT * n_units * 7 + 4 * rows * width,
+                2 * rows * UNIT * n_units * 6 * rows,
+                2 * rows * UNIT * n_units * 8,
                 rows * rows * n_units * UNIT // HEAD_DIM,
             ),
             name="attend",
-        )(recv_a, tag_line, w_out, recv, recv, recv, *made)
+        )(tag_line, grad_attended, recv, recv, recv, *made)
 
     made = attention(recv_a, width // UNIT, 0, ua, ())
     ret, att = attention(recv_b, 0, ua, ub, made)

time: 254 us -> 255 us (level)
  matrix products: 2.51 us -> 6.66 us
  Pallas kernels: 40.5 us -> 37.4 us
    dot_general x1 -> x2, matrix products: 2.51 us -> 6.66 us  [mm(): return lax.dot_general(a, b, (dims, ((), ())), preferred_element_type=F32)]
    pallas_call x2, Pallas kernels: 20.5 us -> 17.5 us  [attention(): pl.pallas_call(lambda *refs: attend(scale, *refs), out_shape=(sds((rows,...]
  transfers between devices with their start and end apart: 29 -> 29, of which waited for: 14 -> 14; matrix products, arithmetic and copies ran while one was open for 4% -> 5% of each run, Pallas kernels for 9% -> 8%
where the time goes in v6:
time: 255 us; the launch traced here: 252 us
  waiting for transfers between devices  120 us (47%)
  starting transfers between devices  78 us (31%)
  Pallas kernels  37.4 us (15%)
  matrix products  6.66 us (3%)
  other arithmetic  5.7 us (2%)
  local copies, waits for them, and re-layouts  3.57 us (1%)
    all_to_all x3, waiting for transfers between devices, exchange(): lax.all_to_all(rows_in.reshape(node_count, bucket, c), 'nodes', split_axi...  74.2 us
    all_to_all x3, starting transfers between devices, exchange(): lax.all_to_all(rows_in.reshape(node_count, bucket, c), 'nodes', split_axi...  29.5 us
    ppermute x7, starting transfers between devices, local(): shares.append(lax.ppermute(sent, 'nodes', hop(0, s, 0)))  18.2 us
    pallas_call x2, Pallas kernels, attention(): pl.pallas_call(lambda *refs: attend(scale, *refs), out_shape=(sds((rows,...  17.5 us
    ppermute x8, starting transfers between devices, around(): lax.ppermute(line, 'nodes', hop(*step(s)))  16.1 us
    ppermute x3, waiting for transfers between devices, local(): came.append(lax.ppermute(sent, 'rep', ring(nx, s)))  13.6 us
    ppermute x2, waiting for transfers between devices, local(): came = lax.ppermute(turn, 'rep', [(i, i ^ mask) for i in range(nx)])  10.2 us
    ppermute x7, waiting for transfers between devices, local(): shares.append(lax.ppermute(sent, 'nodes', hop(0, s, 0)))  8.07 us
  transfers between devices with their start and end apart: 29, of which 14 were waited for; matrix products, arithmetic and copies ran while one was open for 5% of the time, Pallas kernels for 8%

profile of v6, /device:TPU:40, one launch (start us, length us, event | category | flops | bytes accessed | tf_op | source)
XLA Modules:
  0.0 252.1 jit_solution(7242186035092753416)
XLA Ops:
  0.6 6.4 %pack_first.1 = (bf16[512,3328]{1,0:T(8,128)(2,1)}, bf16[512,512]{1,0:T(8,128)(2,1)}, bf16[1,512]{1,0:T(2,128)(2,1)}) custom-call(s32[1,512]{1,0:T(1,128)} %refs_0_.1, bf16[512,1024]{1,0:T(8,128)(2,1)} %bitcast.71, bf16[512,1024]{1,0:T(8,128)(2,1)} %bitcast.64, bf16[512,1024]{1,0:T(8,128)(2,1)} %bitcast.66, bf16[512,1024]{1,0:T(8,128)(2,1)} %bitcast.68), custom_call_target="tpu_custom_call" | custom-call | flops 1744830464 | bytes 6815744 | tf_op jit(solution)/shard_map/pack_first/pallas_call | solution.py:195
  7.0 11.8 %all-to-all-start = ((bf16[64,8,3328]{2,1,0:T(8,128)(2,1)}), bf16[64,8,3328]{2,1,0:T(8,128)(2,1)}, u32[]{:S(2)}, u32[]{:S(2)}) async-start(bf16[64,8,3328]{2,1,0:T(8,128)(2,1)} %bitcast.60), calls=%async_computation | async-start | bytes 6815744 | tf_op jit(solution)/shard_map/all_to_all | solution.py:184
  18.8 2.7 %pack_rest.1 = bf16[512,768]{1,0:T(8,128)(2,1)} custom-call(bf16[512,512]{1,0:T(8,128)(2,1)} %get-tuple-element.14.in_ref.pick_ref, bf16[512,1024]{1,0:T(8,128)(2,1)} %bitcast.65, bf16[512,1024]{1,0:T(8,128)(2,1)} %bitcast.67, bf16[512,1024]{1,0:T(8,128)(2,1)} %bitcast.69), custom_call_target="tpu_custom_call" | custom-call | flops 402653184 | bytes 1572864 | tf_op jit(solution)/shard_map/pack_rest/pallas_call | solution.py:241
  21.6 74.2 %all-to-all-done = bf16[64,8,3328]{2,1,0:T(8,128)(2,1)} async-done(((bf16[64,8,3328]{2,1,0:T(8,128)(2,1)}), bf16[64,8,3328]{2,1,0:T(8,128)(2,1)}, u32[]{:S(2)}, u32[]{:S(2)}) %all-to-all-start) | async-done | bytes 3407904 | tf_op jit(solution)/shard_map/all_to_all | solution.py:184
  95.8 8.0 %all-to-all-start.1 = ((bf16[64,8,768]{2,1,0:T(8,128)(2,1)}), bf16[64,8,768]{2,1,0:T(8,128)(2,1)}, u32[]{:S(2)}, u32[]{:S(2)}) async-start(bf16[64,8,768]{2,1,0:T(8,128)(2,1)} %bitcast.61), calls=%async_computation.1 | async-start | bytes 1572864 | tf_op jit(solution)/shard_map/all_to_all | solution.py:184
  107.6 2.0 collective-permute-done.1
  110.3 2.4 collective-permute-start.2
  112.7 2.8 %collective-permute-done.2 = bf16[4,512]{1,0:T(4,128)(2,1)S(1)} collective-permute-done((bf16[4,512]{1,0:T(4,128)(2,1)S(1)}, bf16[4,512]{1,0:T(4,128)(2,1)S(1)}, u32[]{:S(2)}, u32[]{:S(2)}) %collective-permute-start.2) | collective-permute-done | bytes 4128 | tf_op jit(solution)/shard_map/ppermute | solution.py:228
  117.8 4.0 %collective-permute-start.4 = (bf16[8,512]{1,0:T(8,128)(2,1)S(1)}, bf16[8,512]{1,0:T(8,128)(2,1)S(1)}, u32[]{:S(2)}, u32[]{:S(2)}) collective-permute-start(bf16[8,512]{1,0:T(8,128)(2,1)S(1)} %pad_maximum_fusion.2.refs_1_), channel_id=1, source_target_pairs={{0,16},{4,20},{8,24},{12,28},{16,32},{20,36},{24,40},{28,44},{32,4... | collective-permute-start | bytes 24584 | tf_op jit(solution)/shard_map/ppermute | solution.py:223
  122.0 3.6 %collective-permute-start.6 = (bf16[8,512]{1,0:T(8,128)(2,1)S(1)}, bf16[8,512]{1,0:T(8,128)(2,1)S(1)}, u32[]{:S(2)}, u32[]{:S(2)}) collective-permute-start(bf16[8,512]{1,0:T(8,128)(2,1)S(1)} %pad_maximum_fusion.2.refs_1_), channel_id=1, source_target_pairs={{0,32},{4,36},{8,40},{12,44},{16,48},{20,52},{24,56},{28,60},{32,0... | collective-permute-start | bytes 24584 | tf_op jit(solution)/shard_map/ppermute | solution.py:223
  127.2 2.2 collective-permute-start.8
  129.4 2.7 %collective-permute-start.9 = (bf16[8,512]{1,0:T(8,128)(2,1)S(1)}, bf16[8,512]{1,0:T(8,128)(2,1)S(1)}, u32[]{:S(2)}, u32[]{:S(2)}) collective-permute-start(bf16[8,512]{1,0:T(8,128)(2,1)S(1)} %pad_maximum_fusion.2.refs_1_), channel_id=1, source_target_pairs={{0,56},{4,60},{8,0},{12,4},{16,8},{20,12},{24,16},{28,20},{32,24},... | collective-permute-start | bytes 24584 | tf_op jit(solution)/shard_map/ppermute | solution.py:223
  136.0 4.1 %convolution_convert_fusion.refs_1_ = bf16[512,1024]{1,0:T(8,128)(2,1)} fusion(bf16[1024,1024]{1,0:T(8,128)(2,1)} %param.10, bf16[512,3328]{1,0:T(8,128)(2,1)} %bitcast.8.refs_2_.refs_3_.refs_4_), kind=kOutput, calls=%fused_computation.2 | convolution fusion | flops 1074266112 | bytes 4194304 | tf_op jit(solution)/shard_map/dot_general | solution.py:23
  140.1 11.7 %attend.2 = (bf16[512,3072]{1,0:T(8,128)(2,1)}, bf16[512,1024]{1,0:T(8,128)(2,1)}) custom-call(f32[1,512]{1,0:T(1,128)} %tag_order.1.refs_0_, bf16[512,1024]{1,0:T(8,128)(2,1)} %convolution_convert_fusion.refs_1_, bf16[512,3328]{1,0:T(8,128)(2,1)} %bitcast.8.refs_2_.refs_3_.refs_4_, bf16[512,3328]{1,0:T(8,128)(2,1)} %bitcast.8.refs_2_.refs_3_.refs_4_, ...), custom_call_target="tpu_custom_call" | custom-call | flops 2415919104 | bytes 6291456 | tf_op jit(solution)/shard_map/attend/pallas_call | solution.py:259
  151.8 5.8 %attend.3 = (bf16[512,3072]{1,0:T(8,128)(2,1)}, bf16[512,1024]{1,0:T(8,128)(2,1)}) custom-call(f32[1,512]{1,0:T(1,128)} %tag_order.1.refs_0_, bf16[512,1024]{1,0:T(8,128)(2,1)} %convolution_convert_fusion.refs_1_, bf16[512,768]{1,0:T(8,128)(2,1)} %bitcast.10.refs_2_.refs_3_.refs_4_, ...), custom_call_target="tpu_custom_call", output_to_operand_aliasing={{0}: (5, {}), {1}: (6, {})} | custom-call | flops 805306368 | bytes 2097152 | tf_op jit(solution)/shard_map/attend/pallas_call | solution.py:259
  157.6 9.7 %all-to-all-start.2 = ((bf16[64,8,3072]{2,1,0:T(8,128)(2,1)}), bf16[64,8,3072]{2,1,0:T(8,128)(2,1)}, u32[]{:S(2)}, u32[]{:S(2)}) async-start(bf16[64,8,3072]{2,1,0:T(8,128)(2,1)} %bitcast.57), calls=%async_computation.2 | async-start | bytes 6291456 | tf_op jit(solution)/shard_map/all_to_all | solution.py:184
  167.4 2.5 fusion.1
  172.3 2.5 %collective-permute-done.10 = bf16[32,16,1024]{2,1,0:T(8,128)(2,1)S(1)} collective-permute-done((bf16[32,16,1024]{2,1,0:T(8,128)(2,1)S(1)}, bf16[32,16,1024]{2,1,0:T(8,128)(2,1)S(1)}, u32[]{:S(2)}, u32[]{:S(2)}) %collective-permute-start.10) | collective-permute-done | bytes 1048608 | tf_op jit(solution)/shard_map/ppermute | solution.py:314
  176.8 2.8 %collective-permute-start.13 = (bf16[512,256]{1,0:T(8,128)(2,1)S(1)}, bf16[512,256]{1,0:T(8,128)(2,1)S(1)}, u32[]{:S(2)}, u32[]{:S(2)}) collective-permute-start(bf16[512,256]{1,0:T(8,128)(2,1)S(1)} %get-tuple-element.25), channel_id=1, source_target_pairs={{0,3},{1,0},{2,1},{3,2},{4,7},{5,4},{6,5},{7,6},{8,11},{9,8},{10,9... | collective-permute-start | bytes 786440 | tf_op jit(solution)/shard_map/ppermute | solution.py:320
  181.3 9.8 %collective-permute-done.13 = bf16[512,256]{1,0:T(8,128)(2,1)S(1)} collective-permute-done((bf16[512,256]{1,0:T(8,128)(2,1)S(1)}, bf16[512,256]{1,0:T(8,128)(2,1)S(1)}, u32[]{:S(2)}, u32[]{:S(2)}) %collective-permute-start.13) | collective-permute-done | bytes 262176 | tf_op jit(solution)/shard_map/ppermute | solution.py:320
  191.2 3.8 %collective-permute-done.11 = bf16[512,256]{1,0:T(8,128)(2,1)} collective-permute-done((bf16[512,256]{1,0:T(8,128)(2,1)S(1)}, bf16[512,256]{1,0:T(8,128)(2,1)}, u32[]{:S(2)}, u32[]{:S(2)}) %collective-permute-start.11) | collective-permute-done | bytes 262176 | tf_op jit(solution)/shard_map/ppermute | solution.py:320
  196.7 2.5 collective-permute-start.15
  202.4 3.1 %collective-permute-done.15 = bf16[128,256]{1,0:T(8,128)(2,1)S(1)} collective-permute-done((bf16[128,256]{1,0:T(8,128)(2,1)S(1)}, bf16[128,256]{1,0:T(8,128)(2,1)S(1)}, u32[]{:S(2)}, u32[]{:S(2)}) %collective-permute-start.15) | collective-permute-done | bytes 65568 | tf_op jit(solution)/shard_map/ppermute | solution.py:329
  205.7 4.3 %collective-permute-done.17 = bf16[128,256]{1,0:T(8,128)(2,1)S(1)} collective-permute-done((bf16[128,256]{1,0:T(8,128)(2,1)S(1)}, bf16[128,256]{1,0:T(8,128)(2,1)S(1)}, u32[]{:S(2)}, u32[]{:S(2)}) %collective-permute-start.17) | collective-permute-done | bytes 65568 | tf_op jit(solution)/shard_map/ppermute | solution.py:337
  210.3 6.0 %collective-permute-done.18 = bf16[128,512]{1,0:T(8,128)(2,1)S(1)} collective-permute-done((bf16[128,512]{1,0:T(8,128)(2,1)S(1)}, bf16[128,512]{1,0:T(8,128)(2,1)S(1)}, u32[]{:S(2)}, u32[]{:S(2)}) %collective-permute-start.18) | collective-permute-done | bytes 131104 | tf_op jit(solution)/shard_map/ppermute | solution.py:337
  218.4 4.7 %collective-permute-start.20 = (bf16[16,1024]{1,0:T(8,128)(2,1)S(1)}, bf16[16,1024]{1,0:T(8,128)(2,1)}, u32[]{:S(2)}, u32[]{:S(2)}) collective-permute-start(bf16[16,1024]{1,0:T(8,128)(2,1)S(1)} %get-tuple-element.35), channel_id=1, source_target_pairs={{0,16},{4,20},{8,24},{12,28},{16,32},{20,36},{24,40},{28,44},{32,4... | collective-permute-start | bytes 98312 | tf_op jit(solution)/shard_map/ppermute | solution.py:345
  223.3 3.8 %collective-permute-start.22 = (bf16[16,1024]{1,0:T(8,128)(2,1)}, bf16[16,1024]{1,0:T(8,128)(2,1)}, u32[]{:S(2)}, u32[]{:S(2)}) collective-permute-start(bf16[16,1024]{1,0:T(8,128)(2,1)} %get-tuple-element.33), channel_id=1, source_target_pairs={{0,32},{4,36},{8,40},{12,44},{16,48},{20,52},{24,56},{28,60},{32,0... | collective-permute-start | bytes 98312 | tf_op jit(solution)/shard_map/ppermute | solution.py:345
  228.8 8.0 %collective-permute-done.19.refs_2_ = bf16[16,1024]{1,0:T(8,128)(2,1)} collective-permute-done((bf16[16,1024]{1,0:T(8,128)(2,1)S(1)}, bf16[16,1024]{1,0:T(8,128)(2,1)}, u32[]{:S(2)}, u32[]{:S(2)}) %collective-permute-start.19) | collective-permute-done | bytes 32800 | tf_op jit(solution)/shard_map/ppermute | solution.py:345
  236.8 4.2 %collective-permute-start.24 = (bf16[16,1024]{1,0:T(8,128)(2,1)}, bf16[16,1024]{1,0:T(8,128)(2,1)}, u32[]{:S(2)}, u32[]{:S(2)}) collective-permute-start(bf16[16,1024]{1,0:T(8,128)(2,1)} %get-tuple-element.31), channel_id=1, source_target_pairs={{0,48},{4,52},{8,56},{12,60},{16,0},{20,4},{24,8},{28,12},{32,16},... | collective-permute-start | bytes 98312 | tf_op jit(solution)/shard_map/ppermute | solution.py:345
  241.1 2.1 collective-permute-start.25
  243.2 2.0 flip.1.back_ref
  246.9 5.3 %unpack.1 = (bf16[512,1024]{1,0:T(8,128)(2,1)}, bf16[512,1024]{1,0:T(8,128)(2,1)}, bf16[512,1024]{1,0:T(8,128)(2,1)}) custom-call(bf16[512,512]{1,0:T(8,128)(2,1)} %flip.1.back_ref, bf16[512,3072]{1,0:T(8,128)(2,1)} %bitcast.12.ret_ref), custom_call_target="tpu_custom_call" | custom-call | flops 1610612736 | bytes 6291456 | tf_op jit(solution)/shard_map/unpack/pallas_call | solution.py:296
  (69 shorter events, 29.6 us)
Async XLA Ops:
  7.0 88.8 %all-to-all-start = ((bf16[64,8,3328]{2,1,0:T(8,128)(2,1)}), bf16[64,8,3328]{2,1,0:T(8,128)(2,1)}, u32[]{:S(2)}, u32[]{:S(2)}) async-start(bf16[64,8,3328]{2,1,0:T(8,128)(2,1)} %bitcast.60), calls=%async_computation | async-start | bytes 6815744 | tf_op jit(solution)/shard_map/all_to_all | solution.py:184
  95.8 56.0 %all-to-all-start.1 = ((bf16[64,8,768]{2,1,0:T(8,128)(2,1)}), bf16[64,8,768]{2,1,0:T(8,128)(2,1)}, u32[]{:S(2)}, u32[]{:S(2)}) async-start(bf16[64,8,768]{2,1,0:T(8,128)(2,1)} %bitcast.61), calls=%async_computation.1 | async-start | bytes 1572864 | tf_op jit(solution)/shard_map/all_to_all | solution.py:184
  103.8 1.5 collective-permute-start
  105.9 3.7 %collective-permute-start.1 = (bf16[2,512]{1,0:T(2,128)(2,1)S(1)}, bf16[2,512]{1,0:T(2,128)(2,1)S(1)}, u32[]{:S(2)}, u32[]{:S(2)}) collective-permute-start(bf16[2,512]{1,0:T(2,128)(2,1)S(1)} %pad_maximum_fusion.4), channel_id=1, source_target_pairs={{0,64},{4,68},{8,72},{12,76},{16,80},{20,84},{24,88},{28,92},{32,9... | collective-permute-start | bytes 6152 | tf_op jit(solution)/shard_map/ppermute | solution.py:228
  110.3 5.2 %collective-permute-start.2 = (bf16[4,512]{1,0:T(4,128)(2,1)S(1)}, bf16[4,512]{1,0:T(4,128)(2,1)S(1)}, u32[]{:S(2)}, u32[]{:S(2)}) collective-permute-start(bf16[4,512]{1,0:T(4,128)(2,1)S(1)} %pad_maximum_fusion.3), channel_id=1, source_target_pairs={{0,128},{4,132},{8,136},{12,140},{16,144},{20,148},{24,152},{28,15... | collective-permute-start | bytes 12296 | tf_op jit(solution)/shard_map/ppermute | solution.py:228
  116.2 17.3 %copy-start.2 = (bf16[8,512]{1,0:T(8,128)(2,1)}, bf16[8,512]{1,0:T(8,128)(2,1)S(1)}, u32[]{:S(2)}) copy-start(bf16[8,512]{1,0:T(8,128)(2,1)S(1)} %pad_maximum_fusion.2.refs_1_) | copy-start | bytes 24580
  116.2 11.0 %collective-permute-start.3 = (bf16[8,512]{1,0:T(8,128)(2,1)S(1)}, bf16[8,512]{1,0:T(8,128)(2,1)S(1)}, u32[]{:S(2)}, u32[]{:S(2)}) collective-permute-start(bf16[8,512]{1,0:T(8,128)(2,1)S(1)} %pad_maximum_fusion.2.refs_1_), channel_id=1, source_target_pairs={{0,8},{4,12},{8,16},{12,20},{16,24},{20,28},{24,32},{28,36},{32,40... | collective-permute-start | bytes 24584 | tf_op jit(solution)/shard_map/ppermute | solution.py:223
  117.8 11.6 %collective-permute-start.4 = (bf16[8,512]{1,0:T(8,128)(2,1)S(1)}, bf16[8,512]{1,0:T(8,128)(2,1)S(1)}, u32[]{:S(2)}, u32[]{:S(2)}) collective-permute-start(bf16[8,512]{1,0:T(8,128)(2,1)S(1)} %pad_maximum_fusion.2.refs_1_), channel_id=1, source_target_pairs={{0,16},{4,20},{8,24},{12,28},{16,32},{20,36},{24,40},{28,44},{32,4... | collective-permute-start | bytes 24584 | tf_op jit(solution)/shard_map/ppermute | solution.py:223
  121.8 10.9 %collective-permute-start.5 = (bf16[8,512]{1,0:T(8,128)(2,1)S(1)}, bf16[8,512]{1,0:T(8,128)(2,1)S(1)}, u32[]{:S(2)}, u32[]{:S(2)}) collective-permute-start(bf16[8,512]{1,0:T(8,128)(2,1)S(1)} %pad_maximum_fusion.2.refs_1_), channel_id=1, source_target_pairs={{0,24},{4,28},{8,32},{12,36},{16,40},{20,44},{24,48},{28,52},{32,5... | collective-permute-start | bytes 24584 | tf_op jit(solution)/shard_map/ppermute | solution.py:223
  122.0 10.7 %collective-permute-start.6 = (bf16[8,512]{1,0:T(8,128)(2,1)S(1)}, bf16[8,512]{1,0:T(8,128)(2,1)S(1)}, u32[]{:S(2)}, u32[]{:S(2)}) collective-permute-start(bf16[8,512]{1,0:T(8,128)(2,1)S(1)} %pad_maximum_fusion.2.refs_1_), channel_id=1, source_target_pairs={{0,32},{4,36},{8,40},{12,44},{16,48},{20,52},{24,56},{28,60},{32,0... | collective-permute-start | bytes 24584 | tf_op jit(solution)/shard_map/ppermute | solution.py:223
  125.6 7.1 %collective-permute-start.7 = (bf16[8,512]{1,0:T(8,128)(2,1)S(1)}, bf16[8,512]{1,0:T(8,128)(2,1)S(1)}, u32[]{:S(2)}, u32[]{:S(2)}) collective-permute-start(bf16[8,512]{1,0:T(8,128)(2,1)S(1)} %pad_maximum_fusion.2.refs_1_), channel_id=1, source_target_pairs={{0,40},{4,44},{8,48},{12,52},{16,56},{20,60},{24,0},{28,4},{32,8},... | collective-permute-start | bytes 24584 | tf_op jit(solution)/shard_map/ppermute | solution.py:223
  127.2 6.3 %copy-start.3 = (bf16[8,512]{1,0:T(8,128)(2,1)}, bf16[8,512]{1,0:T(8,128)(2,1)S(1)}, u32[]{:S(2)}) copy-start(bf16[8,512]{1,0:T(8,128)(2,1)S(1)} %collective-permute-done.3.refs_2_) | copy-start | bytes 24580
  127.2 5.6 %collective-permute-start.8 = (bf16[8,512]{1,0:T(8,128)(2,1)S(1)}, bf16[8,512]{1,0:T(8,128)(2,1)S(1)}, u32[]{:S(2)}, u32[]{:S(2)}) collective-permute-start(bf16[8,512]{1,0:T(8,128)(2,1)S(1)} %pad_maximum_fusion.2.refs_1_), channel_id=1, source_target_pairs={{0,48},{4,52},{8,56},{12,60},{16,0},{20,4},{24,8},{28,12},{32,16},... | collective-permute-start | bytes 24584 | tf_op jit(solution)/shard_map/ppermute | solution.py:223
  129.4 4.0 %collective-permute-start.9 = (bf16[8,512]{1,0:T(8,128)(2,1)S(1)}, bf16[8,512]{1,0:T(8,128)(2,1)S(1)}, u32[]{:S(2)}, u32[]{:S(2)}) collective-permute-start(bf16[8,512]{1,0:T(8,128)(2,1)S(1)} %pad_maximum_fusion.2.refs_1_), channel_id=1, source_target_pairs={{0,56},{4,60},{8,0},{12,4},{16,8},{20,12},{24,16},{28,20},{32,24},... | collective-permute-start | bytes 24584 | tf_op jit(solution)/shard_map/ppermute | solution.py:223
  157.6 9.8 %copy-start.1 = (bf16[512,1024]{1,0:T(8,128)(2,1)S(1)}, bf16[512,1024]{1,0:T(8,128)(2,1)}, u32[]{:S(2)}) copy-start(bf16[512,1024]{1,0:T(8,128)(2,1)} %get-tuple-element.23) | copy-start | bytes 3145732
  157.6 89.2 %all-to-all-start.2 = ((bf16[64,8,3072]{2,1,0:T(8,128)(2,1)}), bf16[64,8,3072]{2,1,0:T(8,128)(2,1)}, u32[]{:S(2)}, u32[]{:S(2)}) async-start(bf16[64,8,3072]{2,1,0:T(8,128)(2,1)} %bitcast.57), calls=%async_computation.2 | async-start | bytes 6291456 | tf_op jit(solution)/shard_map/all_to_all | solution.py:184
  172.1 2.7 %collective-permute-start.10 = (bf16[32,16,1024]{2,1,0:T(8,128)(2,1)S(1)}, bf16[32,16,1024]{2,1,0:T(8,128)(2,1)S(1)}, u32[]{:S(2)}, u32[]{:S(2)}) collective-permute-start(bf16[32,16,1024]{2,1,0:T(8,128)(2,1)S(1)} %fusion), channel_id=1, source_target_pairs={{0,4},{4,0},{8,12},{12,8},{16,20},{20,16},{24,28},{28,24},{32,36},... | collective-permute-start | bytes 3145736 | tf_op jit(solution)/shard_map/ppermute | solution.py:314
  176.8 14.4 %collective-permute-start.13 = (bf16[512,256]{1,0:T(8,128)(2,1)S(1)}, bf16[512,256]{1,0:T(8,128)(2,1)S(1)}, u32[]{:S(2)}, u32[]{:S(2)}) collective-permute-start(bf16[512,256]{1,0:T(8,128)(2,1)S(1)} %get-tuple-element.25), channel_id=1, source_target_pairs={{0,3},{1,0},{2,1},{3,2},{4,7},{5,4},{6,5},{7,6},{8,11},{9,8},{10,9... | collective-permute-start | bytes 786440 | tf_op jit(solution)/shard_map/ppermute | solution.py:320
  179.6 11.5 %collective-permute-start.12 = (bf16[512,256]{1,0:T(8,128)(2,1)S(1)}, bf16[512,256]{1,0:T(8,128)(2,1)S(1)}, u32[]{:S(2)}, u32[]{:S(2)}) collective-permute-start(bf16[512,256]{1,0:T(8,128)(2,1)S(1)} %get-tuple-element.26), channel_id=1, source_target_pairs={{0,2},{1,3},{2,0},{3,1},{4,6},{5,7},{6,4},{7,5},{8,10},{9,11},{10,... | collective-permute-start | bytes 786440 | tf_op jit(solution)/shard_map/ppermute | solution.py:320
  180.4 14.5 %collective-permute-start.11 = (bf16[512,256]{1,0:T(8,128)(2,1)S(1)}, bf16[512,256]{1,0:T(8,128)(2,1)}, u32[]{:S(2)}, u32[]{:S(2)}) collective-permute-start(bf16[512,256]{1,0:T(8,128)(2,1)S(1)} %get-tuple-element.24), channel_id=1, source_target_pairs={{0,1},{1,2},{2,3},{3,0},{4,5},{5,6},{6,7},{7,4},{8,9},{9,10},{10,1... | collective-permute-start | bytes 786440 | tf_op jit(solution)/shard_map/ppermute | solution.py:320
  196.1 6.4 %collective-permute-start.16 = (bf16[128,256]{1,0:T(8,128)(2,1)S(1)}, bf16[128,256]{1,0:T(8,128)(2,1)S(1)}, u32[]{:S(2)}, u32[]{:S(2)}) collective-permute-start(bf16[128,256]{1,0:T(8,128)(2,1)S(1)} %get-tuple-element.28), channel_id=1, source_target_pairs={{0,192},{4,196},{8,200},{12,204},{16,208},{20,212},{24,216},{28,22... | collective-permute-start | bytes 196616 | tf_op jit(solution)/shard_map/ppermute | solution.py:329
  196.7 8.9 %collective-permute-start.15 = (bf16[128,256]{1,0:T(8,128)(2,1)S(1)}, bf16[128,256]{1,0:T(8,128)(2,1)S(1)}, u32[]{:S(2)}, u32[]{:S(2)}) collective-permute-start(bf16[128,256]{1,0:T(8,128)(2,1)S(1)} %get-tuple-element.29), channel_id=1, source_target_pairs={{0,128},{4,132},{8,136},{12,140},{16,144},{20,148},{24,152},{28,15... | collective-permute-start | bytes 196616 | tf_op jit(solution)/shard_map/ppermute | solution.py:329
  199.2 6.4 %collective-permute-start.14 = (bf16[128,256]{1,0:T(8,128)(2,1)S(1)}, bf16[128,256]{1,0:T(8,128)(2,1)S(1)}, u32[]{:S(2)}, u32[]{:S(2)}) collective-permute-start(bf16[128,256]{1,0:T(8,128)(2,1)S(1)} %get-tuple-element.27), channel_id=1, source_target_pairs={{0,64},{4,68},{8,72},{12,76},{16,80},{20,84},{24,88},{28,92},{32,9... | collective-permute-start | bytes 196616 | tf_op jit(solution)/shard_map/ppermute | solution.py:329
  205.6 4.4 %collective-permute-start.17 = (bf16[128,256]{1,0:T(8,128)(2,1)S(1)}, bf16[128,256]{1,0:T(8,128)(2,1)S(1)}, u32[]{:S(2)}, u32[]{:S(2)}) collective-permute-start(bf16[128,256]{1,0:T(8,128)(2,1)S(1)} %fusion.5), channel_id=1, source_target_pairs={{0,1},{1,0},{2,3},{3,2},{4,5},{5,4},{6,7},{7,6},{8,9},{9,8},{10,11... | collective-permute-start | bytes 196616 | tf_op jit(solution)/shard_map/ppermute | solution.py:337
  210.0 6.3 %collective-permute-start.18 = (bf16[128,512]{1,0:T(8,128)(2,1)S(1)}, bf16[128,512]{1,0:T(8,128)(2,1)S(1)}, u32[]{:S(2)}, u32[]{:S(2)}) collective-permute-start(bf16[128,512]{1,0:T(8,128)(2,1)S(1)} %pad_maximum_fusion.1), channel_id=1, source_target_pairs={{0,3},{1,2},{2,1},{3,0},{4,7},{5,6},{6,5},{7,4},{8,11},{9,10},{10,... | collective-permute-start | bytes 393224 | tf_op jit(solution)/shard_map/ppermute | solution.py:337
  216.9 19.9 %collective-permute-start.19 = (bf16[16,1024]{1,0:T(8,128)(2,1)S(1)}, bf16[16,1024]{1,0:T(8,128)(2,1)}, u32[]{:S(2)}, u32[]{:S(2)}) collective-permute-start(bf16[16,1024]{1,0:T(8,128)(2,1)S(1)} %get-tuple-element.36), channel_id=1, source_target_pairs={{0,8},{4,12},{8,16},{12,20},{16,24},{20,28},{24,32},{28,36},{32,40... | collective-permute-start | bytes 98312 | tf_op jit(solution)/shard_map/ppermute | solution.py:345
  218.4 22.7 %collective-permute-start.20 = (bf16[16,1024]{1,0:T(8,128)(2,1)S(1)}, bf16[16,1024]{1,0:T(8,128)(2,1)}, u32[]{:S(2)}, u32[]{:S(2)}) collective-permute-start(bf16[16,1024]{1,0:T(8,128)(2,1)S(1)} %get-tuple-element.35), channel_id=1, source_target_pairs={{0,16},{4,20},{8,24},{12,28},{16,32},{20,36},{24,40},{28,44},{32,4... | collective-permute-start | bytes 98312 | tf_op jit(solution)/shard_map/ppermute | solution.py:345
  223.1 22.1 %collective-permute-start.21 = (bf16[16,1024]{1,0:T(8,128)(2,1)}, bf16[16,1024]{1,0:T(8,128)(2,1)}, u32[]{:S(2)}, u32[]{:S(2)}) collective-permute-start(bf16[16,1024]{1,0:T(8,128)(2,1)} %get-tuple-element.34), channel_id=1, source_target_pairs={{0,24},{4,28},{8,32},{12,36},{16,40},{20,44},{24,48},{28,52},{32,5... | collective-permute-start | bytes 98312 | tf_op jit(solution)/shard_map/ppermute | solution.py:345
  223.3 21.9 %collective-permute-start.22 = (bf16[16,1024]{1,0:T(8,128)(2,1)}, bf16[16,1024]{1,0:T(8,128)(2,1)}, u32[]{:S(2)}, u32[]{:S(2)}) collective-permute-start(bf16[16,1024]{1,0:T(8,128)(2,1)} %get-tuple-element.33), channel_id=1, source_target_pairs={{0,32},{4,36},{8,40},{12,44},{16,48},{20,52},{24,56},{28,60},{32,0... | collective-permute-start | bytes 98312 | tf_op jit(solution)/shard_map/ppermute | solution.py:345
  227.1 18.2 %collective-permute-start.23 = (bf16[16,1024]{1,0:T(8,128)(2,1)}, bf16[16,1024]{1,0:T(8,128)(2,1)}, u32[]{:S(2)}, u32[]{:S(2)}) collective-permute-start(bf16[16,1024]{1,0:T(8,128)(2,1)} %get-tuple-element.32), channel_id=1, source_target_pairs={{0,40},{4,44},{8,48},{12,52},{16,56},{20,60},{24,0},{28,4},{32,8},... | collective-permute-start | bytes 98312 | tf_op jit(solution)/shard_map/ppermute | solution.py:345
  236.8 8.4 %collective-permute-start.24 = (bf16[16,1024]{1,0:T(8,128)(2,1)}, bf16[16,1024]{1,0:T(8,128)(2,1)}, u32[]{:S(2)}, u32[]{:S(2)}) collective-permute-start(bf16[16,1024]{1,0:T(8,128)(2,1)} %get-tuple-element.31), channel_id=1, source_target_pairs={{0,48},{4,52},{8,56},{12,60},{16,0},{20,4},{24,8},{28,12},{32,16},... | collective-permute-start | bytes 98312 | tf_op jit(solution)/shard_map/ppermute | solution.py:345
  241.1 4.2 %collective-permute-start.25 = (bf16[16,1024]{1,0:T(8,128)(2,1)}, bf16[16,1024]{1,0:T(8,128)(2,1)}, u32[]{:S(2)}, u32[]{:S(2)}) collective-permute-start(bf16[16,1024]{1,0:T(8,128)(2,1)} %get-tuple-element.30), channel_id=1, source_target_pairs={{0,56},{4,60},{8,0},{12,4},{16,8},{20,12},{24,16},{28,20},{32,24},... | collective-permute-start | bytes 98312 | tf_op jit(solution)/shard_map/ppermute | solution.py:345
  (7 other events, 9.6 us)

commit v7 on v6

--- a/solution.py
+++ b/solution.py
@@ -104,12 +104,8 @@
 
     @pl.when(pl.program_id(0) == 0)
     def _():
-        tags = column_of(tag_ref[...], rows)
-
-        @pl.loop(0, rows // LANES)
-        def _(j):
-            cols = pl.ds(pl.multiple_of(j * LANES, LANES), LANES)
-            bias_ref[:, cols] = jnp.where(tags == tag_ref[:, cols], 0.0, big_negative)
+        tags = tag_ref[...]
+        bias_ref[...] = jnp.where(column_of(tags, rows) == tags, 0.0, big_negative)
 
     for h in range(UNIT // HEAD_DIM):
         cols = slice(h * HEAD_DIM, (h + 1) * HEAD_DIM)

time: 255 us -> 254 us (level)
  no operation moved by 1% of the time
where the time goes in v7:
time: 254 us; the launch traced here: 251 us
  waiting for transfers between devices  120 us (47%)
  starting transfers between devices  78 us (31%)
  Pallas kernels  36.4 us (14%)
  matrix products  6.66 us (3%)
  other arithmetic  5.7 us (2%)
  local copies, waits for them, and re-layouts  3.57 us (1%)
    all_to_all x3, waiting for transfers between devices, exchange(): lax.all_to_all(rows_in.reshape(node_count, bucket, c), 'nodes', split_axi...  74.2 us
    all_to_all x3, starting transfers between devices, exchange(): lax.all_to_all(rows_in.reshape(node_count, bucket, c), 'nodes', split_axi...  29.5 us
    ppermute x7, starting transfers between devices, local(): shares.append(lax.ppermute(sent, 'nodes', hop(0, s, 0)))  18.2 us
    pallas_call x2, Pallas kernels, attention(): pl.pallas_call(lambda *refs: attend(scale, *refs), out_shape=(sds((rows,...  16.5 us
    ppermute x8, starting transfers between devices, around(): lax.ppermute(line, 'nodes', hop(*step(s)))  16.1 us
    ppermute x3, waiting for transfers between devices, local(): came.append(lax.ppermute(sent, 'rep', ring(nx, s)))  13.6 us
    ppermute x2, waiting for transfers between devices, local(): came = lax.ppermute(turn, 'rep', [(i, i ^ mask) for i in range(nx)])  10.2 us
    ppermute x7, waiting for transfers between devices, local(): shares.append(lax.ppermute(sent, 'nodes', hop(0, s, 0)))  8.08 us
  transfers between devices with their start and end apart: 29, of which 14 were waited for; matrix products, arithmetic and copies ran while one was open for 5% of the time, Pallas kernels for 8%

profile of v7, /device:TPU:40, one launch (start us, length us, event | category | flops | bytes accessed | tf_op | source)
XLA Modules:
  0.0 251.2 jit_solution(6745938975684694563)
XLA Ops:
  0.6 6.4 %pack_first.1 = (bf16[512,3328]{1,0:T(8,128)(2,1)}, bf16[512,512]{1,0:T(8,128)(2,1)}, bf16[1,512]{1,0:T(2,128)(2,1)}) custom-call(s32[1,512]{1,0:T(1,128)} %refs_0_.1, bf16[512,1024]{1,0:T(8,128)(2,1)} %bitcast.71, bf16[512,1024]{1,0:T(8,128)(2,1)} %bitcast.64, bf16[512,1024]{1,0:T(8,128)(2,1)} %bitcast.66, bf16[512,1024]{1,0:T(8,128)(2,1)} %bitcast.68), custom_call_target="tpu_custom_call" | custom-call | flops 1744830464 | bytes 6815744 | tf_op jit(solution)/shard_map/pack_first/pallas_call | solution.py:191
  7.0 11.8 %all-to-all-start = ((bf16[64,8,3328]{2,1,0:T(8,128)(2,1)}), bf16[64,8,3328]{2,1,0:T(8,128)(2,1)}, u32[]{:S(2)}, u32[]{:S(2)}) async-start(bf16[64,8,3328]{2,1,0:T(8,128)(2,1)} %bitcast.60), calls=%async_computation | async-start | bytes 6815744 | tf_op jit(solution)/shard_map/all_to_all | solution.py:180
  18.8 2.7 %pack_rest.1 = bf16[512,768]{1,0:T(8,128)(2,1)} custom-call(bf16[512,512]{1,0:T(8,128)(2,1)} %get-tuple-element.14.in_ref.pick_ref, bf16[512,1024]{1,0:T(8,128)(2,1)} %bitcast.65, bf16[512,1024]{1,0:T(8,128)(2,1)} %bitcast.67, bf16[512,1024]{1,0:T(8,128)(2,1)} %bitcast.69), custom_call_target="tpu_custom_call" | custom-call | flops 402653184 | bytes 1572864 | tf_op jit(solution)/shard_map/pack_rest/pallas_call | solution.py:237
  21.6 74.2 %all-to-all-done = bf16[64,8,3328]{2,1,0:T(8,128)(2,1)} async-done(((bf16[64,8,3328]{2,1,0:T(8,128)(2,1)}), bf16[64,8,3328]{2,1,0:T(8,128)(2,1)}, u32[]{:S(2)}, u32[]{:S(2)}) %all-to-all-start) | async-done | bytes 3407904 | tf_op jit(solution)/shard_map/all_to_all | solution.py:180
  95.8 8.0 %all-to-all-start.1 = ((bf16[64,8,768]{2,1,0:T(8,128)(2,1)}), bf16[64,8,768]{2,1,0:T(8,128)(2,1)}, u32[]{:S(2)}, u32[]{:S(2)}) async-start(bf16[64,8,768]{2,1,0:T(8,128)(2,1)} %bitcast.61), calls=%async_computation.1 | async-start | bytes 1572864 | tf_op jit(solution)/shard_map/all_to_all | solution.py:180
  107.6 2.0 collective-permute-done.1
  110.3 2.4 collective-permute-start.2
  112.7 2.8 %collective-permute-done.2 = bf16[4,512]{1,0:T(4,128)(2,1)S(1)} collective-permute-done((bf16[4,512]{1,0:T(4,128)(2,1)S(1)}, bf16[4,512]{1,0:T(4,128)(2,1)S(1)}, u32[]{:S(2)}, u32[]{:S(2)}) %collective-permute-start.2) | collective-permute-done | bytes 4128 | tf_op jit(solution)/shard_map/ppermute | solution.py:224
  117.8 4.0 %collective-permute-start.4 = (bf16[8,512]{1,0:T(8,128)(2,1)S(1)}, bf16[8,512]{1,0:T(8,128)(2,1)S(1)}, u32[]{:S(2)}, u32[]{:S(2)}) collective-permute-start(bf16[8,512]{1,0:T(8,128)(2,1)S(1)} %pad_maximum_fusion.2.refs_1_), channel_id=1, source_target_pairs={{0,16},{4,20},{8,24},{12,28},{16,32},{20,36},{24,40},{28,44},{32,4... | collective-permute-start | bytes 24584 | tf_op jit(solution)/shard_map/ppermute | solution.py:219
  122.0 3.6 %collective-permute-start.6 = (bf16[8,512]{1,0:T(8,128)(2,1)S(1)}, bf16[8,512]{1,0:T(8,128)(2,1)S(1)}, u32[]{:S(2)}, u32[]{:S(2)}) collective-permute-start(bf16[8,512]{1,0:T(8,128)(2,1)S(1)} %pad_maximum_fusion.2.refs_1_), channel_id=1, source_target_pairs={{0,32},{4,36},{8,40},{12,44},{16,48},{20,52},{24,56},{28,60},{32,0... | collective-permute-start | bytes 24584 | tf_op jit(solution)/shard_map/ppermute | solution.py:219
  127.2 2.2 collective-permute-start.8
  129.4 2.7 %collective-permute-start.9 = (bf16[8,512]{1,0:T(8,128)(2,1)S(1)}, bf16[8,512]{1,0:T(8,128)(2,1)S(1)}, u32[]{:S(2)}, u32[]{:S(2)}) collective-permute-start(bf16[8,512]{1,0:T(8,128)(2,1)S(1)} %pad_maximum_fusion.2.refs_1_), channel_id=1, source_target_pairs={{0,56},{4,60},{8,0},{12,4},{16,8},{20,12},{24,16},{28,20},{32,24},... | collective-permute-start | bytes 24584 | tf_op jit(solution)/shard_map/ppermute | solution.py:219
  136.0 4.1 %convolution_convert_fusion.refs_1_ = bf16[512,1024]{1,0:T(8,128)(2,1)} fusion(bf16[1024,1024]{1,0:T(8,128)(2,1)} %param.10, bf16[512,3328]{1,0:T(8,128)(2,1)} %bitcast.8.refs_2_.refs_3_.refs_4_), kind=kOutput, calls=%fused_computation.2 | convolution fusion | flops 1074266112 | bytes 4194304 | tf_op jit(solution)/shard_map/dot_general | solution.py:23
  140.1 11.3 %attend.2 = (bf16[512,3072]{1,0:T(8,128)(2,1)}, bf16[512,1024]{1,0:T(8,128)(2,1)}) custom-call(f32[1,512]{1,0:T(1,128)} %tag_order.1.refs_0_, bf16[512,1024]{1,0:T(8,128)(2,1)} %convolution_convert_fusion.refs_1_, bf16[512,3328]{1,0:T(8,128)(2,1)} %bitcast.8.refs_2_.refs_3_.refs_4_, bf16[512,3328]{1,0:T(8,128)(2,1)} %bitcast.8.refs_2_.refs_3_.refs_4_, ...), custom_call_target="tpu_custom_call" | custom-call | flops 2415919104 | bytes 6291456 | tf_op jit(solution)/shard_map/attend/pallas_call | solution.py:255
  151.4 5.3 %attend.3 = (bf16[512,3072]{1,0:T(8,128)(2,1)}, bf16[512,1024]{1,0:T(8,128)(2,1)}) custom-call(f32[1,512]{1,0:T(1,128)} %tag_order.1.refs_0_, bf16[512,1024]{1,0:T(8,128)(2,1)} %convolution_convert_fusion.refs_1_, bf16[512,768]{1,0:T(8,128)(2,1)} %bitcast.10.refs_2_.refs_3_.refs_4_, ...), custom_call_target="tpu_custom_call", output_to_operand_aliasing={{0}: (5, {}), {1}: (6, {})} | custom-call | flops 805306368 | bytes 2097152 | tf_op jit(solution)/shard_map/attend/pallas_call | solution.py:255
  156.7 9.7 %all-to-all-start.2 = ((bf16[64,8,3072]{2,1,0:T(8,128)(2,1)}), bf16[64,8,3072]{2,1,0:T(8,128)(2,1)}, u32[]{:S(2)}, u32[]{:S(2)}) async-start(bf16[64,8,3072]{2,1,0:T(8,128)(2,1)} %bitcast.57), calls=%async_computation.2 | async-start | bytes 6291456 | tf_op jit(solution)/shard_map/all_to_all | solution.py:180
  166.4 2.5 %fusion.1 = f32[1024,1024]{1,0:T(8,128)S(1)} fusion(bf16[512,1024]{1,0:T(8,128)(2,1)S(1)} %copy-done.1, bf16[512,3328]{1,0:T(8,128)(2,1)} %bitcast.8.refs_2_.refs_3_.refs_4_), kind=kOutput, calls=%fused_computation.4 | convolution fusion | flops 1073741824 | bytes 6291456 | tf_op jit(solution)/shard_map/dot_general | solution.py:23
  171.3 2.5 %collective-permute-done.10 = bf16[32,16,1024]{2,1,0:T(8,128)(2,1)S(1)} collective-permute-done((bf16[32,16,1024]{2,1,0:T(8,128)(2,1)S(1)}, bf16[32,16,1024]{2,1,0:T(8,128)(2,1)S(1)}, u32[]{:S(2)}, u32[]{:S(2)}) %collective-permute-start.10) | collective-permute-done | bytes 1048608 | tf_op jit(solution)/shard_map/ppermute | solution.py:310
  175.8 2.8 %collective-permute-start.13 = (bf16[512,256]{1,0:T(8,128)(2,1)S(1)}, bf16[512,256]{1,0:T(8,128)(2,1)S(1)}, u32[]{:S(2)}, u32[]{:S(2)}) collective-permute-start(bf16[512,256]{1,0:T(8,128)(2,1)S(1)} %get-tuple-element.25), channel_id=1, source_target_pairs={{0,3},{1,0},{2,1},{3,2},{4,7},{5,4},{6,5},{7,6},{8,11},{9,8},{10,9... | collective-permute-start | bytes 786440 | tf_op jit(solution)/shard_map/ppermute | solution.py:316
  180.4 9.8 %collective-permute-done.13 = bf16[512,256]{1,0:T(8,128)(2,1)S(1)} collective-permute-done((bf16[512,256]{1,0:T(8,128)(2,1)S(1)}, bf16[512,256]{1,0:T(8,128)(2,1)S(1)}, u32[]{:S(2)}, u32[]{:S(2)}) %collective-permute-start.13) | collective-permute-done | bytes 262176 | tf_op jit(solution)/shard_map/ppermute | solution.py:316
  190.2 3.8 %collective-permute-done.11 = bf16[512,256]{1,0:T(8,128)(2,1)} collective-permute-done((bf16[512,256]{1,0:T(8,128)(2,1)S(1)}, bf16[512,256]{1,0:T(8,128)(2,1)}, u32[]{:S(2)}, u32[]{:S(2)}) %collective-permute-start.11) | collective-permute-done | bytes 262176 | tf_op jit(solution)/shard_map/ppermute | solution.py:316
  195.7 2.5 collective-permute-start.15
  201.4 3.1 %collective-permute-done.15 = bf16[128,256]{1,0:T(8,128)(2,1)S(1)} collective-permute-done((bf16[128,256]{1,0:T(8,128)(2,1)S(1)}, bf16[128,256]{1,0:T(8,128)(2,1)S(1)}, u32[]{:S(2)}, u32[]{:S(2)}) %collective-permute-start.15) | collective-permute-done | bytes 65568 | tf_op jit(solution)/shard_map/ppermute | solution.py:325
  204.7 4.3 %collective-permute-done.17 = bf16[128,256]{1,0:T(8,128)(2,1)S(1)} collective-permute-done((bf16[128,256]{1,0:T(8,128)(2,1)S(1)}, bf16[128,256]{1,0:T(8,128)(2,1)S(1)}, u32[]{:S(2)}, u32[]{:S(2)}) %collective-permute-start.17) | collective-permute-done | bytes 65568 | tf_op jit(solution)/shard_map/ppermute | solution.py:333
  209.3 6.0 %collective-permute-done.18 = bf16[128,512]{1,0:T(8,128)(2,1)S(1)} collective-permute-done((bf16[128,512]{1,0:T(8,128)(2,1)S(1)}, bf16[128,512]{1,0:T(8,128)(2,1)S(1)}, u32[]{:S(2)}, u32[]{:S(2)}) %collective-permute-start.18) | collective-permute-done | bytes 131104 | tf_op jit(solution)/shard_map/ppermute | solution.py:333
  217.4 4.7 %collective-permute-start.20 = (bf16[16,1024]{1,0:T(8,128)(2,1)S(1)}, bf16[16,1024]{1,0:T(8,128)(2,1)}, u32[]{:S(2)}, u32[]{:S(2)}) collective-permute-start(bf16[16,1024]{1,0:T(8,128)(2,1)S(1)} %get-tuple-element.35), channel_id=1, source_target_pairs={{0,16},{4,20},{8,24},{12,28},{16,32},{20,36},{24,40},{28,44},{32,4... | collective-permute-start | bytes 98312 | tf_op jit(solution)/shard_map/ppermute | solution.py:341
  222.3 3.7 %collective-permute-start.22 = (bf16[16,1024]{1,0:T(8,128)(2,1)}, bf16[16,1024]{1,0:T(8,128)(2,1)}, u32[]{:S(2)}, u32[]{:S(2)}) collective-permute-start(bf16[16,1024]{1,0:T(8,128)(2,1)} %get-tuple-element.33), channel_id=1, source_target_pairs={{0,32},{4,36},{8,40},{12,44},{16,48},{20,52},{24,56},{28,60},{32,0... | collective-permute-start | bytes 98312 | tf_op jit(solution)/shard_map/ppermute | solution.py:341
  227.9 8.0 %collective-permute-done.19.refs_2_ = bf16[16,1024]{1,0:T(8,128)(2,1)} collective-permute-done((bf16[16,1024]{1,0:T(8,128)(2,1)S(1)}, bf16[16,1024]{1,0:T(8,128)(2,1)}, u32[]{:S(2)}, u32[]{:S(2)}) %collective-permute-start.19) | collective-permute-done | bytes 32800 | tf_op jit(solution)/shard_map/ppermute | solution.py:341
  235.9 4.2 %collective-permute-start.24 = (bf16[16,1024]{1,0:T(8,128)(2,1)}, bf16[16,1024]{1,0:T(8,128)(2,1)}, u32[]{:S(2)}, u32[]{:S(2)}) collective-permute-start(bf16[16,1024]{1,0:T(8,128)(2,1)} %get-tuple-element.31), channel_id=1, source_target_pairs={{0,48},{4,52},{8,56},{12,60},{16,0},{20,4},{24,8},{28,12},{32,16},... | collective-permute-start | bytes 98312 | tf_op jit(solution)/shard_map/ppermute | solution.py:341
  240.1 2.1 collective-permute-start.25
  242.2 2.0 flip.1.back_ref
  245.9 5.3 %unpack.1 = (bf16[512,1024]{1,0:T(8,128)(2,1)}, bf16[512,1024]{1,0:T(8,128)(2,1)}, bf16[512,1024]{1,0:T(8,128)(2,1)}) custom-call(bf16[512,512]{1,0:T(8,128)(2,1)} %flip.1.back_ref, bf16[512,3072]{1,0:T(8,128)(2,1)} %bitcast.12.ret_ref), custom_call_target="tpu_custom_call" | custom-call | flops 1610612736 | bytes 6291456 | tf_op jit(solution)/shard_map/unpack/pallas_call | solution.py:292
  (69 shorter events, 29.6 us)
Async XLA Ops:
  7.0 88.8 %all-to-all-start = ((bf16[64,8,3328]{2,1,0:T(8,128)(2,1)}), bf16[64,8,3328]{2,1,0:T(8,128)(2,1)}, u32[]{:S(2)}, u32[]{:S(2)}) async-start(bf16[64,8,3328]{2,1,0:T(8,128)(2,1)} %bitcast.60), calls=%async_computation | async-start | bytes 6815744 | tf_op jit(solution)/shard_map/all_to_all | solution.py:180
  95.8 55.6 %all-to-all-start.1 = ((bf16[64,8,768]{2,1,0:T(8,128)(2,1)}), bf16[64,8,768]{2,1,0:T(8,128)(2,1)}, u32[]{:S(2)}, u32[]{:S(2)}) async-start(bf16[64,8,768]{2,1,0:T(8,128)(2,1)} %bitcast.61), calls=%async_computation.1 | async-start | bytes 1572864 | tf_op jit(solution)/shard_map/all_to_all | solution.py:180
  103.8 1.5 collective-permute-start
  105.9 3.7 %collective-permute-start.1 = (bf16[2,512]{1,0:T(2,128)(2,1)S(1)}, bf16[2,512]{1,0:T(2,128)(2,1)S(1)}, u32[]{:S(2)}, u32[]{:S(2)}) collective-permute-start(bf16[2,512]{1,0:T(2,128)(2,1)S(1)} %pad_maximum_fusion.4), channel_id=1, source_target_pairs={{0,64},{4,68},{8,72},{12,76},{16,80},{20,84},{24,88},{28,92},{32,9... | collective-permute-start | bytes 6152 | tf_op jit(solution)/shard_map/ppermute | solution.py:224
  110.3 5.2 %collective-permute-start.2 = (bf16[4,512]{1,0:T(4,128)(2,1)S(1)}, bf16[4,512]{1,0:T(4,128)(2,1)S(1)}, u32[]{:S(2)}, u32[]{:S(2)}) collective-permute-start(bf16[4,512]{1,0:T(4,128)(2,1)S(1)} %pad_maximum_fusion.3), channel_id=1, source_target_pairs={{0,128},{4,132},{8,136},{12,140},{16,144},{20,148},{24,152},{28,15... | collective-permute-start | bytes 12296 | tf_op jit(solution)/shard_map/ppermute | solution.py:224
  116.2 17.3 %copy-start.2 = (bf16[8,512]{1,0:T(8,128)(2,1)}, bf16[8,512]{1,0:T(8,128)(2,1)S(1)}, u32[]{:S(2)}) copy-start(bf16[8,512]{1,0:T(8,128)(2,1)S(1)} %pad_maximum_fusion.2.refs_1_) | copy-start | bytes 24580
  116.2 11.0 %collective-permute-start.3 = (bf16[8,512]{1,0:T(8,128)(2,1)S(1)}, bf16[8,512]{1,0:T(8,128)(2,1)S(1)}, u32[]{:S(2)}, u32[]{:S(2)}) collective-permute-start(bf16[8,512]{1,0:T(8,128)(2,1)S(1)} %pad_maximum_fusion.2.refs_1_), channel_id=1, source_target_pairs={{0,8},{4,12},{8,16},{12,20},{16,24},{20,28},{24,32},{28,36},{32,40... | collective-permute-start | bytes 24584 | tf_op jit(solution)/shard_map/ppermute | solution.py:219
  117.8 11.6 %collective-permute-start.4 = (bf16[8,512]{1,0:T(8,128)(2,1)S(1)}, bf16[8,512]{1,0:T(8,128)(2,1)S(1)}, u32[]{:S(2)}, u32[]{:S(2)}) collective-permute-start(bf16[8,512]{1,0:T(8,128)(2,1)S(1)} %pad_maximum_fusion.2.refs_1_), channel_id=1, source_target_pairs={{0,16},{4,20},{8,24},{12,28},{16,32},{20,36},{24,40},{28,44},{32,4... | collective-permute-start | bytes 24584 | tf_op jit(solution)/shard_map/ppermute | solution.py:219
  121.8 10.9 %collective-permute-start.5 = (bf16[8,512]{1,0:T(8,128)(2,1)S(1)}, bf16[8,512]{1,0:T(8,128)(2,1)S(1)}, u32[]{:S(2)}, u32[]{:S(2)}) collective-permute-start(bf16[8,512]{1,0:T(8,128)(2,1)S(1)} %pad_maximum_fusion.2.refs_1_), channel_id=1, source_target_pairs={{0,24},{4,28},{8,32},{12,36},{16,40},{20,44},{24,48},{28,52},{32,5... | collective-permute-start | bytes 24584 | tf_op jit(solution)/shard_map/ppermute | solution.py:219
  122.0 10.7 %collective-permute-start.6 = (bf16[8,512]{1,0:T(8,128)(2,1)S(1)}, bf16[8,512]{1,0:T(8,128)(2,1)S(1)}, u32[]{:S(2)}, u32[]{:S(2)}) collective-permute-start(bf16[8,512]{1,0:T(8,128)(2,1)S(1)} %pad_maximum_fusion.2.refs_1_), channel_id=1, source_target_pairs={{0,32},{4,36},{8,40},{12,44},{16,48},{20,52},{24,56},{28,60},{32,0... | collective-permute-start | bytes 24584 | tf_op jit(solution)/shard_map/ppermute | solution.py:219
  125.6 7.1 %collective-permute-start.7 = (bf16[8,512]{1,0:T(8,128)(2,1)S(1)}, bf16[8,512]{1,0:T(8,128)(2,1)S(1)}, u32[]{:S(2)}, u32[]{:S(2)}) collective-permute-start(bf16[8,512]{1,0:T(8,128)(2,1)S(1)} %pad_maximum_fusion.2.refs_1_), channel_id=1, source_target_pairs={{0,40},{4,44},{8,48},{12,52},{16,56},{20,60},{24,0},{28,4},{32,8},... | collective-permute-start | bytes 24584 | tf_op jit(solution)/shard_map/ppermute | solution.py:219
  127.2 6.3 %copy-start.3 = (bf16[8,512]{1,0:T(8,128)(2,1)}, bf16[8,512]{1,0:T(8,128)(2,1)S(1)}, u32[]{:S(2)}) copy-start(bf16[8,512]{1,0:T(8,128)(2,1)S(1)} %collective-permute-done.3.refs_2_) | copy-start | bytes 24580
  127.2 5.6 %collective-permute-start.8 = (bf16[8,512]{1,0:T(8,128)(2,1)S(1)}, bf16[8,512]{1,0:T(8,128)(2,1)S(1)}, u32[]{:S(2)}, u32[]{:S(2)}) collective-permute-start(bf16[8,512]{1,0:T(8,128)(2,1)S(1)} %pad_maximum_fusion.2.refs_1_), channel_id=1, source_target_pairs={{0,48},{4,52},{8,56},{12,60},{16,0},{20,4},{24,8},{28,12},{32,16},... | collective-permute-start | bytes 24584 | tf_op jit(solution)/shard_map/ppermute | solution.py:219
  129.4 4.0 %collective-permute-start.9 = (bf16[8,512]{1,0:T(8,128)(2,1)S(1)}, bf16[8,512]{1,0:T(8,128)(2,1)S(1)}, u32[]{:S(2)}, u32[]{:S(2)}) collective-permute-start(bf16[8,512]{1,0:T(8,128)(2,1)S(1)} %pad_maximum_fusion.2.refs_1_), channel_id=1, source_target_pairs={{0,56},{4,60},{8,0},{12,4},{16,8},{20,12},{24,16},{28,20},{32,24},... | collective-permute-start | bytes 24584 | tf_op jit(solution)/shard_map/ppermute | solution.py:219
  156.7 9.8 %copy-start.1 = (bf16[512,1024]{1,0:T(8,128)(2,1)S(1)}, bf16[512,1024]{1,0:T(8,128)(2,1)}, u32[]{:S(2)}) copy-start(bf16[512,1024]{1,0:T(8,128)(2,1)} %get-tuple-element.23) | copy-start | bytes 3145732
  156.7 89.2 %all-to-all-start.2 = ((bf16[64,8,3072]{2,1,0:T(8,128)(2,1)}), bf16[64,8,3072]{2,1,0:T(8,128)(2,1)}, u32[]{:S(2)}, u32[]{:S(2)}) async-start(bf16[64,8,3072]{2,1,0:T(8,128)(2,1)} %bitcast.57), calls=%async_computation.2 | async-start | bytes 6291456 | tf_op jit(solution)/shard_map/all_to_all | solution.py:180
  171.1 2.7 %collective-permute-start.10 = (bf16[32,16,1024]{2,1,0:T(8,128)(2,1)S(1)}, bf16[32,16,1024]{2,1,0:T(8,128)(2,1)S(1)}, u32[]{:S(2)}, u32[]{:S(2)}) collective-permute-start(bf16[32,16,1024]{2,1,0:T(8,128)(2,1)S(1)} %fusion), channel_id=1, source_target_pairs={{0,4},{4,0},{8,12},{12,8},{16,20},{20,16},{24,28},{28,24},{32,36},... | collective-permute-start | bytes 3145736 | tf_op jit(solution)/shard_map/ppermute | solution.py:310
  175.8 14.3 %collective-permute-start.13 = (bf16[512,256]{1,0:T(8,128)(2,1)S(1)}, bf16[512,256]{1,0:T(8,128)(2,1)S(1)}, u32[]{:S(2)}, u32[]{:S(2)}) collective-permute-start(bf16[512,256]{1,0:T(8,128)(2,1)S(1)} %get-tuple-element.25), channel_id=1, source_target_pairs={{0,3},{1,0},{2,1},{3,2},{4,7},{5,4},{6,5},{7,6},{8,11},{9,8},{10,9... | collective-permute-start | bytes 786440 | tf_op jit(solution)/shard_map/ppermute | solution.py:316
  178.7 11.5 %collective-permute-start.12 = (bf16[512,256]{1,0:T(8,128)(2,1)S(1)}, bf16[512,256]{1,0:T(8,128)(2,1)S(1)}, u32[]{:S(2)}, u32[]{:S(2)}) collective-permute-start(bf16[512,256]{1,0:T(8,128)(2,1)S(1)} %get-tuple-element.26), channel_id=1, source_target_pairs={{0,2},{1,3},{2,0},{3,1},{4,6},{5,7},{6,4},{7,5},{8,10},{9,11},{10,... | collective-permute-start | bytes 786440 | tf_op jit(solution)/shard_map/ppermute | solution.py:316
  179.5 14.5 %collective-permute-start.11 = (bf16[512,256]{1,0:T(8,128)(2,1)S(1)}, bf16[512,256]{1,0:T(8,128)(2,1)}, u32[]{:S(2)}, u32[]{:S(2)}) collective-permute-start(bf16[512,256]{1,0:T(8,128)(2,1)S(1)} %get-tuple-element.24), channel_id=1, source_target_pairs={{0,1},{1,2},{2,3},{3,0},{4,5},{5,6},{6,7},{7,4},{8,9},{9,10},{10,1... | collective-permute-start | bytes 786440 | tf_op jit(solution)/shard_map/ppermute | solution.py:316
  195.1 6.4 %collective-permute-start.16 = (bf16[128,256]{1,0:T(8,128)(2,1)S(1)}, bf16[128,256]{1,0:T(8,128)(2,1)S(1)}, u32[]{:S(2)}, u32[]{:S(2)}) collective-permute-start(bf16[128,256]{1,0:T(8,128)(2,1)S(1)} %get-tuple-element.28), channel_id=1, source_target_pairs={{0,192},{4,196},{8,200},{12,204},{16,208},{20,212},{24,216},{28,22... | collective-permute-start | bytes 196616 | tf_op jit(solution)/shard_map/ppermute | solution.py:325
  195.7 8.9 %collective-permute-start.15 = (bf16[128,256]{1,0:T(8,128)(2,1)S(1)}, bf16[128,256]{1,0:T(8,128)(2,1)S(1)}, u32[]{:S(2)}, u32[]{:S(2)}) collective-permute-start(bf16[128,256]{1,0:T(8,128)(2,1)S(1)} %get-tuple-element.29), channel_id=1, source_target_pairs={{0,128},{4,132},{8,136},{12,140},{16,144},{20,148},{24,152},{28,15... | collective-permute-start | bytes 196616 | tf_op jit(solution)/shard_map/ppermute | solution.py:325
  198.2 6.4 %collective-permute-start.14 = (bf16[128,256]{1,0:T(8,128)(2,1)S(1)}, bf16[128,256]{1,0:T(8,128)(2,1)S(1)}, u32[]{:S(2)}, u32[]{:S(2)}) collective-permute-start(bf16[128,256]{1,0:T(8,128)(2,1)S(1)} %get-tuple-element.27), channel_id=1, source_target_pairs={{0,64},{4,68},{8,72},{12,76},{16,80},{20,84},{24,88},{28,92},{32,9... | collective-permute-start | bytes 196616 | tf_op jit(solution)/shard_map/ppermute | solution.py:325
  204.6 4.4 %collective-permute-start.17 = (bf16[128,256]{1,0:T(8,128)(2,1)S(1)}, bf16[128,256]{1,0:T(8,128)(2,1)S(1)}, u32[]{:S(2)}, u32[]{:S(2)}) collective-permute-start(bf16[128,256]{1,0:T(8,128)(2,1)S(1)} %fusion.5), channel_id=1, source_target_pairs={{0,1},{1,0},{2,3},{3,2},{4,5},{5,4},{6,7},{7,6},{8,9},{9,8},{10,11... | collective-permute-start | bytes 196616 | tf_op jit(solution)/shard_map/ppermute | solution.py:333
  209.0 6.3 %collective-permute-start.18 = (bf16[128,512]{1,0:T(8,128)(2,1)S(1)}, bf16[128,512]{1,0:T(8,128)(2,1)S(1)}, u32[]{:S(2)}, u32[]{:S(2)}) collective-permute-start(bf16[128,512]{1,0:T(8,128)(2,1)S(1)} %pad_maximum_fusion.1), channel_id=1, source_target_pairs={{0,3},{1,2},{2,1},{3,0},{4,7},{5,6},{6,5},{7,4},{8,11},{9,10},{10,... | collective-permute-start | bytes 393224 | tf_op jit(solution)/shard_map/ppermute | solution.py:333
  216.0 19.9 %collective-permute-start.19 = (bf16[16,1024]{1,0:T(8,128)(2,1)S(1)}, bf16[16,1024]{1,0:T(8,128)(2,1)}, u32[]{:S(2)}, u32[]{:S(2)}) collective-permute-start(bf16[16,1024]{1,0:T(8,128)(2,1)S(1)} %get-tuple-element.36), channel_id=1, source_target_pairs={{0,8},{4,12},{8,16},{12,20},{16,24},{20,28},{24,32},{28,36},{32,40... | collective-permute-start | bytes 98312 | tf_op jit(solution)/shard_map/ppermute | solution.py:341
  217.4 22.7 %collective-permute-start.20 = (bf16[16,1024]{1,0:T(8,128)(2,1)S(1)}, bf16[16,1024]{1,0:T(8,128)(2,1)}, u32[]{:S(2)}, u32[]{:S(2)}) collective-permute-start(bf16[16,1024]{1,0:T(8,128)(2,1)S(1)} %get-tuple-element.35), channel_id=1, source_target_pairs={{0,16},{4,20},{8,24},{12,28},{16,32},{20,36},{24,40},{28,44},{32,4... | collective-permute-start | bytes 98312 | tf_op jit(solution)/shard_map/ppermute | solution.py:341
  222.1 22.1 %collective-permute-start.21 = (bf16[16,1024]{1,0:T(8,128)(2,1)}, bf16[16,1024]{1,0:T(8,128)(2,1)}, u32[]{:S(2)}, u32[]{:S(2)}) collective-permute-start(bf16[16,1024]{1,0:T(8,128)(2,1)} %get-tuple-element.34), channel_id=1, source_target_pairs={{0,24},{4,28},{8,32},{12,36},{16,40},{20,44},{24,48},{28,52},{32,5... | collective-permute-start | bytes 98312 | tf_op jit(solution)/shard_map/ppermute | solution.py:341
  222.3 21.9 %collective-permute-start.22 = (bf16[16,1024]{1,0:T(8,128)(2,1)}, bf16[16,1024]{1,0:T(8,128)(2,1)}, u32[]{:S(2)}, u32[]{:S(2)}) collective-permute-start(bf16[16,1024]{1,0:T(8,128)(2,1)} %get-tuple-element.33), channel_id=1, source_target_pairs={{0,32},{4,36},{8,40},{12,44},{16,48},{20,52},{24,56},{28,60},{32,0... | collective-permute-start | bytes 98312 | tf_op jit(solution)/shard_map/ppermute | solution.py:341
  226.1 18.2 %collective-permute-start.23 = (bf16[16,1024]{1,0:T(8,128)(2,1)}, bf16[16,1024]{1,0:T(8,128)(2,1)}, u32[]{:S(2)}, u32[]{:S(2)}) collective-permute-start(bf16[16,1024]{1,0:T(8,128)(2,1)} %get-tuple-element.32), channel_id=1, source_target_pairs={{0,40},{4,44},{8,48},{12,52},{16,56},{20,60},{24,0},{28,4},{32,8},... | collective-permute-start | bytes 98312 | tf_op jit(solution)/shard_map/ppermute | solution.py:341
  235.9 8.4 %collective-permute-start.24 = (bf16[16,1024]{1,0:T(8,128)(2,1)}, bf16[16,1024]{1,0:T(8,128)(2,1)}, u32[]{:S(2)}, u32[]{:S(2)}) collective-permute-start(bf16[16,1024]{1,0:T(8,128)(2,1)} %get-tuple-element.31), channel_id=1, source_target_pairs={{0,48},{4,52},{8,56},{12,60},{16,0},{20,4},{24,8},{28,12},{32,16},... | collective-permute-start | bytes 98312 | tf_op jit(solution)/shard_map/ppermute | solution.py:341
  240.1 4.2 %collective-permute-start.25 = (bf16[16,1024]{1,0:T(8,128)(2,1)}, bf16[16,1024]{1,0:T(8,128)(2,1)}, u32[]{:S(2)}, u32[]{:S(2)}) collective-permute-start(bf16[16,1024]{1,0:T(8,128)(2,1)} %get-tuple-element.30), channel_id=1, source_target_pairs={{0,56},{4,60},{8,0},{12,4},{16,8},{20,12},{24,16},{28,20},{32,24},... | collective-permute-start | bytes 98312 | tf_op jit(solution)/shard_map/ppermute | solution.py:341
  (7 other events, 9.6 us)
